TPU v7x, 32 devices: a whole 2x2x4 slice. The times are simulated.
32 devices in a mesh: row: 2 (over y), col: 8 (over z, x), rep: 2 (over core).
Axes of the slice: x: 2, y: 2, z: 4, core: 2. Of those that a mesh axis runs over, the one named last changes fastest.
Arguments:
- ancestor_inverse: float32 [2048, 2048], P('row', 'col'), may hold values from -6 to 6
- tile_structure: int32 [16, 16], P('row', 'col'), may hold values from 0 to 1, as said below
- factor: float32 [2048, 512], P(('row', 'col')), may hold values from -0.125 to 0.125
- factor_normalizer: float32 [512, 512], replicated, may hold values from -1 to 1, as said below
- pivot_inverse: float32 [512, 512], P(None, 'rep'), may hold values from -6 to 6, as said below
Outputs:
- ancestor_columns: float32 [2048, 512], P(('row', 'col'), 'rep')
- diag_block: float32 [512, 512], P(None, 'rep')
Inputs may be any that keep to these rules, and one draw needn't show every extreme that they name: `tile_structure`: symmetric, with ones on the diagonal. `factor_normalizer`: lower triangular with ones on its diagonal. `pivot_inverse`: symmetric.
All inputs are finite; a program needn't handle non-finite values.
Results may differ from a plain program's by a relative error of at most 0.000078.
Values sent between devices are 32-bit elements; how exact they have to be, the bound alone decides.
No kernel may reach another device: no remote copies, remote signals or barrier semaphores. Data moves between devices by JAX's collectives and lax.ppermute only.
A program may use at most 64 MiB of HBM per device.

v0:
```python
import functools

import jax
import jax.numpy as jnp
from jax import lax
from jax.experimental import pallas as pl
from jax.experimental.pallas import tpu as pltpu
from jax.sharding import PartitionSpec as P


AXES = ("row", "col", "rep")
PAIR = 2
F32, BF16 = jnp.float32, jnp.bfloat16


def send(block, target):
    rows, cols, reps = (lax.axis_size(axis) for axis in AXES)

    def flat(r, c, p):
        return (r * cols + c) * reps + p

    route = [
        (flat(r, c, p), flat(*target(r, c, p)))
        for r in range(rows)
        for c in range(cols)
        for p in range(reps)
    ]
    return lax.ppermute(block, AXES, route)


def swap_core(block):
    return send(block, lambda r, c, p: (r, c, 1 - p))


def dot(left, right):
    return jnp.dot(left, right, precision=lax.Precision.HIGH, preferred_element_type=F32)


def split(value):
    high = value.astype(BF16)
    return high, (value - high.astype(F32)).astype(BF16)


def split_dot(left, right, contract=(1, 0)):
    dims = (((contract[0],), (contract[1],)), ((), ()))
    product = functools.partial(
        lax.dot_general, dimension_numbers=dims, preferred_element_type=F32
    )
    return (
        product(left[0], right[1]) + product(left[1], right[0]) + product(left[0], right[0])
    )


def tile_at(index, size):
    return pl.ds(pl.multiple_of(index * size, size), size)


def prepare_kernel(planes, rows, tile, place_ref, marks_ref, full_ref, kept_ref, given_ref):
    row, plane, side, rep = (place_ref[i] for i in range(4))
    cut = planes // 2

    def masked(k, wanted, m):
        source, across = (plane ^ k) * PAIR + wanted, row ^ m
        mark = marks_ref[source, across].astype(F32)
        return full_ref[tile_at(source, tile), tile_at(across, tile)] * mark

    for m in range(rows):
        columns = pl.ds(m * tile, tile)

        @pl.loop(0, cut)
        def _(k):
            given_ref[k, :, columns] = masked(k + rep * cut, 1 - side, m)

        @pl.loop(0, planes)
        def _(k):
            kept_ref[k, :, columns] = masked(k, side, m)


def product_kernel(planes, members, place_ref, kept_ref, mine_ref, theirs_ref, *refs):
    arrived, outs = refs[:members], refs[members:]
    cut = planes // 2
    rep = place_ref[3]
    right = split(jnp.concatenate([ref[...] for ref in arrived], 0))
    for k in range(planes):
        taken = jnp.where(rep == k // cut, mine_ref[k % cut], theirs_ref[k % cut])
        left = jnp.concatenate([kept_ref[k], taken], 1)
        outs[k][...] = split_dot(split(left), right)


def coupling_kernel(members, place_ref, normed_ref, other_normed_ref, columns_ref, other_ref, *refs):
    outs, total_ref = refs[:members], refs[members]
    place, first = place_ref[4], place_ref[3] == 0
    half = normed_ref.shape[1]
    quarter, step = half // 2, half // members
    own_normed, own = normed_ref[...], columns_ref[...]
    other_normed, other = other_normed_ref[...], other_ref[...]
    mixed = split_dot(split(own_normed), split(own), (0, 0))
    total_ref[:, :half] = mixed + mixed.T

    def left(mine, theirs):
        return split(jnp.where(first, mine, theirs))

    def right(mine, theirs):
        return split(jnp.where(first, theirs[:, :quarter], mine[:, quarter:]))

    total_ref[:, half:] = split_dot(
        left(own_normed, other_normed), right(own, other), (0, 0)
    ) + split_dot(left(own, other), right(own_normed, other_normed), (0, 0))
    for k in range(members):
        outs[k][...] = total_ref[tile_at(place ^ k, step), :]


def finish_kernel(members, place_ref, pivot_ref, other_ref, *refs):
    parts, out_ref, total_ref, between_ref = refs[:members], *refs[members:]
    place, rep = place_ref[4], place_ref[3]
    half = out_ref.shape[1]
    step = half // members
    for k in range(members):
        rows = tile_at(place ^ k, step)
        total_ref[rows, :] = parts[k][...]
        between_ref[rows, :] = other_ref[k * step : (k + 1) * step, :]

    @pl.when(rep == 0)
    def _():
        across = jnp.concatenate([total_ref[:, half:], between_ref[...]], 1)
        out_ref[:half, :] = pivot_ref[:half, :] - 0.5 * total_ref[:, :half]
        out_ref[half:, :] = pivot_ref[half:, :] - 0.5 * across.T

    @pl.when(rep != 0)
    def _():
        across = jnp.concatenate([between_ref[...], total_ref[:, half:]], 1)
        out_ref[:half, :] = pivot_ref[:half, :] - 0.5 * across
        out_ref[half:, :] = pivot_ref[half:, :] - 0.5 * total_ref[:, :half]


def call(kernel, shapes, in_smem, args, scratch=(), flops=0):
    smem, vmem = pl.BlockSpec(memory_space=pltpu.SMEM), pl.BlockSpec(memory_space=pltpu.VMEM)
    moved = sum(4 * a.size for a in args) + sum(4 * functools.reduce(int.__mul__, s) for s in shapes)
    return pl.pallas_call(
        kernel,
        out_shape=[jax.ShapeDtypeStruct(shape, F32) for shape in shapes],
        in_specs=[smem] * in_smem + [vmem] * (len(args) - in_smem),
        out_specs=[vmem] * len(shapes),
        scratch_shapes=[pltpu.VMEM(shape, F32) for shape in scratch],
        compiler_params=pltpu.CompilerParams(vmem_limit_bytes=3 * moved + 2**21),
        cost_estimate=pl.CostEstimate(flops=flops, bytes_accessed=moved, transcendentals=0),
    )(*args)


def body(ancestor_inverse, tile_structure, factor, factor_normalizer, pivot_inverse):
    tile = factor.shape[0]
    half = pivot_inverse.shape[1]
    rows, cols = lax.axis_size("row"), lax.axis_size("col")
    row, col, rep = (lax.axis_index(name) for name in AXES)
    planes, members = cols // PAIR, rows * PAIR
    plane, side = col // PAIR, col % PAIR
    place = jnp.stack([row, plane, side, rep, row * PAIR + side]).astype(jnp.int32)
    depth = rows * tile

    def half_of(matrix, index):
        return lax.dynamic_slice_in_dim(matrix, index * half, half, 1)

    own_normed = dot(factor, half_of(factor_normalizer, rep))

    def to_plane(k):
        def target(r, c, p):
            block = r * cols + c
            peer = (block % members) ^ k
            return peer % rows, block // members * PAIR + peer // rows, p

        return target

    arrived = [send(own_normed, to_plane(k)) for k in range(members)]
    other_normed = dot(factor, half_of(factor_normalizer, 1 - rep))

    cut = planes // 2
    kept, given = call(
        functools.partial(prepare_kernel, planes, rows, tile),
        [(planes, tile, depth), (cut, tile, depth)],
        2,
        [place, tile_structure, ancestor_inverse],
    )
    mine = send(given, lambda r, c, p: (r, c ^ 1, p))
    theirs = swap_core(mine)
    shares = call(
        functools.partial(product_kernel, planes, members),
        [(tile, half)] * planes,
        1,
        [place, kept, mine, theirs, *arrived],
        flops=12 * planes * tile * depth * half,
    )
    ancestor_columns = -(
        shares[0]
        + sum(
            send(shares[k], lambda r, c, p, k=k: (r, c ^ (k * PAIR), p))
            for k in range(1, planes)
        )
    )

    other_columns = swap_core(ancestor_columns)
    quarter, step = half // 2, half // members
    width = half + quarter
    parts = call(
        functools.partial(coupling_kernel, members),
        [(step, width)] * members,
        1,
        [place, own_normed, other_normed, ancestor_columns, other_columns],
        [(half, width)],
        flops=12 * tile * half * half,
    )

    def in_plane(k):
        def target(r, c, p):
            peer = (r * PAIR + c % PAIR) ^ k
            return peer // PAIR, c // PAIR * PAIR + peer % PAIR, p

        return target

    part = parts[0] + sum(send(parts[k], in_plane(k)) for k in range(1, members))
    part = part + sum(
        send(part, lambda r, c, p, k=k: (r, c ^ (k * PAIR), p))
        for k in range(1, planes)
    )
    parts = [part] + [send(part, in_plane(k)) for k in range(1, members)]
    other_between = swap_core(jnp.concatenate([one[:, half:] for one in parts], 0))
    (diag_block,) = call(
        functools.partial(finish_kernel, members),
        [pivot_inverse.shape],
        1,
        [place, pivot_inverse, other_between, *parts],
        [(half, width), (half, quarter)],
    )
    return ancestor_columns, diag_block


def solution(mesh):
    return jax.shard_map(
        body,
        mesh=mesh,
        in_specs=(P("row", "col"), P("row", "col"), P(("row", "col"), None), P(), P(None, "rep")),
        out_specs=(P(("row", "col"), "rep"), P(None, "rep")),
        check_vma=False,
    )
```

profile of v0, /device:TPU:0, one launch (start us, length us, event | category | flops | bytes accessed | tf_op | source)
XLA Modules:
  0.0 90.6 jit_solution(13692978590125257170)
XLA Ops:
  0.6 0.0 copy-start
  0.7 0.8 copy-done.5
  1.4 0.1 copy.7.marks_ref
  1.5 0.1 stack.23.place_ref
  1.6 1.2 %copy-done.1 = f32[1024,256]{1,0:T(8,128)S(1)} copy-done((f32[1024,256]{1,0:T(8,128)S(1)}, f32[1024,256]{1,0:T(8,128)}, u32[]{:S(2)}) %copy-start.1) | copy-done | bytes 1048600
  2.8 0.8 shard_map.68
  3.6 3.0 %collective-permute-start = (f32[2,128,256]{2,1,0:T(8,128)S(1)}, f32[2,128,256]{2,1,0:T(8,128)S(1)}, u32[]{:S(2)}, u32[]{:S(2)}) collective-permute-start(f32[2,128,256]{2,1,0:T(8,128)S(1)} %get-tuple-element.13), channel_id=1, source_target_pairs={{0,2},{1,3},{2,0},{3,1},{4,6},{5,7},{6,4},{7,5},{8,10},{9,11},{10,... | collective-permute-start | bytes 786440 | tf_op jit(solution)/shard_map/ppermute | solution.py:28
  6.6 6.3 %collective-permute-done.mine_ref = f32[2,128,256]{2,1,0:T(8,128)S(1)} collective-permute-done((f32[2,128,256]{2,1,0:T(8,128)S(1)}, f32[2,128,256]{2,1,0:T(8,128)S(1)}, u32[]{:S(2)}, u32[]{:S(2)}) %collective-permute-start) | collective-permute-done | bytes 262176 | tf_op jit(solution)/shard_map/ppermute | solution.py:28
  12.9 0.3 convolution_bitcast_fusion.1.normed_ref
  13.3 0.7 collective-permute-start.2
  13.9 5.6 %collective-permute-start.3 = (f32[128,256]{1,0:T(8,128)S(1)}, f32[128,256]{1,0:T(8,128)S(1)}, u32[]{:S(2)}, u32[]{:S(2)}) collective-permute-start(f32[128,256]{1,0:T(8,128)S(1)} %convolution_bitcast_fusion.1.normed_ref), channel_id=1, source_target_pairs={{0,16},{1,17},{2,0},{3,1},{4,18},{5,19},{6,2},{7,3},{8,20},{9,21},... | collective-permute-start | bytes 393224 | tf_op jit(solution)/shard_map/ppermute | solution.py:28
  19.5 5.6 %collective-permute-start.5 = (f32[128,256]{1,0:T(8,128)S(1)}, f32[128,256]{1,0:T(8,128)S(1)}, u32[]{:S(2)}, u32[]{:S(2)}) collective-permute-start(f32[128,256]{1,0:T(8,128)S(1)} %convolution_bitcast_fusion.1.normed_ref), channel_id=1, source_target_pairs={{0,18},{1,19},{2,2},{3,3},{4,16},{5,17},{6,0},{7,1},{8,22},{9,23},... | collective-permute-start | bytes 393224 | tf_op jit(solution)/shard_map/ppermute | solution.py:28
  25.2 0.0 collective-permute-done.3.refs_1_
  25.2 3.9 %collective-permute-done.4.refs_2_ = f32[128,256]{1,0:T(8,128)S(1)} collective-permute-done((f32[128,256]{1,0:T(8,128)S(1)}, f32[128,256]{1,0:T(8,128)S(1)}, u32[]{:S(2)}, u32[]{:S(2)}) %collective-permute-start.4) | collective-permute-done | bytes 131104 | tf_op jit(solution)/shard_map/ppermute | solution.py:28
  29.1 2.5 %collective-permute-done.5.refs_3_ = f32[128,256]{1,0:T(8,128)S(1)} collective-permute-done((f32[128,256]{1,0:T(8,128)S(1)}, f32[128,256]{1,0:T(8,128)S(1)}, u32[]{:S(2)}, u32[]{:S(2)}) %collective-permute-start.5) | collective-permute-done | bytes 131104 | tf_op jit(solution)/shard_map/ppermute | solution.py:28
  31.6 1.1 %shard_map.69 = (f32[128,256]{1,0:T(8,128)S(1)}, f32[128,256]{1,0:T(8,128)S(1)}, f32[128,256]{1,0:T(8,128)S(1)}, f32[128,256]{1,0:T(8,128)S(1)}) custom-call(s32[5]{0:T(128)S(1)} %stack.23.place_ref, f32[4,128,256]{2,1,0:T(8,128)S(1)} %get-tuple-element.12.kept_ref, f32[2,128,256]{2,1,0:T(8,128)S(1)} %collective-permute-done.mine_ref, ...), custom_call_target="tpu_custom_call" | custom-call | flops 402653184 | bytes 2097172 | tf_op jit(solution)/shard_map/pallas_call | solution.py:139
  32.8 7.8 %collective-permute-start.6 = (f32[128,256]{1,0:T(8,128)S(1)}, f32[128,256]{1,0:T(8,128)S(1)}, u32[]{:S(2)}, u32[]{:S(2)}) collective-permute-start(f32[128,256]{1,0:T(8,128)S(1)} %get-tuple-element.15), channel_id=1, source_target_pairs={{0,4},{1,5},{2,6},{3,7},{4,0},{5,1},{6,2},{7,3},{8,12},{9,13},{10,... | collective-permute-start | bytes 393224 | tf_op jit(solution)/shard_map/ppermute | solution.py:28
  40.6 7.0 %collective-permute-start.7 = (f32[128,256]{1,0:T(8,128)S(1)}, f32[128,256]{1,0:T(8,128)S(1)}, u32[]{:S(2)}, u32[]{:S(2)}) collective-permute-start(f32[128,256]{1,0:T(8,128)S(1)} %get-tuple-element.16), channel_id=1, source_target_pairs={{0,8},{1,9},{2,10},{3,11},{4,12},{5,13},{6,14},{7,15},{8,0},{9,1},... | collective-permute-start | bytes 393224 | tf_op jit(solution)/shard_map/ppermute | solution.py:28
  47.5 1.4 %collective-permute-start.8 = (f32[128,256]{1,0:T(8,128)S(1)}, f32[128,256]{1,0:T(8,128)S(1)}, u32[]{:S(2)}, u32[]{:S(2)}) collective-permute-start(f32[128,256]{1,0:T(8,128)S(1)} %get-tuple-element.17), channel_id=1, source_target_pairs={{0,12},{1,13},{2,14},{3,15},{4,8},{5,9},{6,10},{7,11},{8,4},{9,5},... | collective-permute-start | bytes 393224 | tf_op jit(solution)/shard_map/ppermute | solution.py:28
  48.9 0.0 collective-permute-done.6
  48.9 2.6 %collective-permute-done.7 = f32[128,256]{1,0:T(8,128)S(1)} collective-permute-done((f32[128,256]{1,0:T(8,128)S(1)}, f32[128,256]{1,0:T(8,128)S(1)}, u32[]{:S(2)}, u32[]{:S(2)}) %collective-permute-start.7) | collective-permute-done | bytes 131104 | tf_op jit(solution)/shard_map/ppermute | solution.py:28
  51.6 6.1 %collective-permute-done.8 = f32[128,256]{1,0:T(8,128)S(1)} collective-permute-done((f32[128,256]{1,0:T(8,128)S(1)}, f32[128,256]{1,0:T(8,128)S(1)}, u32[]{:S(2)}, u32[]{:S(2)}) %collective-permute-start.8) | collective-permute-done | bytes 131104 | tf_op jit(solution)/shard_map/ppermute | solution.py:28
  57.7 0.0 copy-start.2
  57.7 0.1 collective-permute-start.9
  57.8 0.3 convolution_bitcast_fusion.other_normed_ref
  58.1 1.0 %collective-permute-done.9.other_ref = f32[128,256]{1,0:T(8,128)S(1)} collective-permute-done((f32[128,256]{1,0:T(8,128)S(1)}, f32[128,256]{1,0:T(8,128)S(1)}, u32[]{:S(2)}, u32[]{:S(2)}) %collective-permute-start.9) | collective-permute-done | bytes 131104 | tf_op jit(solution)/shard_map/ppermute | solution.py:28
  59.1 1.0 %shard_map.70 = (f32[64,384]{1,0:T(8,128)S(1)}, f32[64,384]{1,0:T(8,128)S(1)}, f32[64,384]{1,0:T(8,128)S(1)}, f32[64,384]{1,0:T(8,128)S(1)}) custom-call(s32[5]{0:T(128)S(1)} %stack.23.place_ref, f32[128,256]{1,0:T(8,128)S(1)} %convolution_bitcast_fusion.1.normed_ref, f32[128,256]{1,0:T(8,128)S(1)} %convolution_bitcast_fusion.other_normed_ref, ...), custom_call_target="tpu_custom_call" | custom-call | flops 100663296 | bytes 917524 | tf_op jit(solution)/shard_map/pallas_call | solution.py:139
  60.2 0.6 collective-permute-start.10
  60.8 1.3 %collective-permute-start.11 = (f32[64,384]{1,0:T(8,128)S(1)}, f32[64,384]{1,0:T(8,128)S(1)}, u32[]{:S(2)}, u32[]{:S(2)}) collective-permute-start(f32[64,384]{1,0:T(8,128)S(1)} %get-tuple-element.20), channel_id=1, source_target_pairs={{0,16},{1,17},{2,18},{3,19},{4,20},{5,21},{6,22},{7,23},{8,24},{9,... | collective-permute-start | bytes 294920 | tf_op jit(solution)/shard_map/ppermute | solution.py:28
  62.1 1.6 %collective-permute-start.12 = (f32[64,384]{1,0:T(8,128)S(1)}, f32[64,384]{1,0:T(8,128)S(1)}, u32[]{:S(2)}, u32[]{:S(2)}) collective-permute-start(f32[64,384]{1,0:T(8,128)S(1)} %get-tuple-element.21), channel_id=1, source_target_pairs={{0,18},{1,19},{2,16},{3,17},{4,22},{5,23},{6,20},{7,21},{8,26},{9,... | collective-permute-start | bytes 294920 | tf_op jit(solution)/shard_map/ppermute | solution.py:28
  63.7 2.0 %collective-permute-done.10 = f32[64,384]{1,0:T(8,128)S(1)} collective-permute-done((f32[64,384]{1,0:T(8,128)S(1)}, f32[64,384]{1,0:T(8,128)S(1)}, u32[]{:S(2)}, u32[]{:S(2)}) %collective-permute-start.10) | collective-permute-done | bytes 98336 | tf_op jit(solution)/shard_map/ppermute | solution.py:28
  65.7 0.8 collective-permute-done.11
  66.5 1.2 %collective-permute-done.12 = f32[64,384]{1,0:T(8,128)S(1)} collective-permute-done((f32[64,384]{1,0:T(8,128)S(1)}, f32[64,384]{1,0:T(8,128)S(1)}, u32[]{:S(2)}, u32[]{:S(2)}) %collective-permute-start.12) | collective-permute-done | bytes 98336 | tf_op jit(solution)/shard_map/ppermute | solution.py:28
  67.7 0.0 copy-start.3
  67.7 3.3 %collective-permute-start.13 = (f32[64,384]{1,0:T(8,128)S(1)}, f32[64,384]{1,0:T(8,128)S(1)}, u32[]{:S(2)}, u32[]{:S(2)}) collective-permute-start(f32[64,384]{1,0:T(8,128)S(1)} %add_add_fusion.1), channel_id=1, source_target_pairs={{0,4},{1,5},{2,6},{3,7},{4,0},{5,1},{6,2},{7,3},{8,12},{9,13},{10,... | collective-permute-start | bytes 294920 | tf_op jit(solution)/shard_map/ppermute | solution.py:28
  71.0 0.7 collective-permute-start.14
  71.7 1.8 %collective-permute-start.15 = (f32[64,384]{1,0:T(8,128)S(1)}, f32[64,384]{1,0:T(8,128)S(1)}, u32[]{:S(2)}, u32[]{:S(2)}) collective-permute-start(f32[64,384]{1,0:T(8,128)S(1)} %add_add_fusion.1), channel_id=1, source_target_pairs={{0,12},{1,13},{2,14},{3,15},{4,8},{5,9},{6,10},{7,11},{8,4},{9,5},... | collective-permute-start | bytes 294920 | tf_op jit(solution)/shard_map/ppermute | solution.py:28
  73.5 1.2 %collective-permute-done.13 = f32[64,384]{1,0:T(8,128)S(1)} collective-permute-done((f32[64,384]{1,0:T(8,128)S(1)}, f32[64,384]{1,0:T(8,128)S(1)}, u32[]{:S(2)}, u32[]{:S(2)}) %collective-permute-start.13) | collective-permute-done | bytes 98336 | tf_op jit(solution)/shard_map/ppermute | solution.py:28
  74.7 5.5 %collective-permute-done.14 = f32[64,384]{1,0:T(8,128)S(1)} collective-permute-done((f32[64,384]{1,0:T(8,128)S(1)}, f32[64,384]{1,0:T(8,128)S(1)}, u32[]{:S(2)}, u32[]{:S(2)}) %collective-permute-start.14) | collective-permute-done | bytes 98336 | tf_op jit(solution)/shard_map/ppermute | solution.py:28
  80.2 0.8 collective-permute-start.16
  80.9 1.1 %collective-permute-start.17 = (f32[64,384]{1,0:T(8,128)S(1)}, f32[64,384]{1,0:T(8,128)S(1)}, u32[]{:S(2)}, u32[]{:S(2)}) collective-permute-start(f32[64,384]{1,0:T(8,128)S(1)} %add_add_fusion.refs_0_), channel_id=1, source_target_pairs={{0,16},{1,17},{2,18},{3,19},{4,20},{5,21},{6,22},{7,23},{8,24},{9,... | collective-permute-start | bytes 294920 | tf_op jit(solution)/shard_map/ppermute | solution.py:28
  82.1 1.6 %collective-permute-start.18 = (f32[64,384]{1,0:T(8,128)S(1)}, f32[64,384]{1,0:T(8,128)S(1)}, u32[]{:S(2)}, u32[]{:S(2)}) collective-permute-start(f32[64,384]{1,0:T(8,128)S(1)} %add_add_fusion.refs_0_), channel_id=1, source_target_pairs={{0,18},{1,19},{2,16},{3,17},{4,22},{5,23},{6,20},{7,21},{8,26},{9,... | collective-permute-start | bytes 294920 | tf_op jit(solution)/shard_map/ppermute | solution.py:28
  83.7 1.7 %collective-permute-done.16.refs_1_ = f32[64,384]{1,0:T(8,128)S(1)} collective-permute-done((f32[64,384]{1,0:T(8,128)S(1)}, f32[64,384]{1,0:T(8,128)S(1)}, u32[]{:S(2)}, u32[]{:S(2)}) %collective-permute-start.16) | collective-permute-done | bytes 98336 | tf_op jit(solution)/shard_map/ppermute | solution.py:28
  85.4 1.0 %collective-permute-done.17.refs_2_ = f32[64,384]{1,0:T(8,128)S(1)} collective-permute-done((f32[64,384]{1,0:T(8,128)S(1)}, f32[64,384]{1,0:T(8,128)S(1)}, u32[]{:S(2)}, u32[]{:S(2)}) %collective-permute-start.17) | collective-permute-done | bytes 98336 | tf_op jit(solution)/shard_map/ppermute | solution.py:28
  86.4 1.2 %collective-permute-done.18.refs_3_ = f32[64,384]{1,0:T(8,128)S(1)} collective-permute-done((f32[64,384]{1,0:T(8,128)S(1)}, f32[64,384]{1,0:T(8,128)S(1)}, u32[]{:S(2)}, u32[]{:S(2)}) %collective-permute-start.18) | collective-permute-done | bytes 98336 | tf_op jit(solution)/shard_map/ppermute | solution.py:28
  87.6 0.1 collective-permute-start.19
  87.7 1.3 %collective-permute-done.19.other_ref = f32[256,128]{1,0:T(8,128)S(1)} collective-permute-done((f32[256,128]{1,0:T(8,128)S(1)}, f32[256,128]{1,0:T(8,128)S(1)}, u32[]{:S(2)}, u32[]{:S(2)}) %collective-permute-start.19) | collective-permute-done | bytes 131104 | tf_op jit(solution)/shard_map/ppermute | solution.py:28
  89.0 1.5 %shard_map.71 = f32[512,256]{1,0:T(8,128)} custom-call(s32[5]{0:T(128)S(1)} %stack.23.place_ref, f32[512,256]{1,0:T(8,128)S(1)} %copy-done.3, f32[256,128]{1,0:T(8,128)S(1)} %collective-permute-done.19.other_ref, f32[64,384]{1,0:T(8,128)S(1)} %add_add_fusion.refs_0_, f32[64,384]{1,0:T(8,128)S(1)} %collective-permute-done.16.refs_1_, ...), custom_call_target="tpu_custom_call" | custom-call | bytes 1572884 | tf_op jit(solution)/shard_map/pallas_call | solution.py:139
  (20 shorter events, 0.1 us)
Async XLA Ops:
  0.6 12.3 %copy-start = (f32[512,512]{1,0:T(8,128)S(1)}, f32[512,512]{1,0:T(8,128)}, u32[]{:S(2)}) copy-start(f32[512,512]{1,0:T(8,128)} %param.8) | copy-start | bytes 3145732
  0.7 0.8 copy-start.5
  1.6 1.2 %copy-start.1 = (f32[1024,256]{1,0:T(8,128)S(1)}, f32[1024,256]{1,0:T(8,128)}, u32[]{:S(2)}) copy-start(f32[1024,256]{1,0:T(8,128)} %full_ref.1) | copy-start | bytes 3145732
  2.8 10.1 %copy-start.4 = (f32[128,512]{1,0:T(8,128)S(1)}, f32[128,512]{1,0:T(8,128)}, u32[]{:S(2)}) copy-start(f32[128,512]{1,0:T(8,128)} %param.7) | copy-start | bytes 786436
  3.6 9.3 %collective-permute-start = (f32[2,128,256]{2,1,0:T(8,128)S(1)}, f32[2,128,256]{2,1,0:T(8,128)S(1)}, u32[]{:S(2)}, u32[]{:S(2)}) collective-permute-start(f32[2,128,256]{2,1,0:T(8,128)S(1)} %get-tuple-element.13), channel_id=1, source_target_pairs={{0,2},{1,3},{2,0},{3,1},{4,6},{5,7},{6,4},{7,5},{8,10},{9,11},{10,... | collective-permute-start | bytes 786440 | tf_op jit(solution)/shard_map/ppermute | solution.py:28
  12.9 18.7 %collective-permute-start.1 = (f32[2,128,256]{2,1,0:T(8,128)S(1)}, f32[2,128,256]{2,1,0:T(8,128)S(1)}, u32[]{:S(2)}, u32[]{:S(2)}) collective-permute-start(f32[2,128,256]{2,1,0:T(8,128)S(1)} %collective-permute-done.mine_ref), channel_id=1, source_target_pairs={{0,1},{1,0},{2,3},{3,2},{4,5},{5,4},{6,7},{7,6},{8,9},{9,8},{10,11... | collective-permute-start | bytes 786440 | tf_op jit(solution)/shard_map/ppermute | solution.py:28
  13.3 11.9 %collective-permute-start.2 = (f32[128,256]{1,0:T(8,128)S(1)}, f32[128,256]{1,0:T(8,128)S(1)}, u32[]{:S(2)}, u32[]{:S(2)}) collective-permute-start(f32[128,256]{1,0:T(8,128)S(1)} %convolution_bitcast_fusion.1.normed_ref), channel_id=1, source_target_pairs={{0,0},{1,1},{2,16},{3,17},{4,2},{5,3},{6,18},{7,19},{8,4},{9,5},{1... | collective-permute-start | bytes 393224 | tf_op jit(solution)/shard_map/ppermute | solution.py:28
  13.9 11.2 %collective-permute-start.3 = (f32[128,256]{1,0:T(8,128)S(1)}, f32[128,256]{1,0:T(8,128)S(1)}, u32[]{:S(2)}, u32[]{:S(2)}) collective-permute-start(f32[128,256]{1,0:T(8,128)S(1)} %convolution_bitcast_fusion.1.normed_ref), channel_id=1, source_target_pairs={{0,16},{1,17},{2,0},{3,1},{4,18},{5,19},{6,2},{7,3},{8,20},{9,21},... | collective-permute-start | bytes 393224 | tf_op jit(solution)/shard_map/ppermute | solution.py:28
  19.5 9.6 %collective-permute-start.4 = (f32[128,256]{1,0:T(8,128)S(1)}, f32[128,256]{1,0:T(8,128)S(1)}, u32[]{:S(2)}, u32[]{:S(2)}) collective-permute-start(f32[128,256]{1,0:T(8,128)S(1)} %convolution_bitcast_fusion.1.normed_ref), channel_id=1, source_target_pairs={{0,2},{1,3},{2,18},{3,19},{4,0},{5,1},{6,16},{7,17},{8,6},{9,7},{1... | collective-permute-start | bytes 393224 | tf_op jit(solution)/shard_map/ppermute | solution.py:28
  19.5 12.1 %collective-permute-start.5 = (f32[128,256]{1,0:T(8,128)S(1)}, f32[128,256]{1,0:T(8,128)S(1)}, u32[]{:S(2)}, u32[]{:S(2)}) collective-permute-start(f32[128,256]{1,0:T(8,128)S(1)} %convolution_bitcast_fusion.1.normed_ref), channel_id=1, source_target_pairs={{0,18},{1,19},{2,2},{3,3},{4,16},{5,17},{6,0},{7,1},{8,22},{9,23},... | collective-permute-start | bytes 393224 | tf_op jit(solution)/shard_map/ppermute | solution.py:28
  32.8 16.2 %collective-permute-start.6 = (f32[128,256]{1,0:T(8,128)S(1)}, f32[128,256]{1,0:T(8,128)S(1)}, u32[]{:S(2)}, u32[]{:S(2)}) collective-permute-start(f32[128,256]{1,0:T(8,128)S(1)} %get-tuple-element.15), channel_id=1, source_target_pairs={{0,4},{1,5},{2,6},{3,7},{4,0},{5,1},{6,2},{7,3},{8,12},{9,13},{10,... | collective-permute-start | bytes 393224 | tf_op jit(solution)/shard_map/ppermute | solution.py:28
  40.6 11.0 %collective-permute-start.7 = (f32[128,256]{1,0:T(8,128)S(1)}, f32[128,256]{1,0:T(8,128)S(1)}, u32[]{:S(2)}, u32[]{:S(2)}) collective-permute-start(f32[128,256]{1,0:T(8,128)S(1)} %get-tuple-element.16), channel_id=1, source_target_pairs={{0,8},{1,9},{2,10},{3,11},{4,12},{5,13},{6,14},{7,15},{8,0},{9,1},... | collective-permute-start | bytes 393224 | tf_op jit(solution)/shard_map/ppermute | solution.py:28
  47.5 10.1 %collective-permute-start.8 = (f32[128,256]{1,0:T(8,128)S(1)}, f32[128,256]{1,0:T(8,128)S(1)}, u32[]{:S(2)}, u32[]{:S(2)}) collective-permute-start(f32[128,256]{1,0:T(8,128)S(1)} %get-tuple-element.17), channel_id=1, source_target_pairs={{0,12},{1,13},{2,14},{3,15},{4,8},{5,9},{6,10},{7,11},{8,4},{9,5},... | collective-permute-start | bytes 393224 | tf_op jit(solution)/shard_map/ppermute | solution.py:28
  57.7 1.4 %copy-start.2 = (f32[128,256]{1,0:T(8,128)}, f32[128,256]{1,0:T(8,128)S(1)}, u32[]{:S(2)}) copy-start(f32[128,256]{1,0:T(8,128)S(1)} %add_negate_fusion.columns_ref) | copy-start | bytes 393220
  57.7 1.4 %collective-permute-start.9 = (f32[128,256]{1,0:T(8,128)S(1)}, f32[128,256]{1,0:T(8,128)S(1)}, u32[]{:S(2)}, u32[]{:S(2)}) collective-permute-start(f32[128,256]{1,0:T(8,128)S(1)} %add_negate_fusion.columns_ref), channel_id=1, source_target_pairs={{0,1},{1,0},{2,3},{3,2},{4,5},{5,4},{6,7},{7,6},{8,9},{9,8},{10,11... | collective-permute-start | bytes 393224 | tf_op jit(solution)/shard_map/ppermute | solution.py:28
  60.2 5.5 %collective-permute-start.10 = (f32[64,384]{1,0:T(8,128)S(1)}, f32[64,384]{1,0:T(8,128)S(1)}, u32[]{:S(2)}, u32[]{:S(2)}) collective-permute-start(f32[64,384]{1,0:T(8,128)S(1)} %get-tuple-element.19), channel_id=1, source_target_pairs={{0,2},{1,3},{2,0},{3,1},{4,6},{5,7},{6,4},{7,5},{8,10},{9,11},{10,... | collective-permute-start | bytes 294920 | tf_op jit(solution)/shard_map/ppermute | solution.py:28
  60.8 5.7 %collective-permute-start.11 = (f32[64,384]{1,0:T(8,128)S(1)}, f32[64,384]{1,0:T(8,128)S(1)}, u32[]{:S(2)}, u32[]{:S(2)}) collective-permute-start(f32[64,384]{1,0:T(8,128)S(1)} %get-tuple-element.20), channel_id=1, source_target_pairs={{0,16},{1,17},{2,18},{3,19},{4,20},{5,21},{6,22},{7,23},{8,24},{9,... | collective-permute-start | bytes 294920 | tf_op jit(solution)/shard_map/ppermute | solution.py:28
  62.1 5.5 %collective-permute-start.12 = (f32[64,384]{1,0:T(8,128)S(1)}, f32[64,384]{1,0:T(8,128)S(1)}, u32[]{:S(2)}, u32[]{:S(2)}) collective-permute-start(f32[64,384]{1,0:T(8,128)S(1)} %get-tuple-element.21), channel_id=1, source_target_pairs={{0,18},{1,19},{2,16},{3,17},{4,22},{5,23},{6,20},{7,21},{8,26},{9,... | collective-permute-start | bytes 294920 | tf_op jit(solution)/shard_map/ppermute | solution.py:28
  67.7 21.4 %copy-start.3 = (f32[512,256]{1,0:T(8,128)S(1)}, f32[512,256]{1,0:T(8,128)}, u32[]{:S(2)}) copy-start(f32[512,256]{1,0:T(8,128)} %pivot_ref.1) | copy-start | bytes 1572868
  67.7 7.0 %collective-permute-start.13 = (f32[64,384]{1,0:T(8,128)S(1)}, f32[64,384]{1,0:T(8,128)S(1)}, u32[]{:S(2)}, u32[]{:S(2)}) collective-permute-start(f32[64,384]{1,0:T(8,128)S(1)} %add_add_fusion.1), channel_id=1, source_target_pairs={{0,4},{1,5},{2,6},{3,7},{4,0},{5,1},{6,2},{7,3},{8,12},{9,13},{10,... | collective-permute-start | bytes 294920 | tf_op jit(solution)/shard_map/ppermute | solution.py:28
  71.0 9.1 %collective-permute-start.14 = (f32[64,384]{1,0:T(8,128)S(1)}, f32[64,384]{1,0:T(8,128)S(1)}, u32[]{:S(2)}, u32[]{:S(2)}) collective-permute-start(f32[64,384]{1,0:T(8,128)S(1)} %add_add_fusion.1), channel_id=1, source_target_pairs={{0,8},{1,9},{2,10},{3,11},{4,12},{5,13},{6,14},{7,15},{8,0},{9,1},... | collective-permute-start | bytes 294920 | tf_op jit(solution)/shard_map/ppermute | solution.py:28
  71.7 8.4 %collective-permute-start.15 = (f32[64,384]{1,0:T(8,128)S(1)}, f32[64,384]{1,0:T(8,128)S(1)}, u32[]{:S(2)}, u32[]{:S(2)}) collective-permute-start(f32[64,384]{1,0:T(8,128)S(1)} %add_add_fusion.1), channel_id=1, source_target_pairs={{0,12},{1,13},{2,14},{3,15},{4,8},{5,9},{6,10},{7,11},{8,4},{9,5},... | collective-permute-start | bytes 294920 | tf_op jit(solution)/shard_map/ppermute | solution.py:28
  80.2 5.2 %collective-permute-start.16 = (f32[64,384]{1,0:T(8,128)S(1)}, f32[64,384]{1,0:T(8,128)S(1)}, u32[]{:S(2)}, u32[]{:S(2)}) collective-permute-start(f32[64,384]{1,0:T(8,128)S(1)} %add_add_fusion.refs_0_), channel_id=1, source_target_pairs={{0,2},{1,3},{2,0},{3,1},{4,6},{5,7},{6,4},{7,5},{8,10},{9,11},{10,... | collective-permute-start | bytes 294920 | tf_op jit(solution)/shard_map/ppermute | solution.py:28
  80.9 5.4 %collective-permute-start.17 = (f32[64,384]{1,0:T(8,128)S(1)}, f32[64,384]{1,0:T(8,128)S(1)}, u32[]{:S(2)}, u32[]{:S(2)}) collective-permute-start(f32[64,384]{1,0:T(8,128)S(1)} %add_add_fusion.refs_0_), channel_id=1, source_target_pairs={{0,16},{1,17},{2,18},{3,19},{4,20},{5,21},{6,22},{7,23},{8,24},{9,... | collective-permute-start | bytes 294920 | tf_op jit(solution)/shard_map/ppermute | solution.py:28
  82.1 5.5 %collective-permute-start.18 = (f32[64,384]{1,0:T(8,128)S(1)}, f32[64,384]{1,0:T(8,128)S(1)}, u32[]{:S(2)}, u32[]{:S(2)}) collective-permute-start(f32[64,384]{1,0:T(8,128)S(1)} %add_add_fusion.refs_0_), channel_id=1, source_target_pairs={{0,18},{1,19},{2,16},{3,17},{4,22},{5,23},{6,20},{7,21},{8,26},{9,... | collective-permute-start | bytes 294920 | tf_op jit(solution)/shard_map/ppermute | solution.py:28
  87.6 1.4 %collective-permute-start.19 = (f32[256,128]{1,0:T(8,128)S(1)}, f32[256,128]{1,0:T(8,128)S(1)}, u32[]{:S(2)}, u32[]{:S(2)}) collective-permute-start(f32[256,128]{1,0:T(8,128)S(1)} %pad_maximum_fusion), channel_id=1, source_target_pairs={{0,1},{1,0},{2,3},{3,2},{4,5},{5,4},{6,7},{7,6},{8,9},{9,8},{10,11... | collective-permute-start | bytes 393224 | tf_op jit(solution)/shard_map/ppermute | solution.py:28
where the time goes:
time: 90.8 us; the launch traced here: 90.6 us
  starting transfers between devices  44.1 us (49%)
  waiting for transfers between devices  38.3 us (42%)
  Pallas kernels  4.45 us (5%)
  local copies, waits for them, and re-layouts  2.18 us (2%)
    ppermute x20, starting transfers between devices, send(): return lax.ppermute(block, AXES, route)  44.1 us
    ppermute x20, waiting for transfers between devices, send(): return lax.ppermute(block, AXES, route)  38.3 us
    pallas_call x4, Pallas kernels, call(): pl.pallas_call(kernel, out_shape=[jax.ShapeDtypeStruct(shape, F32) for sh...  4.45 us
    unnamed x13, local copies, waits for them, and re-layouts  2.09 us
  transfers between devices with their start and end apart: 20, of which 15 were waited for; matrix products, arithmetic and copies ran while one was open for 1% of the time, Pallas kernels for 0%

commit v1 on v0

--- a/solution.py
+++ b/solution.py
@@ -84,16 +84,21 @@
     for k in range(planes):
         taken = jnp.where(rep == k // cut, mine_ref[k % cut], theirs_ref[k % cut])
         left = jnp.concatenate([kept_ref[k], taken], 1)
-        outs[k][...] = split_dot(split(left), right)
-
-
-def coupling_kernel(members, place_ref, normed_ref, other_normed_ref, columns_ref, other_ref, *refs):
-    outs, total_ref = refs[:members], refs[members]
+        share = split_dot(split(left), right)
+        outs[0][k] = share
+        if k:
+            outs[k][...] = share
+
+
+def coupling_kernel(members, planes, place_ref, share_ref, other_ref, gathered_ref, *refs):
+    strip, outs, total_ref = refs[: planes + 1], refs[planes + 1 : -1], refs[-1]
     place, first = place_ref[4], place_ref[3] == 0
-    half = normed_ref.shape[1]
+    tile, half = strip[0].shape
     quarter, step = half // 2, half // members
-    own_normed, own = normed_ref[...], columns_ref[...]
-    other_normed, other = other_normed_ref[...], other_ref[...]
+    own_normed = jnp.concatenate([ref[...] for ref in strip[:planes]], 0)
+    other_normed = jnp.concatenate([strip[planes][...], gathered_ref[...]], 0)
+    own = share_ref[...].reshape(planes * tile, half)
+    other = other_ref[...].reshape(planes * tile, half)
     mixed = split_dot(split(own_normed), split(own), (0, 0))
     total_ref[:, :half] = mixed + mixed.T
 
@@ -123,14 +128,14 @@
     @pl.when(rep == 0)
     def _():
         across = jnp.concatenate([total_ref[:, half:], between_ref[...]], 1)
-        out_ref[:half, :] = pivot_ref[:half, :] - 0.5 * total_ref[:, :half]
-        out_ref[half:, :] = pivot_ref[half:, :] - 0.5 * across.T
+        out_ref[:half, :] = pivot_ref[:half, :] + 0.5 * total_ref[:, :half]
+        out_ref[half:, :] = pivot_ref[half:, :] + 0.5 * across.T
 
     @pl.when(rep != 0)
     def _():
         across = jnp.concatenate([between_ref[...], total_ref[:, half:]], 1)
-        out_ref[:half, :] = pivot_ref[:half, :] - 0.5 * across
-        out_ref[half:, :] = pivot_ref[half:, :] - 0.5 * total_ref[:, :half]
+        out_ref[:half, :] = pivot_ref[:half, :] + 0.5 * across
+        out_ref[half:, :] = pivot_ref[half:, :] + 0.5 * total_ref[:, :half]
 
 
 def call(kernel, shapes, in_smem, args, scratch=(), flops=0):
@@ -162,15 +167,25 @@
 
     own_normed = dot(factor, half_of(factor_normalizer, rep))
 
-    def to_plane(k):
+    def to_plane(r, c, p):
+        block = r * cols + c
+        peer = block % members
+        return peer % rows, block // members * PAIR + peer // rows, p
+
+    def beside(k):
         def target(r, c, p):
-            block = r * cols + c
-            peer = (block % members) ^ k
-            return peer % rows, block // members * PAIR + peer // rows, p
+            peer = (c % PAIR * rows + r) ^ k
+            return peer % rows, c // PAIR * PAIR + peer // rows, p
 
         return target
 
-    arrived = [send(own_normed, to_plane(k)) for k in range(members)]
+    def along(k):
+        return lambda r, c, p: (r, c ^ (k * PAIR), p)
+
+    arrived = [send(own_normed, to_plane)]
+    arrived += [send(arrived[0], beside(k)) for k in range(1, members)]
+    strip = [own_normed] + [send(own_normed, along(k)) for k in range(1, planes)]
+    other_strip = swap_core(jnp.concatenate(strip[1:], 0))
     other_normed = dot(factor, half_of(factor_normalizer, 1 - rep))
 
     cut = planes // 2
@@ -182,31 +197,25 @@
     )
     mine = send(given, lambda r, c, p: (r, c ^ 1, p))
     theirs = swap_core(mine)
-    shares = call(
+    product, *shares = call(
         functools.partial(product_kernel, planes, members),
-        [(tile, half)] * planes,
+        [(planes, tile, half)] + [(tile, half)] * (planes - 1),
         1,
         [place, kept, mine, theirs, *arrived],
         flops=12 * planes * tile * depth * half,
     )
-    ancestor_columns = -(
-        shares[0]
-        + sum(
-            send(shares[k], lambda r, c, p, k=k: (r, c ^ (k * PAIR), p))
-            for k in range(1, planes)
-        )
-    )
-
-    other_columns = swap_core(ancestor_columns)
+    other_product = swap_core(product)
+    ancestor_columns = -(product[0] + sum(send(shares[k - 1], along(k)) for k in range(1, planes)))
+
     quarter, step = half // 2, half // members
     width = half + quarter
     parts = call(
-        functools.partial(coupling_kernel, members),
+        functools.partial(coupling_kernel, members, planes),
         [(step, width)] * members,
         1,
-        [place, own_normed, other_normed, ancestor_columns, other_columns],
+        [place, product, other_product, other_strip, *strip, other_normed],
         [(half, width)],
-        flops=12 * tile * half * half,
+        flops=12 * planes * tile * half * half,
     )
 
     def in_plane(k):
@@ -217,10 +226,7 @@
         return target
 
     part = parts[0] + sum(send(parts[k], in_plane(k)) for k in range(1, members))
-    part = part + sum(
-        send(part, lambda r, c, p, k=k: (r, c ^ (k * PAIR), p))
-        for k in range(1, planes)
-    )
+    part = part + sum(send(part, along(k)) for k in range(1, planes))
     parts = [part] + [send(part, in_plane(k)) for k in range(1, members)]
     other_between = swap_core(jnp.concatenate([one[:, half:] for one in parts], 0))
     (diag_block,) = call(

time: 90.8 us -> 76.5 us (0.84)
  starting transfers between devices: 44.1 us -> 32.5 us
  waiting for transfers between devices: 38.3 us -> 32.9 us
  other arithmetic: 0.09 us -> 1.52 us
  matrix products: 0.59 us -> 1.53 us
    ppermute x20 -> x24, starting transfers between devices: 44.1 us -> 32.5 us  [send(): return lax.ppermute(block, AXES, route)]
    ppermute x20 -> x24, waiting for transfers between devices: 38.3 us -> 32.9 us  [send(): return lax.ppermute(block, AXES, route)]
    dot_general x2, matrix products: 0.59 us -> 1.53 us  [dot(): jnp.dot(left, right, precision=lax.Precision.HIGH, preferred_element_type...]
    unnamed x13 -> x11, local copies, waits for them, and re-layouts: 2.09 us -> 2.07 us
  transfers between devices with their start and end apart: 20 -> 24, of which waited for: 15 -> 12; matrix products, arithmetic and copies ran while one was open for 1% -> 4% of each run, Pallas kernels for 0% -> 2%
where the time goes in v1:
time: 76.5 us; the launch traced here: 76.3 us
  waiting for transfers between devices  32.9 us (43%)
  starting transfers between devices  32.5 us (42%)
  Pallas kernels  4.87 us (6%)
  local copies, waits for them, and re-layouts  2.17 us (3%)
  matrix products  1.53 us (2%)
  other arithmetic  1.52 us (2%)
  between operations  0.8 us (1%)
    ppermute x24, waiting for transfers between devices, send(): return lax.ppermute(block, AXES, route)  32.9 us
    ppermute x24, starting transfers between devices, send(): return lax.ppermute(block, AXES, route)  32.5 us
    pallas_call x4, Pallas kernels, call(): pl.pallas_call(kernel, out_shape=[jax.ShapeDtypeStruct(shape, F32) for sh...  4.87 us
    unnamed x11, local copies, waits for them, and re-layouts  2.07 us
  transfers between devices with their start and end apart: 24, of which 12 were waited for; matrix products, arithmetic and copies ran while one was open for 4% of the time, Pallas kernels for 2%

profile of v1, /device:TPU:0, one launch (start us, length us, event | category | flops | bytes accessed | tf_op | source)
XLA Modules:
  0.0 76.3 jit_solution(462813064372417358)
XLA Ops:
  0.6 0.0 copy-start
  0.7 0.7 copy-done.4
  1.4 0.1 copy.7.marks_ref
  1.5 0.1 stack.23.place_ref
  1.6 1.2 %copy-done.1 = f32[1024,256]{1,0:T(8,128)S(1)} copy-done((f32[1024,256]{1,0:T(8,128)S(1)}, f32[1024,256]{1,0:T(8,128)}, u32[]{:S(2)}) %copy-start.1) | copy-done | bytes 1048600
  2.8 0.8 %shard_map.68 = (f32[4,128,256]{2,1,0:T(8,128)S(1)}, f32[2,128,256]{2,1,0:T(8,128)S(1)}) custom-call(s32[5]{0:T(128)S(1)} %stack.23.place_ref, s32[8,2]{1,0:T(8,128)S(1)} %copy.7.marks_ref, f32[1024,256]{1,0:T(8,128)S(1)} %copy-done.1), custom_call_target="tpu_custom_call" | custom-call | bytes 1835092 | tf_op jit(solution)/shard_map/pallas_call | solution.py:144
  3.6 3.0 %collective-permute-start = (f32[2,128,256]{2,1,0:T(8,128)S(1)}, f32[2,128,256]{2,1,0:T(8,128)S(1)}, u32[]{:S(2)}, u32[]{:S(2)}) collective-permute-start(f32[2,128,256]{2,1,0:T(8,128)S(1)} %get-tuple-element.13), channel_id=1, source_target_pairs={{0,2},{1,3},{2,0},{3,1},{4,6},{5,7},{6,4},{7,5},{8,10},{9,11},{10,... | collective-permute-start | bytes 786440 | tf_op jit(solution)/shard_map/ppermute | solution.py:28
  6.6 0.3 convolution_bitcast_fusion.1.refs_0_
  6.9 0.7 collective-permute-start.2
  7.6 7.4 %collective-permute-done.mine_ref = f32[2,128,256]{2,1,0:T(8,128)S(1)} collective-permute-done((f32[2,128,256]{2,1,0:T(8,128)S(1)}, f32[2,128,256]{2,1,0:T(8,128)S(1)}, u32[]{:S(2)}, u32[]{:S(2)}) %collective-permute-start) | collective-permute-done | bytes 262176 | tf_op jit(solution)/shard_map/ppermute | solution.py:28
  15.0 0.0 collective-permute-start.1
  15.0 0.0 collective-permute-done.2.refs_0_
  15.0 2.2 %collective-permute-start.3 = (f32[128,256]{1,0:T(8,128)S(1)}, f32[128,256]{1,0:T(8,128)S(1)}, u32[]{:S(2)}, u32[]{:S(2)}) collective-permute-start(f32[128,256]{1,0:T(8,128)S(1)} %collective-permute-done.2.refs_0_), channel_id=1, source_target_pairs={{0,16},{1,17},{2,18},{3,19},{4,20},{5,21},{6,22},{7,23},{8,24},{9,... | collective-permute-start | bytes 393224 | tf_op jit(solution)/shard_map/ppermute | solution.py:28
  17.2 0.4 collective-permute-start.4
  17.6 1.4 %collective-permute-start.5 = (f32[128,256]{1,0:T(8,128)S(1)}, f32[128,256]{1,0:T(8,128)S(1)}, u32[]{:S(2)}, u32[]{:S(2)}) collective-permute-start(f32[128,256]{1,0:T(8,128)S(1)} %collective-permute-done.2.refs_0_), channel_id=1, source_target_pairs={{0,18},{1,19},{2,16},{3,17},{4,22},{5,23},{6,20},{7,21},{8,26},{9,... | collective-permute-start | bytes 393224 | tf_op jit(solution)/shard_map/ppermute | solution.py:28
  19.0 4.5 %collective-permute-start.12 = (f32[128,256]{1,0:T(8,128)S(1)}, f32[128,256]{1,0:T(8,128)S(1)}, u32[]{:S(2)}, u32[]{:S(2)}) collective-permute-start(f32[128,256]{1,0:T(8,128)S(1)} %convolution_bitcast_fusion.1.refs_0_), channel_id=1, source_target_pairs={{0,12},{1,13},{2,14},{3,15},{4,8},{5,9},{6,10},{7,11},{8,4},{9,5},... | collective-permute-start | bytes 393224 | tf_op jit(solution)/shard_map/ppermute | solution.py:28
  23.5 1.4 %collective-permute-start.11 = (f32[128,256]{1,0:T(8,128)S(1)}, f32[128,256]{1,0:T(8,128)S(1)}, u32[]{:S(2)}, u32[]{:S(2)}) collective-permute-start(f32[128,256]{1,0:T(8,128)S(1)} %convolution_bitcast_fusion.1.refs_0_), channel_id=1, source_target_pairs={{0,8},{1,9},{2,10},{3,11},{4,12},{5,13},{6,14},{7,15},{8,0},{9,1},... | collective-permute-start | bytes 393224 | tf_op jit(solution)/shard_map/ppermute | solution.py:28
  25.0 2.9 %collective-permute-start.10 = (f32[128,256]{1,0:T(8,128)S(1)}, f32[128,256]{1,0:T(8,128)S(1)}, u32[]{:S(2)}, u32[]{:S(2)}) collective-permute-start(f32[128,256]{1,0:T(8,128)S(1)} %convolution_bitcast_fusion.1.refs_0_), channel_id=1, source_target_pairs={{0,4},{1,5},{2,6},{3,7},{4,0},{5,1},{6,2},{7,3},{8,12},{9,13},{10,... | collective-permute-start | bytes 393224 | tf_op jit(solution)/shard_map/ppermute | solution.py:28
  27.8 0.0 collective-permute-done.1.theirs_ref
  27.8 1.2 %shard_map.69 = (f32[4,128,256]{2,1,0:T(8,128)S(1)}, f32[128,256]{1,0:T(8,128)S(1)}, f32[128,256]{1,0:T(8,128)S(1)}, f32[128,256]{1,0:T(8,128)S(1)}) custom-call(s32[5]{0:T(128)S(1)} %stack.23.place_ref, f32[4,128,256]{2,1,0:T(8,128)S(1)} %get-tuple-element.12.kept_ref, f32[2,128,256]{2,1,0:T(8,128)S(1)} %collective-permute-done.mine_ref, ...), custom_call_target="tpu_custom_call" | custom-call | flops 402653184 | bytes 2490388 | tf_op jit(solution)/shard_map/pallas_call | solution.py:144
  29.0 0.1 collective-permute-start.9
  29.1 5.5 %collective-permute-done.11.refs_2_ = f32[128,256]{1,0:T(8,128)S(1)} collective-permute-done((f32[128,256]{1,0:T(8,128)S(1)}, f32[128,256]{1,0:T(8,128)S(1)}, u32[]{:S(2)}, u32[]{:S(2)}) %collective-permute-start.11) | collective-permute-done | bytes 131104 | tf_op jit(solution)/shard_map/ppermute | solution.py:28
  34.6 0.8 %pad_maximum_fusion = f32[384,256]{1,0:T(8,128)} fusion(f32[128,256]{1,0:T(8,128)S(1)} %collective-permute-done.12.refs_3_, f32[128,256]{1,0:T(8,128)S(1)} %collective-permute-done.11.refs_2_, f32[128,256]{1,0:T(8,128)S(1)} %collective-permute-done.10.refs_1_), kind=kLoop, calls=%fused_computation.4 | loop fusion | flops 196608 | bytes 786432 | tf_op jit(solution)/shard_map/concatenate | solution.py:188
  35.4 1.2 %convolution_bitcast_fusion.refs_4_ = f32[128,256]{1,0:T(8,128)S(1)} fusion(f32[128,512]{1,0:T(8,128)} %param.7, f32[512,512]{1,0:T(8,128)S(1)} %copy-done, s32[]{:T(128)S(6)} %select_n.20), kind=kOutput, calls=%fused_computation | convolution fusion | flops 100663296 | bytes 917508 | tf_op jit(solution)/shard_map/dot_general | solution.py:36
  36.6 0.7 collective-permute-done.13.gathered_ref
  37.3 1.4 %shard_map.70 = (f32[64,384]{1,0:T(8,128)S(1)}, f32[64,384]{1,0:T(8,128)S(1)}, f32[64,384]{1,0:T(8,128)S(1)}, f32[64,384]{1,0:T(8,128)S(1)}) custom-call(s32[5]{0:T(128)S(1)} %stack.23.place_ref, f32[4,128,256]{2,1,0:T(8,128)S(1)} %get-tuple-element.14.share_ref, f32[4,128,256]{2,1,0:T(8,128)S(1)} %collective-permute-done.9.other_ref, ...), custom_call_target="tpu_custom_call" | custom-call | flops 402653184 | bytes 2490388 | tf_op jit(solution)/shard_map/pallas_call | solution.py:144
  38.8 1.5 %collective-permute-start.16 = (f32[64,384]{1,0:T(8,128)S(1)}, f32[64,384]{1,0:T(8,128)S(1)}, u32[]{:S(2)}, u32[]{:S(2)}) collective-permute-start(f32[64,384]{1,0:T(8,128)S(1)} %get-tuple-element.21), channel_id=1, source_target_pairs={{0,18},{1,19},{2,16},{3,17},{4,22},{5,23},{6,20},{7,21},{8,26},{9,... | collective-permute-start | bytes 294920 | tf_op jit(solution)/shard_map/ppermute | solution.py:28
  40.3 1.7 %collective-permute-start.14 = (f32[64,384]{1,0:T(8,128)S(1)}, f32[64,384]{1,0:T(8,128)S(1)}, u32[]{:S(2)}, u32[]{:S(2)}) collective-permute-start(f32[64,384]{1,0:T(8,128)S(1)} %get-tuple-element.19), channel_id=1, source_target_pairs={{0,2},{1,3},{2,0},{3,1},{4,6},{5,7},{6,4},{7,5},{8,10},{9,11},{10,... | collective-permute-start | bytes 294920 | tf_op jit(solution)/shard_map/ppermute | solution.py:28
  42.0 0.3 collective-permute-start.15
  42.3 3.0 %collective-permute-done.16 = f32[64,384]{1,0:T(8,128)S(1)} collective-permute-done((f32[64,384]{1,0:T(8,128)S(1)}, f32[64,384]{1,0:T(8,128)S(1)}, u32[]{:S(2)}, u32[]{:S(2)}) %collective-permute-start.16) | collective-permute-done | bytes 98336 | tf_op jit(solution)/shard_map/ppermute | solution.py:28
  45.4 1.6 %collective-permute-done.14 = f32[64,384]{1,0:T(8,128)S(1)} collective-permute-done((f32[64,384]{1,0:T(8,128)S(1)}, f32[64,384]{1,0:T(8,128)S(1)}, u32[]{:S(2)}, u32[]{:S(2)}) %collective-permute-start.14) | collective-permute-done | bytes 98336 | tf_op jit(solution)/shard_map/ppermute | solution.py:28
  47.0 2.3 %collective-permute-start.19 = (f32[64,384]{1,0:T(8,128)S(1)}, f32[64,384]{1,0:T(8,128)S(1)}, u32[]{:S(2)}, u32[]{:S(2)}) collective-permute-start(f32[64,384]{1,0:T(8,128)S(1)} %add_add_fusion.1), channel_id=1, source_target_pairs={{0,12},{1,13},{2,14},{3,15},{4,8},{5,9},{6,10},{7,11},{8,4},{9,5},... | collective-permute-start | bytes 294920 | tf_op jit(solution)/shard_map/ppermute | solution.py:28
  49.3 2.2 %collective-permute-start.18 = (f32[64,384]{1,0:T(8,128)S(1)}, f32[64,384]{1,0:T(8,128)S(1)}, u32[]{:S(2)}, u32[]{:S(2)}) collective-permute-start(f32[64,384]{1,0:T(8,128)S(1)} %add_add_fusion.1), channel_id=1, source_target_pairs={{0,8},{1,9},{2,10},{3,11},{4,12},{5,13},{6,14},{7,15},{8,0},{9,1},... | collective-permute-start | bytes 294920 | tf_op jit(solution)/shard_map/ppermute | solution.py:28
  51.4 3.1 %collective-permute-done.19 = f32[64,384]{1,0:T(8,128)S(1)} collective-permute-done((f32[64,384]{1,0:T(8,128)S(1)}, f32[64,384]{1,0:T(8,128)S(1)}, u32[]{:S(2)}, u32[]{:S(2)}) %collective-permute-start.19) | collective-permute-done | bytes 98336 | tf_op jit(solution)/shard_map/ppermute | solution.py:28
  54.5 2.5 %collective-permute-done.17 = f32[64,384]{1,0:T(8,128)S(1)} collective-permute-done((f32[64,384]{1,0:T(8,128)S(1)}, f32[64,384]{1,0:T(8,128)S(1)}, u32[]{:S(2)}, u32[]{:S(2)}) %collective-permute-start.17) | collective-permute-done | bytes 98336 | tf_op jit(solution)/shard_map/ppermute | solution.py:28
  57.1 1.5 %collective-permute-start.22 = (f32[64,384]{1,0:T(8,128)S(1)}, f32[64,384]{1,0:T(8,128)S(1)}, u32[]{:S(2)}, u32[]{:S(2)}) collective-permute-start(f32[64,384]{1,0:T(8,128)S(1)} %add_add_fusion.refs_0_), channel_id=1, source_target_pairs={{0,18},{1,19},{2,16},{3,17},{4,22},{5,23},{6,20},{7,21},{8,26},{9,... | collective-permute-start | bytes 294920 | tf_op jit(solution)/shard_map/ppermute | solution.py:28
  58.6 1.9 %collective-permute-start.21 = (f32[64,384]{1,0:T(8,128)S(1)}, f32[64,384]{1,0:T(8,128)S(1)}, u32[]{:S(2)}, u32[]{:S(2)}) collective-permute-start(f32[64,384]{1,0:T(8,128)S(1)} %add_add_fusion.refs_0_), channel_id=1, source_target_pairs={{0,16},{1,17},{2,18},{3,19},{4,20},{5,21},{6,22},{7,23},{8,24},{9,... | collective-permute-start | bytes 294920 | tf_op jit(solution)/shard_map/ppermute | solution.py:28
  60.5 0.2 collective-permute-start.20
  60.7 2.2 %collective-permute-start.8 = (f32[128,256]{1,0:T(8,128)S(1)}, f32[128,256]{1,0:T(8,128)S(1)}, u32[]{:S(2)}, u32[]{:S(2)}) collective-permute-start(f32[128,256]{1,0:T(8,128)S(1)} %get-tuple-element.17), channel_id=1, source_target_pairs={{0,12},{1,13},{2,14},{3,15},{4,8},{5,9},{6,10},{7,11},{8,4},{9,5},... | collective-permute-start | bytes 393224 | tf_op jit(solution)/shard_map/ppermute | solution.py:28
  62.9 0.2 collective-permute-done.22.refs_3_
  63.1 2.0 %collective-permute-start.7 = (f32[128,256]{1,0:T(8,128)S(1)}, f32[128,256]{1,0:T(8,128)S(1)}, u32[]{:S(2)}, u32[]{:S(2)}) collective-permute-start(f32[128,256]{1,0:T(8,128)S(1)} %get-tuple-element.16), channel_id=1, source_target_pairs={{0,8},{1,9},{2,10},{3,11},{4,12},{5,13},{6,14},{7,15},{8,0},{9,1},... | collective-permute-start | bytes 393224 | tf_op jit(solution)/shard_map/ppermute | solution.py:28
  65.2 0.3 collective-permute-done.20.refs_1_
  65.5 0.1 collective-permute-start.23
  65.6 3.3 %collective-permute-done.8 = f32[128,256]{1,0:T(8,128)S(1)} collective-permute-done((f32[128,256]{1,0:T(8,128)S(1)}, f32[128,256]{1,0:T(8,128)S(1)}, u32[]{:S(2)}, u32[]{:S(2)}) %collective-permute-start.8) | collective-permute-done | bytes 131104 | tf_op jit(solution)/shard_map/ppermute | solution.py:28
  68.9 1.5 %collective-permute-done.6 = f32[128,256]{1,0:T(8,128)S(1)} collective-permute-done((f32[128,256]{1,0:T(8,128)S(1)}, f32[128,256]{1,0:T(8,128)S(1)}, u32[]{:S(2)}, u32[]{:S(2)}) %collective-permute-start.6) | collective-permute-done | bytes 131104 | tf_op jit(solution)/shard_map/ppermute | solution.py:28
  70.4 3.7 %collective-permute-done.7 = f32[128,256]{1,0:T(8,128)S(1)} collective-permute-done((f32[128,256]{1,0:T(8,128)S(1)}, f32[128,256]{1,0:T(8,128)S(1)}, u32[]{:S(2)}, u32[]{:S(2)}) %collective-permute-start.7) | collective-permute-done | bytes 131104 | tf_op jit(solution)/shard_map/ppermute | solution.py:28
  74.1 0.7 fusion.2
  74.8 1.5 %shard_map.71 = f32[512,256]{1,0:T(8,128)} custom-call(s32[5]{0:T(128)S(1)} %stack.23.place_ref, f32[512,256]{1,0:T(8,128)S(1)} %copy-done.2, f32[256,128]{1,0:T(8,128)S(1)} %collective-permute-done.23.other_ref, f32[64,384]{1,0:T(8,128)S(1)} %add_add_fusion.refs_0_, f32[64,384]{1,0:T(8,128)S(1)} %collective-permute-done.20.refs_1_, ...), custom_call_target="tpu_custom_call" | custom-call | bytes 1572884 | tf_op jit(solution)/shard_map/pallas_call | solution.py:144
  (27 shorter events, 0.1 us)
Async XLA Ops:
  0.6 6.0 %copy-start = (f32[512,512]{1,0:T(8,128)S(1)}, f32[512,512]{1,0:T(8,128)}, u32[]{:S(2)}) copy-start(f32[512,512]{1,0:T(8,128)} %param.8) | copy-start | bytes 3145732
  0.7 0.8 %copy-start.4 = (s32[8,2]{0,1:T(2,128)S(1)}, s32[8,2]{0,1:T(2,128)}, u32[]{:S(2)}) copy-start(s32[8,2]{0,1:T(2,128)} %param.6) | copy-start | bytes 196
  1.6 1.2 %copy-start.1 = (f32[1024,256]{1,0:T(8,128)S(1)}, f32[1024,256]{1,0:T(8,128)}, u32[]{:S(2)}) copy-start(f32[1024,256]{1,0:T(8,128)} %full_ref.1) | copy-start | bytes 3145732
  2.8 3.8 %copy-start.3 = (f32[128,512]{1,0:T(8,128)S(1)}, f32[128,512]{1,0:T(8,128)}, u32[]{:S(2)}) copy-start(f32[128,512]{1,0:T(8,128)} %param.7) | copy-start | bytes 786436
  3.6 11.4 %collective-permute-start = (f32[2,128,256]{2,1,0:T(8,128)S(1)}, f32[2,128,256]{2,1,0:T(8,128)S(1)}, u32[]{:S(2)}, u32[]{:S(2)}) collective-permute-start(f32[2,128,256]{2,1,0:T(8,128)S(1)} %get-tuple-element.13), channel_id=1, source_target_pairs={{0,2},{1,3},{2,0},{3,1},{4,6},{5,7},{6,4},{7,5},{8,10},{9,11},{10,... | collective-permute-start | bytes 786440 | tf_op jit(solution)/shard_map/ppermute | solution.py:28
  6.9 8.1 %collective-permute-start.2 = (f32[128,256]{1,0:T(8,128)S(1)}, f32[128,256]{1,0:T(8,128)S(1)}, u32[]{:S(2)}, u32[]{:S(2)}) collective-permute-start(f32[128,256]{1,0:T(8,128)S(1)} %convolution_bitcast_fusion.1.refs_0_), channel_id=1, source_target_pairs={{0,0},{1,1},{2,16},{3,17},{4,2},{5,3},{6,18},{7,19},{8,4},{9,5},{1... | collective-permute-start | bytes 393224 | tf_op jit(solution)/shard_map/ppermute | solution.py:28
  15.0 12.8 %collective-permute-start.1 = (f32[2,128,256]{2,1,0:T(8,128)S(1)}, f32[2,128,256]{2,1,0:T(8,128)S(1)}, u32[]{:S(2)}, u32[]{:S(2)}) collective-permute-start(f32[2,128,256]{2,1,0:T(8,128)S(1)} %collective-permute-done.mine_ref), channel_id=1, source_target_pairs={{0,1},{1,0},{2,3},{3,2},{4,5},{5,4},{6,7},{7,6},{8,9},{9,8},{10,11... | collective-permute-start | bytes 786440 | tf_op jit(solution)/shard_map/ppermute | solution.py:28
  15.0 8.5 %collective-permute-start.3 = (f32[128,256]{1,0:T(8,128)S(1)}, f32[128,256]{1,0:T(8,128)S(1)}, u32[]{:S(2)}, u32[]{:S(2)}) collective-permute-start(f32[128,256]{1,0:T(8,128)S(1)} %collective-permute-done.2.refs_0_), channel_id=1, source_target_pairs={{0,16},{1,17},{2,18},{3,19},{4,20},{5,21},{6,22},{7,23},{8,24},{9,... | collective-permute-start | bytes 393224 | tf_op jit(solution)/shard_map/ppermute | solution.py:28
  17.2 7.8 %collective-permute-start.4 = (f32[128,256]{1,0:T(8,128)S(1)}, f32[128,256]{1,0:T(8,128)S(1)}, u32[]{:S(2)}, u32[]{:S(2)}) collective-permute-start(f32[128,256]{1,0:T(8,128)S(1)} %collective-permute-done.2.refs_0_), channel_id=1, source_target_pairs={{0,2},{1,3},{2,0},{3,1},{4,6},{5,7},{6,4},{7,5},{8,10},{9,11},{10,... | collective-permute-start | bytes 393224 | tf_op jit(solution)/shard_map/ppermute | solution.py:28
  17.6 10.3 %collective-permute-start.5 = (f32[128,256]{1,0:T(8,128)S(1)}, f32[128,256]{1,0:T(8,128)S(1)}, u32[]{:S(2)}, u32[]{:S(2)}) collective-permute-start(f32[128,256]{1,0:T(8,128)S(1)} %collective-permute-done.2.refs_0_), channel_id=1, source_target_pairs={{0,18},{1,19},{2,16},{3,17},{4,22},{5,23},{6,20},{7,21},{8,26},{9,... | collective-permute-start | bytes 393224 | tf_op jit(solution)/shard_map/ppermute | solution.py:28
  19.0 10.1 %collective-permute-start.12 = (f32[128,256]{1,0:T(8,128)S(1)}, f32[128,256]{1,0:T(8,128)S(1)}, u32[]{:S(2)}, u32[]{:S(2)}) collective-permute-start(f32[128,256]{1,0:T(8,128)S(1)} %convolution_bitcast_fusion.1.refs_0_), channel_id=1, source_target_pairs={{0,12},{1,13},{2,14},{3,15},{4,8},{5,9},{6,10},{7,11},{8,4},{9,5},... | collective-permute-start | bytes 393224 | tf_op jit(solution)/shard_map/ppermute | solution.py:28
  23.5 11.1 %collective-permute-start.11 = (f32[128,256]{1,0:T(8,128)S(1)}, f32[128,256]{1,0:T(8,128)S(1)}, u32[]{:S(2)}, u32[]{:S(2)}) collective-permute-start(f32[128,256]{1,0:T(8,128)S(1)} %convolution_bitcast_fusion.1.refs_0_), channel_id=1, source_target_pairs={{0,8},{1,9},{2,10},{3,11},{4,12},{5,13},{6,14},{7,15},{8,0},{9,1},... | collective-permute-start | bytes 393224 | tf_op jit(solution)/shard_map/ppermute | solution.py:28
  25.0 9.7 %collective-permute-start.10 = (f32[128,256]{1,0:T(8,128)S(1)}, f32[128,256]{1,0:T(8,128)S(1)}, u32[]{:S(2)}, u32[]{:S(2)}) collective-permute-start(f32[128,256]{1,0:T(8,128)S(1)} %convolution_bitcast_fusion.1.refs_0_), channel_id=1, source_target_pairs={{0,4},{1,5},{2,6},{3,7},{4,0},{5,1},{6,2},{7,3},{8,12},{9,13},{10,... | collective-permute-start | bytes 393224 | tf_op jit(solution)/shard_map/ppermute | solution.py:28
  29.0 8.3 %collective-permute-start.9 = (f32[4,128,256]{2,1,0:T(8,128)S(1)}, f32[4,128,256]{2,1,0:T(8,128)S(1)}, u32[]{:S(2)}, u32[]{:S(2)}) collective-permute-start(f32[4,128,256]{2,1,0:T(8,128)S(1)} %get-tuple-element.14.share_ref), channel_id=1, source_target_pairs={{0,1},{1,0},{2,3},{3,2},{4,5},{5,4},{6,7},{7,6},{8,9},{9,8},{10,11... | collective-permute-start | bytes 1572872 | tf_op jit(solution)/shard_map/ppermute | solution.py:28
  35.4 1.9 %collective-permute-start.13 = (f32[384,256]{1,0:T(8,128)}, f32[384,256]{1,0:T(8,128)S(1)}, u32[]{:S(2)}, u32[]{:S(2)}) collective-permute-start(f32[384,256]{1,0:T(8,128)} %pad_maximum_fusion), channel_id=1, source_target_pairs={{0,1},{1,0},{2,3},{3,2},{4,5},{5,4},{6,7},{7,6},{8,9},{9,8},{10,11... | collective-permute-start | bytes 1179656 | tf_op jit(solution)/shard_map/ppermute | solution.py:28
  38.8 6.6 %collective-permute-start.16 = (f32[64,384]{1,0:T(8,128)S(1)}, f32[64,384]{1,0:T(8,128)S(1)}, u32[]{:S(2)}, u32[]{:S(2)}) collective-permute-start(f32[64,384]{1,0:T(8,128)S(1)} %get-tuple-element.21), channel_id=1, source_target_pairs={{0,18},{1,19},{2,16},{3,17},{4,22},{5,23},{6,20},{7,21},{8,26},{9,... | collective-permute-start | bytes 294920 | tf_op jit(solution)/shard_map/ppermute | solution.py:28
  40.3 6.7 %collective-permute-start.14 = (f32[64,384]{1,0:T(8,128)S(1)}, f32[64,384]{1,0:T(8,128)S(1)}, u32[]{:S(2)}, u32[]{:S(2)}) collective-permute-start(f32[64,384]{1,0:T(8,128)S(1)} %get-tuple-element.19), channel_id=1, source_target_pairs={{0,2},{1,3},{2,0},{3,1},{4,6},{5,7},{6,4},{7,5},{8,10},{9,11},{10,... | collective-permute-start | bytes 294920 | tf_op jit(solution)/shard_map/ppermute | solution.py:28
  42.0 4.9 %collective-permute-start.15 = (f32[64,384]{1,0:T(8,128)S(1)}, f32[64,384]{1,0:T(8,128)S(1)}, u32[]{:S(2)}, u32[]{:S(2)}) collective-permute-start(f32[64,384]{1,0:T(8,128)S(1)} %get-tuple-element.20), channel_id=1, source_target_pairs={{0,16},{1,17},{2,18},{3,19},{4,20},{5,21},{6,22},{7,23},{8,24},{9,... | collective-permute-start | bytes 294920 | tf_op jit(solution)/shard_map/ppermute | solution.py:28
  47.0 7.5 %collective-permute-start.19 = (f32[64,384]{1,0:T(8,128)S(1)}, f32[64,384]{1,0:T(8,128)S(1)}, u32[]{:S(2)}, u32[]{:S(2)}) collective-permute-start(f32[64,384]{1,0:T(8,128)S(1)} %add_add_fusion.1), channel_id=1, source_target_pairs={{0,12},{1,13},{2,14},{3,15},{4,8},{5,9},{6,10},{7,11},{8,4},{9,5},... | collective-permute-start | bytes 294920 | tf_op jit(solution)/shard_map/ppermute | solution.py:28
  49.3 7.8 %collective-permute-start.17 = (f32[64,384]{1,0:T(8,128)S(1)}, f32[64,384]{1,0:T(8,128)S(1)}, u32[]{:S(2)}, u32[]{:S(2)}) collective-permute-start(f32[64,384]{1,0:T(8,128)S(1)} %add_add_fusion.1), channel_id=1, source_target_pairs={{0,4},{1,5},{2,6},{3,7},{4,0},{5,1},{6,2},{7,3},{8,12},{9,13},{10,... | collective-permute-start | bytes 294920 | tf_op jit(solution)/shard_map/ppermute | solution.py:28
  49.3 7.8 %collective-permute-start.18 = (f32[64,384]{1,0:T(8,128)S(1)}, f32[64,384]{1,0:T(8,128)S(1)}, u32[]{:S(2)}, u32[]{:S(2)}) collective-permute-start(f32[64,384]{1,0:T(8,128)S(1)} %add_add_fusion.1), channel_id=1, source_target_pairs={{0,8},{1,9},{2,10},{3,11},{4,12},{5,13},{6,14},{7,15},{8,0},{9,1},... | collective-permute-start | bytes 294920 | tf_op jit(solution)/shard_map/ppermute | solution.py:28
  57.1 6.1 %collective-permute-start.22 = (f32[64,384]{1,0:T(8,128)S(1)}, f32[64,384]{1,0:T(8,128)S(1)}, u32[]{:S(2)}, u32[]{:S(2)}) collective-permute-start(f32[64,384]{1,0:T(8,128)S(1)} %add_add_fusion.refs_0_), channel_id=1, source_target_pairs={{0,18},{1,19},{2,16},{3,17},{4,22},{5,23},{6,20},{7,21},{8,26},{9,... | collective-permute-start | bytes 294920 | tf_op jit(solution)/shard_map/ppermute | solution.py:28
  58.6 6.6 %collective-permute-start.21 = (f32[64,384]{1,0:T(8,128)S(1)}, f32[64,384]{1,0:T(8,128)S(1)}, u32[]{:S(2)}, u32[]{:S(2)}) collective-permute-start(f32[64,384]{1,0:T(8,128)S(1)} %add_add_fusion.refs_0_), channel_id=1, source_target_pairs={{0,16},{1,17},{2,18},{3,19},{4,20},{5,21},{6,22},{7,23},{8,24},{9,... | collective-permute-start | bytes 294920 | tf_op jit(solution)/shard_map/ppermute | solution.py:28
  60.5 5.0 %collective-permute-start.20 = (f32[64,384]{1,0:T(8,128)S(1)}, f32[64,384]{1,0:T(8,128)S(1)}, u32[]{:S(2)}, u32[]{:S(2)}) collective-permute-start(f32[64,384]{1,0:T(8,128)S(1)} %add_add_fusion.refs_0_), channel_id=1, source_target_pairs={{0,2},{1,3},{2,0},{3,1},{4,6},{5,7},{6,4},{7,5},{8,10},{9,11},{10,... | collective-permute-start | bytes 294920 | tf_op jit(solution)/shard_map/ppermute | solution.py:28
  60.7 8.2 %collective-permute-start.8 = (f32[128,256]{1,0:T(8,128)S(1)}, f32[128,256]{1,0:T(8,128)S(1)}, u32[]{:S(2)}, u32[]{:S(2)}) collective-permute-start(f32[128,256]{1,0:T(8,128)S(1)} %get-tuple-element.17), channel_id=1, source_target_pairs={{0,12},{1,13},{2,14},{3,15},{4,8},{5,9},{6,10},{7,11},{8,4},{9,5},... | collective-permute-start | bytes 393224 | tf_op jit(solution)/shard_map/ppermute | solution.py:28
  62.9 7.5 %collective-permute-start.6 = (f32[128,256]{1,0:T(8,128)S(1)}, f32[128,256]{1,0:T(8,128)S(1)}, u32[]{:S(2)}, u32[]{:S(2)}) collective-permute-start(f32[128,256]{1,0:T(8,128)S(1)} %get-tuple-element.15), channel_id=1, source_target_pairs={{0,4},{1,5},{2,6},{3,7},{4,0},{5,1},{6,2},{7,3},{8,12},{9,13},{10,... | collective-permute-start | bytes 393224 | tf_op jit(solution)/shard_map/ppermute | solution.py:28
  63.1 11.0 %collective-permute-start.7 = (f32[128,256]{1,0:T(8,128)S(1)}, f32[128,256]{1,0:T(8,128)S(1)}, u32[]{:S(2)}, u32[]{:S(2)}) collective-permute-start(f32[128,256]{1,0:T(8,128)S(1)} %get-tuple-element.16), channel_id=1, source_target_pairs={{0,8},{1,9},{2,10},{3,11},{4,12},{5,13},{6,14},{7,15},{8,0},{9,1},... | collective-permute-start | bytes 393224 | tf_op jit(solution)/shard_map/ppermute | solution.py:28
  65.1 9.7 %copy-start.2 = (f32[512,256]{1,0:T(8,128)S(1)}, f32[512,256]{1,0:T(8,128)}, u32[]{:S(2)}) copy-start(f32[512,256]{1,0:T(8,128)} %pivot_ref.1) | copy-start | bytes 1572868
  65.5 9.3 %collective-permute-start.23 = (f32[256,128]{1,0:T(8,128)S(1)}, f32[256,128]{1,0:T(8,128)S(1)}, u32[]{:S(2)}, u32[]{:S(2)}) collective-permute-start(f32[256,128]{1,0:T(8,128)S(1)} %pad_maximum_fusion.1), channel_id=1, source_target_pairs={{0,1},{1,0},{2,3},{3,2},{4,5},{5,4},{6,7},{7,6},{8,9},{9,8},{10,11... | collective-permute-start | bytes 393224 | tf_op jit(solution)/shard_map/ppermute | solution.py:28

commit v2 on v1

--- a/solution.py
+++ b/solution.py
@@ -10,6 +10,7 @@
 
 AXES = ("row", "col", "rep")
 PAIR = 2
+ROOM = 56000000
 F32, BF16 = jnp.float32, jnp.bfloat16
 
 
@@ -32,10 +33,6 @@
     return send(block, lambda r, c, p: (r, c, 1 - p))
 
 
-def dot(left, right):
-    return jnp.dot(left, right, precision=lax.Precision.HIGH, preferred_element_type=F32)
-
-
 def split(value):
     high = value.astype(BF16)
     return high, (value - high.astype(F32)).astype(BF16)
@@ -55,14 +52,38 @@
     return pl.ds(pl.multiple_of(index * size, size), size)
 
 
-def prepare_kernel(planes, rows, tile, place_ref, marks_ref, full_ref, kept_ref, given_ref):
+def front_kernel(planes, rows, place_ref, marks_ref, factor_ref, normalizer_ref, full_ref, *refs):
+    normed_ref, other_ref, kept_ref, given_ref, *scratch = refs
+    factor_in, normalizer_in, full_in, sems = scratch
     row, plane, side, rep = (place_ref[i] for i in range(4))
+    tile, half = normed_ref.shape
     cut = planes // 2
+    band = PAIR * tile
+    loads = [
+        pltpu.make_async_copy(factor_ref, factor_in, sems.at[0]),
+    ] + [
+        pltpu.make_async_copy(
+            normalizer_ref.at[:, tile_at(columns, half)], normalizer_in.at[i], sems.at[1 + i]
+        )
+        for i, columns in enumerate((rep, 1 - rep))
+    ] + [
+        pltpu.make_async_copy(full_ref.at[tile_at(plane ^ k, band), :], full_in.at[k], sems.at[3 + k])
+        for k in range(planes)
+    ]
+    for load in loads:
+        load.start()
+    for load in loads[:2]:
+        load.wait()
+    left = split(factor_in[...])
+    normed_ref[...] = split_dot(left, split(normalizer_in[0]))
+    for load in loads[2:]:
+        load.wait()
+    other_ref[...] = split_dot(left, split(normalizer_in[1]))
 
     def masked(k, wanted, m):
-        source, across = (plane ^ k) * PAIR + wanted, row ^ m
-        mark = marks_ref[source, across].astype(F32)
-        return full_ref[tile_at(source, tile), tile_at(across, tile)] * mark
+        across = row ^ m
+        mark = marks_ref[across, (plane ^ k) * PAIR + wanted].astype(F32)
+        return full_in[k, tile_at(wanted, tile), tile_at(across, tile)] * mark
 
     for m in range(rows):
         columns = pl.ds(m * tile, tile)
@@ -138,16 +159,22 @@
         out_ref[half:, :] = pivot_ref[half:, :] + 0.5 * total_ref[:, :half]
 
 
-def call(kernel, shapes, in_smem, args, scratch=(), flops=0):
-    smem, vmem = pl.BlockSpec(memory_space=pltpu.SMEM), pl.BlockSpec(memory_space=pltpu.VMEM)
+def call(kernel, shapes, spaces, args, scratch=(), flops=0, room=None):
+    vmem = pl.BlockSpec(memory_space=pltpu.VMEM)
+    space = {
+        "s": pl.BlockSpec(memory_space=pltpu.SMEM),
+        "h": pl.BlockSpec(memory_space=pltpu.HBM),
+        "v": vmem,
+    }
+    spaces += "v" * (len(args) - len(spaces))
     moved = sum(4 * a.size for a in args) + sum(4 * functools.reduce(int.__mul__, s) for s in shapes)
     return pl.pallas_call(
         kernel,
         out_shape=[jax.ShapeDtypeStruct(shape, F32) for shape in shapes],
-        in_specs=[smem] * in_smem + [vmem] * (len(args) - in_smem),
+        in_specs=[space[one] for one in spaces],
         out_specs=[vmem] * len(shapes),
-        scratch_shapes=[pltpu.VMEM(shape, F32) for shape in scratch],
-        compiler_params=pltpu.CompilerParams(vmem_limit_bytes=3 * moved + 2**21),
+        scratch_shapes=[pltpu.VMEM(one, F32) if isinstance(one, tuple) else one for one in scratch],
+        compiler_params=pltpu.CompilerParams(vmem_limit_bytes=room or 3 * moved + 2**21),
         cost_estimate=pl.CostEstimate(flops=flops, bytes_accessed=moved, transcendentals=0),
     )(*args)
 
@@ -162,10 +189,21 @@
     place = jnp.stack([row, plane, side, rep, row * PAIR + side]).astype(jnp.int32)
     depth = rows * tile
 
-    def half_of(matrix, index):
-        return lax.dynamic_slice_in_dim(matrix, index * half, half, 1)
-
-    own_normed = dot(factor, half_of(factor_normalizer, rep))
+    cut = planes // 2
+    inner = factor.shape[1]
+    own_normed, other_normed, kept, given = call(
+        functools.partial(front_kernel, planes, rows),
+        [(tile, half), (tile, half), (planes, tile, depth), (cut, tile, depth)],
+        "sshhh",
+        [place, tile_structure.T, factor, factor_normalizer, ancestor_inverse],
+        [
+            (tile, inner),
+            (PAIR, inner, half),
+            (planes, PAIR * tile, depth),
+            pltpu.SemaphoreType.DMA((3 + planes,)),
+        ],
+        room=ROOM,
+    )
 
     def to_plane(r, c, p):
         block = r * cols + c
@@ -185,34 +223,27 @@
     arrived = [send(own_normed, to_plane)]
     arrived += [send(arrived[0], beside(k)) for k in range(1, members)]
     strip = [own_normed] + [send(own_normed, along(k)) for k in range(1, planes)]
-    other_strip = swap_core(jnp.concatenate(strip[1:], 0))
-    other_normed = dot(factor, half_of(factor_normalizer, 1 - rep))
-
-    cut = planes // 2
-    kept, given = call(
-        functools.partial(prepare_kernel, planes, rows, tile),
-        [(planes, tile, depth), (cut, tile, depth)],
-        2,
-        [place, tile_structure, ancestor_inverse],
-    )
+    packed = jnp.concatenate(strip[1:], 0)
+    other_strip = swap_core(packed)
     mine = send(given, lambda r, c, p: (r, c ^ 1, p))
     theirs = swap_core(mine)
     product, *shares = call(
         functools.partial(product_kernel, planes, members),
         [(planes, tile, half)] + [(tile, half)] * (planes - 1),
-        1,
+        "s",
         [place, kept, mine, theirs, *arrived],
         flops=12 * planes * tile * depth * half,
     )
     other_product = swap_core(product)
-    ancestor_columns = -(product[0] + sum(send(shares[k - 1], along(k)) for k in range(1, planes)))
+    landed = [send(shares[k - 1], along(k)) for k in range(1, planes)]
+    ancestor_columns = -(product[0] + sum(landed))
 
     quarter, step = half // 2, half // members
     width = half + quarter
     parts = call(
         functools.partial(coupling_kernel, members, planes),
         [(step, width)] * members,
-        1,
+        "s",
         [place, product, other_product, other_strip, *strip, other_normed],
         [(half, width)],
         flops=12 * planes * tile * half * half,
@@ -232,7 +263,7 @@
     (diag_block,) = call(
         functools.partial(finish_kernel, members),
         [pivot_inverse.shape],
-        1,
+        "s",
         [place, pivot_inverse, other_between, *parts],
         [(half, width), (half, quarter)],
     )

time: 76.5 us -> 77 us (level)
  Pallas kernels: 4.87 us -> 7.66 us
  matrix products: 1.53 us -> 0 us
  waiting for transfers between devices: 32.9 us -> 34.1 us
  starting transfers between devices: 32.5 us -> 31.7 us
    pallas_call x4, Pallas kernels: 4.87 us -> 7.66 us  [call(): pl.pallas_call(kernel, out_shape=[jax.ShapeDtypeStruct(shape, F32) for sh...]
    dot_general x2 -> x0, matrix products: 1.53 us -> none  [dot(): jnp.dot(left, right, precision=lax.Precision.HIGH, preferred_element_type...]
    ppermute x24, waiting for transfers between devices: 32.9 us -> 34.1 us  [send(): return lax.ppermute(block, AXES, route)]
    ppermute x24, starting transfers between devices: 32.5 us -> 31.7 us  [send(): return lax.ppermute(block, AXES, route)]
    unnamed x11 -> x6, local copies, waits for them, and re-layouts: 2.07 us -> 1.72 us
  transfers between devices with their start and end apart: 24 -> 24, of which waited for: 12 -> 11; matrix products, arithmetic and copies ran while one was open for 4% -> 1% of each run, Pallas kernels for 2% -> 1%
where the time goes in v2:
time: 77 us; the launch traced here: 76.8 us
  waiting for transfers between devices  34.1 us (44%)
  starting transfers between devices  31.7 us (41%)
  Pallas kernels  7.66 us (10%)
  local copies, waits for them, and re-layouts  1.82 us (2%)
  between operations  0.78 us (1%)
  other arithmetic  0.77 us (1%)
    ppermute x24, waiting for transfers between devices, send(): return lax.ppermute(block, AXES, route)  34.1 us
    ppermute x24, starting transfers between devices, send(): return lax.ppermute(block, AXES, route)  31.7 us
    pallas_call x4, Pallas kernels, call(): pl.pallas_call(kernel, out_shape=[jax.ShapeDtypeStruct(shape, F32) for sh...  7.66 us
    unnamed x6, local copies, waits for them, and re-layouts  1.72 us
  transfers between devices with their start and end apart: 24, of which 11 were waited for; matrix products, arithmetic and copies ran while one was open for 1% of the time, Pallas kernels for 1%

profile of v2, /device:TPU:0, one launch (start us, length us, event | category | flops | bytes accessed | tf_op | source)
XLA Modules:
  0.0 76.8 jit_solution(8460869712378684936)
XLA Ops:
  0.7 0.1 stack.23.place_ref
  0.7 0.7 copy-done.2
  1.4 3.5 %shard_map.68 = (f32[128,256]{1,0:T(8,128)S(1)}, f32[128,256]{1,0:T(8,128)S(1)}, f32[4,128,256]{2,1,0:T(8,128)}, f32[2,128,256]{2,1,0:T(8,128)S(1)}) custom-call(s32[5]{0:T(128)S(1)} %stack.23.place_ref, s32[2,8]{1,0:T(2,128)S(1)} %bitcast.10, f32[128,512]{1,0:T(8,128)} %factor_ref.1, f32[512,512]{1,0:T(8,128)} %normalizer_ref.1, f32[1024,256]{1,0:T(8,128)} %full_ref.1), custom_call_target="tpu_custom_call" | custom-call | bytes 3407956 | tf_op jit(solution)/shard_map/pallas_call | solution.py:171
  4.9 3.0 %collective-permute-start = (f32[2,128,256]{2,1,0:T(8,128)S(1)}, f32[2,128,256]{2,1,0:T(8,128)S(1)}, u32[]{:S(2)}, u32[]{:S(2)}) collective-permute-start(f32[2,128,256]{2,1,0:T(8,128)S(1)} %get-tuple-element.15), channel_id=1, source_target_pairs={{0,2},{1,3},{2,0},{3,1},{4,6},{5,7},{6,4},{7,5},{8,10},{9,11},{10,... | collective-permute-start | bytes 786440 | tf_op jit(solution)/shard_map/ppermute | solution.py:29
  8.0 0.7 collective-permute-start.2
  8.6 7.7 %collective-permute-done.mine_ref = f32[2,128,256]{2,1,0:T(8,128)S(1)} collective-permute-done((f32[2,128,256]{2,1,0:T(8,128)S(1)}, f32[2,128,256]{2,1,0:T(8,128)S(1)}, u32[]{:S(2)}, u32[]{:S(2)}) %collective-permute-start) | collective-permute-done | bytes 262176 | tf_op jit(solution)/shard_map/ppermute | solution.py:29
  16.3 0.0 collective-permute-start.1
  16.3 2.2 %collective-permute-start.3 = (f32[128,256]{1,0:T(8,128)S(1)}, f32[128,256]{1,0:T(8,128)S(1)}, u32[]{:S(2)}, u32[]{:S(2)}) collective-permute-start(f32[128,256]{1,0:T(8,128)S(1)} %collective-permute-done.2.refs_0_), channel_id=1, source_target_pairs={{0,16},{1,17},{2,18},{3,19},{4,20},{5,21},{6,22},{7,23},{8,24},{9,... | collective-permute-start | bytes 393224 | tf_op jit(solution)/shard_map/ppermute | solution.py:29
  18.5 0.4 collective-permute-start.4
  18.9 1.4 %collective-permute-start.5 = (f32[128,256]{1,0:T(8,128)S(1)}, f32[128,256]{1,0:T(8,128)S(1)}, u32[]{:S(2)}, u32[]{:S(2)}) collective-permute-start(f32[128,256]{1,0:T(8,128)S(1)} %collective-permute-done.2.refs_0_), channel_id=1, source_target_pairs={{0,18},{1,19},{2,16},{3,17},{4,22},{5,23},{6,20},{7,21},{8,26},{9,... | collective-permute-start | bytes 393224 | tf_op jit(solution)/shard_map/ppermute | solution.py:29
  20.3 4.5 %collective-permute-start.12 = (f32[128,256]{1,0:T(8,128)S(1)}, f32[128,256]{1,0:T(8,128)S(1)}, u32[]{:S(2)}, u32[]{:S(2)}) collective-permute-start(f32[128,256]{1,0:T(8,128)S(1)} %get-tuple-element.16.refs_0_), channel_id=1, source_target_pairs={{0,12},{1,13},{2,14},{3,15},{4,8},{5,9},{6,10},{7,11},{8,4},{9,5},... | collective-permute-start | bytes 393224 | tf_op jit(solution)/shard_map/ppermute | solution.py:29
  24.8 0.0 collective-permute-done.3.refs_1_
  24.8 1.1 %collective-permute-start.11 = (f32[128,256]{1,0:T(8,128)S(1)}, f32[128,256]{1,0:T(8,128)S(1)}, u32[]{:S(2)}, u32[]{:S(2)}) collective-permute-start(f32[128,256]{1,0:T(8,128)S(1)} %get-tuple-element.16.refs_0_), channel_id=1, source_target_pairs={{0,8},{1,9},{2,10},{3,11},{4,12},{5,13},{6,14},{7,15},{8,0},{9,1},... | collective-permute-start | bytes 393224 | tf_op jit(solution)/shard_map/ppermute | solution.py:29
  26.0 0.0 collective-permute-done.4.refs_2_
  26.0 2.9 %collective-permute-start.10 = (f32[128,256]{1,0:T(8,128)S(1)}, f32[128,256]{1,0:T(8,128)S(1)}, u32[]{:S(2)}, u32[]{:S(2)}) collective-permute-start(f32[128,256]{1,0:T(8,128)S(1)} %get-tuple-element.16.refs_0_), channel_id=1, source_target_pairs={{0,4},{1,5},{2,6},{3,7},{4,0},{5,1},{6,2},{7,3},{8,12},{9,13},{10,... | collective-permute-start | bytes 393224 | tf_op jit(solution)/shard_map/ppermute | solution.py:29
  28.9 1.0 %copy-done.1 = f32[4,128,256]{2,1,0:T(8,128)S(1)} copy-done((f32[4,128,256]{2,1,0:T(8,128)S(1)}, f32[4,128,256]{2,1,0:T(8,128)}, u32[]{:S(2)}) %copy-start.1) | copy-done | bytes 524312
  29.9 1.1 %shard_map.69 = (f32[4,128,256]{2,1,0:T(8,128)S(1)}, f32[128,256]{1,0:T(8,128)S(1)}, f32[128,256]{1,0:T(8,128)S(1)}, f32[128,256]{1,0:T(8,128)S(1)}) custom-call(s32[5]{0:T(128)S(1)} %stack.23.place_ref, f32[4,128,256]{2,1,0:T(8,128)S(1)} %copy-done.1, f32[2,128,256]{2,1,0:T(8,128)S(1)} %collective-permute-done.mine_ref, ...), custom_call_target="tpu_custom_call" | custom-call | flops 402653184 | bytes 2490388 | tf_op jit(solution)/shard_map/pallas_call | solution.py:171
  31.0 0.1 collective-permute-start.9
  31.1 0.0 collective-permute-done.12.refs_3_
  31.1 4.8 %collective-permute-done.11.refs_2_ = f32[128,256]{1,0:T(8,128)S(1)} collective-permute-done((f32[128,256]{1,0:T(8,128)S(1)}, f32[128,256]{1,0:T(8,128)S(1)}, u32[]{:S(2)}, u32[]{:S(2)}) %collective-permute-start.11) | collective-permute-done | bytes 131104 | tf_op jit(solution)/shard_map/ppermute | solution.py:29
  36.0 0.0 collective-permute-done.10.refs_1_
  36.0 0.1 collective-permute-start.13
  36.1 1.7 %collective-permute-done.13.gathered_ref = f32[384,256]{1,0:T(8,128)S(1)} collective-permute-done((f32[384,256]{1,0:T(8,128)S(1)}, f32[384,256]{1,0:T(8,128)S(1)}, u32[]{:S(2)}, u32[]{:S(2)}) %collective-permute-start.13) | collective-permute-done | bytes 393248 | tf_op jit(solution)/shard_map/ppermute | solution.py:29
  37.8 0.0 collective-permute-done.9.other_ref
  37.8 1.5 %shard_map.70 = (f32[64,384]{1,0:T(8,128)S(1)}, f32[64,384]{1,0:T(8,128)S(1)}, f32[64,384]{1,0:T(8,128)S(1)}, f32[64,384]{1,0:T(8,128)S(1)}) custom-call(s32[5]{0:T(128)S(1)} %stack.23.place_ref, f32[4,128,256]{2,1,0:T(8,128)S(1)} %get-tuple-element.17.share_ref, f32[4,128,256]{2,1,0:T(8,128)S(1)} %collective-permute-done.9.other_ref, ...), custom_call_target="tpu_custom_call" | custom-call | flops 402653184 | bytes 2490388 | tf_op jit(solution)/shard_map/pallas_call | solution.py:171
  39.3 1.5 %collective-permute-start.16 = (f32[64,384]{1,0:T(8,128)S(1)}, f32[64,384]{1,0:T(8,128)S(1)}, u32[]{:S(2)}, u32[]{:S(2)}) collective-permute-start(f32[64,384]{1,0:T(8,128)S(1)} %get-tuple-element.25), channel_id=1, source_target_pairs={{0,18},{1,19},{2,16},{3,17},{4,22},{5,23},{6,20},{7,21},{8,26},{9,... | collective-permute-start | bytes 294920 | tf_op jit(solution)/shard_map/ppermute | solution.py:29
  40.8 1.7 %collective-permute-start.14 = (f32[64,384]{1,0:T(8,128)S(1)}, f32[64,384]{1,0:T(8,128)S(1)}, u32[]{:S(2)}, u32[]{:S(2)}) collective-permute-start(f32[64,384]{1,0:T(8,128)S(1)} %get-tuple-element.23), channel_id=1, source_target_pairs={{0,2},{1,3},{2,0},{3,1},{4,6},{5,7},{6,4},{7,5},{8,10},{9,11},{10,... | collective-permute-start | bytes 294920 | tf_op jit(solution)/shard_map/ppermute | solution.py:29
  42.5 0.3 collective-permute-start.15
  42.8 3.1 %collective-permute-done.16 = f32[64,384]{1,0:T(8,128)S(1)} collective-permute-done((f32[64,384]{1,0:T(8,128)S(1)}, f32[64,384]{1,0:T(8,128)S(1)}, u32[]{:S(2)}, u32[]{:S(2)}) %collective-permute-start.16) | collective-permute-done | bytes 98336 | tf_op jit(solution)/shard_map/ppermute | solution.py:29
  45.9 1.6 %collective-permute-done.14 = f32[64,384]{1,0:T(8,128)S(1)} collective-permute-done((f32[64,384]{1,0:T(8,128)S(1)}, f32[64,384]{1,0:T(8,128)S(1)}, u32[]{:S(2)}, u32[]{:S(2)}) %collective-permute-start.14) | collective-permute-done | bytes 98336 | tf_op jit(solution)/shard_map/ppermute | solution.py:29
  47.5 2.1 %collective-permute-start.19 = (f32[64,384]{1,0:T(8,128)S(1)}, f32[64,384]{1,0:T(8,128)S(1)}, u32[]{:S(2)}, u32[]{:S(2)}) collective-permute-start(f32[64,384]{1,0:T(8,128)S(1)} %add_add_fusion.1), channel_id=1, source_target_pairs={{0,12},{1,13},{2,14},{3,15},{4,8},{5,9},{6,10},{7,11},{8,4},{9,5},... | collective-permute-start | bytes 294920 | tf_op jit(solution)/shard_map/ppermute | solution.py:29
  49.6 0.0 collective-permute-start.17
  49.6 2.4 %collective-permute-start.18 = (f32[64,384]{1,0:T(8,128)S(1)}, f32[64,384]{1,0:T(8,128)S(1)}, u32[]{:S(2)}, u32[]{:S(2)}) collective-permute-start(f32[64,384]{1,0:T(8,128)S(1)} %add_add_fusion.1), channel_id=1, source_target_pairs={{0,8},{1,9},{2,10},{3,11},{4,12},{5,13},{6,14},{7,15},{8,0},{9,1},... | collective-permute-start | bytes 294920 | tf_op jit(solution)/shard_map/ppermute | solution.py:29
  52.0 3.1 %collective-permute-done.19 = f32[64,384]{1,0:T(8,128)S(1)} collective-permute-done((f32[64,384]{1,0:T(8,128)S(1)}, f32[64,384]{1,0:T(8,128)S(1)}, u32[]{:S(2)}, u32[]{:S(2)}) %collective-permute-start.19) | collective-permute-done | bytes 98336 | tf_op jit(solution)/shard_map/ppermute | solution.py:29
  55.0 2.5 %collective-permute-done.17 = f32[64,384]{1,0:T(8,128)S(1)} collective-permute-done((f32[64,384]{1,0:T(8,128)S(1)}, f32[64,384]{1,0:T(8,128)S(1)}, u32[]{:S(2)}, u32[]{:S(2)}) %collective-permute-start.17) | collective-permute-done | bytes 98336 | tf_op jit(solution)/shard_map/ppermute | solution.py:29
  57.6 1.5 %collective-permute-start.22 = (f32[64,384]{1,0:T(8,128)S(1)}, f32[64,384]{1,0:T(8,128)S(1)}, u32[]{:S(2)}, u32[]{:S(2)}) collective-permute-start(f32[64,384]{1,0:T(8,128)S(1)} %add_add_fusion.refs_0_), channel_id=1, source_target_pairs={{0,18},{1,19},{2,16},{3,17},{4,22},{5,23},{6,20},{7,21},{8,26},{9,... | collective-permute-start | bytes 294920 | tf_op jit(solution)/shard_map/ppermute | solution.py:29
  59.1 1.4 %collective-permute-start.21 = (f32[64,384]{1,0:T(8,128)S(1)}, f32[64,384]{1,0:T(8,128)S(1)}, u32[]{:S(2)}, u32[]{:S(2)}) collective-permute-start(f32[64,384]{1,0:T(8,128)S(1)} %add_add_fusion.refs_0_), channel_id=1, source_target_pairs={{0,16},{1,17},{2,18},{3,19},{4,20},{5,21},{6,22},{7,23},{8,24},{9,... | collective-permute-start | bytes 294920 | tf_op jit(solution)/shard_map/ppermute | solution.py:29
  60.5 0.7 collective-permute-start.20
  61.2 1.9 %collective-permute-start.8 = (f32[128,256]{1,0:T(8,128)S(1)}, f32[128,256]{1,0:T(8,128)S(1)}, u32[]{:S(2)}, u32[]{:S(2)}) collective-permute-start(f32[128,256]{1,0:T(8,128)S(1)} %get-tuple-element.20), channel_id=1, source_target_pairs={{0,12},{1,13},{2,14},{3,15},{4,8},{5,9},{6,10},{7,11},{8,4},{9,5},... | collective-permute-start | bytes 393224 | tf_op jit(solution)/shard_map/ppermute | solution.py:29
  63.2 0.8 %collective-permute-done.22.refs_3_ = f32[64,384]{1,0:T(8,128)S(1)} collective-permute-done((f32[64,384]{1,0:T(8,128)S(1)}, f32[64,384]{1,0:T(8,128)S(1)}, u32[]{:S(2)}, u32[]{:S(2)}) %collective-permute-start.22) | collective-permute-done | bytes 98336 | tf_op jit(solution)/shard_map/ppermute | solution.py:29
  64.0 1.7 %collective-permute-start.7 = (f32[128,256]{1,0:T(8,128)S(1)}, f32[128,256]{1,0:T(8,128)S(1)}, u32[]{:S(2)}, u32[]{:S(2)}) collective-permute-start(f32[128,256]{1,0:T(8,128)S(1)} %get-tuple-element.19), channel_id=1, source_target_pairs={{0,8},{1,9},{2,10},{3,11},{4,12},{5,13},{6,14},{7,15},{8,0},{9,1},... | collective-permute-start | bytes 393224 | tf_op jit(solution)/shard_map/ppermute | solution.py:29
  65.7 0.0 collective-permute-done.20.refs_1_
  65.7 0.1 collective-permute-start.23
  65.8 3.6 %collective-permute-done.8 = f32[128,256]{1,0:T(8,128)S(1)} collective-permute-done((f32[128,256]{1,0:T(8,128)S(1)}, f32[128,256]{1,0:T(8,128)S(1)}, u32[]{:S(2)}, u32[]{:S(2)}) %collective-permute-start.8) | collective-permute-done | bytes 131104 | tf_op jit(solution)/shard_map/ppermute | solution.py:29
  69.4 1.8 %collective-permute-done.6 = f32[128,256]{1,0:T(8,128)S(1)} collective-permute-done((f32[128,256]{1,0:T(8,128)S(1)}, f32[128,256]{1,0:T(8,128)S(1)}, u32[]{:S(2)}, u32[]{:S(2)}) %collective-permute-start.6) | collective-permute-done | bytes 131104 | tf_op jit(solution)/shard_map/ppermute | solution.py:29
  71.2 3.3 %collective-permute-done.7 = f32[128,256]{1,0:T(8,128)S(1)} collective-permute-done((f32[128,256]{1,0:T(8,128)S(1)}, f32[128,256]{1,0:T(8,128)S(1)}, u32[]{:S(2)}, u32[]{:S(2)}) %collective-permute-start.7) | collective-permute-done | bytes 131104 | tf_op jit(solution)/shard_map/ppermute | solution.py:29
  74.5 0.7 fusion
  75.2 1.5 %shard_map.71 = f32[512,256]{1,0:T(8,128)} custom-call(s32[5]{0:T(128)S(1)} %stack.23.place_ref, f32[512,256]{1,0:T(8,128)S(1)} %copy-done, f32[256,128]{1,0:T(8,128)S(1)} %collective-permute-done.23.other_ref, f32[64,384]{1,0:T(8,128)S(1)} %add_add_fusion.refs_0_, f32[64,384]{1,0:T(8,128)S(1)} %collective-permute-done.20.refs_1_, ...), custom_call_target="tpu_custom_call" | custom-call | bytes 1572884 | tf_op jit(solution)/shard_map/pallas_call | solution.py:171
  (20 shorter events, 0.1 us)
Async XLA Ops:
  0.7 0.7 copy-start.2
  4.9 11.4 %collective-permute-start = (f32[2,128,256]{2,1,0:T(8,128)S(1)}, f32[2,128,256]{2,1,0:T(8,128)S(1)}, u32[]{:S(2)}, u32[]{:S(2)}) collective-permute-start(f32[2,128,256]{2,1,0:T(8,128)S(1)} %get-tuple-element.15), channel_id=1, source_target_pairs={{0,2},{1,3},{2,0},{3,1},{4,6},{5,7},{6,4},{7,5},{8,10},{9,11},{10,... | collective-permute-start | bytes 786440 | tf_op jit(solution)/shard_map/ppermute | solution.py:29
  8.0 8.4 %collective-permute-start.2 = (f32[128,256]{1,0:T(8,128)S(1)}, f32[128,256]{1,0:T(8,128)S(1)}, u32[]{:S(2)}, u32[]{:S(2)}) collective-permute-start(f32[128,256]{1,0:T(8,128)S(1)} %get-tuple-element.16.refs_0_), channel_id=1, source_target_pairs={{0,0},{1,1},{2,16},{3,17},{4,2},{5,3},{6,18},{7,19},{8,4},{9,5},{1... | collective-permute-start | bytes 393224 | tf_op jit(solution)/shard_map/ppermute | solution.py:29
  16.3 12.5 %collective-permute-start.1 = (f32[2,128,256]{2,1,0:T(8,128)S(1)}, f32[2,128,256]{2,1,0:T(8,128)S(1)}, u32[]{:S(2)}, u32[]{:S(2)}) collective-permute-start(f32[2,128,256]{2,1,0:T(8,128)S(1)} %collective-permute-done.mine_ref), channel_id=1, source_target_pairs={{0,1},{1,0},{2,3},{3,2},{4,5},{5,4},{6,7},{7,6},{8,9},{9,8},{10,11... | collective-permute-start | bytes 786440 | tf_op jit(solution)/shard_map/ppermute | solution.py:29
  16.3 8.5 %collective-permute-start.3 = (f32[128,256]{1,0:T(8,128)S(1)}, f32[128,256]{1,0:T(8,128)S(1)}, u32[]{:S(2)}, u32[]{:S(2)}) collective-permute-start(f32[128,256]{1,0:T(8,128)S(1)} %collective-permute-done.2.refs_0_), channel_id=1, source_target_pairs={{0,16},{1,17},{2,18},{3,19},{4,20},{5,21},{6,22},{7,23},{8,24},{9,... | collective-permute-start | bytes 393224 | tf_op jit(solution)/shard_map/ppermute | solution.py:29
  18.5 7.4 %collective-permute-start.4 = (f32[128,256]{1,0:T(8,128)S(1)}, f32[128,256]{1,0:T(8,128)S(1)}, u32[]{:S(2)}, u32[]{:S(2)}) collective-permute-start(f32[128,256]{1,0:T(8,128)S(1)} %collective-permute-done.2.refs_0_), channel_id=1, source_target_pairs={{0,2},{1,3},{2,0},{3,1},{4,6},{5,7},{6,4},{7,5},{8,10},{9,11},{10,... | collective-permute-start | bytes 393224 | tf_op jit(solution)/shard_map/ppermute | solution.py:29
  18.9 9.9 %collective-permute-start.5 = (f32[128,256]{1,0:T(8,128)S(1)}, f32[128,256]{1,0:T(8,128)S(1)}, u32[]{:S(2)}, u32[]{:S(2)}) collective-permute-start(f32[128,256]{1,0:T(8,128)S(1)} %collective-permute-done.2.refs_0_), channel_id=1, source_target_pairs={{0,18},{1,19},{2,16},{3,17},{4,22},{5,23},{6,20},{7,21},{8,26},{9,... | collective-permute-start | bytes 393224 | tf_op jit(solution)/shard_map/ppermute | solution.py:29
  20.3 10.8 %collective-permute-start.12 = (f32[128,256]{1,0:T(8,128)S(1)}, f32[128,256]{1,0:T(8,128)S(1)}, u32[]{:S(2)}, u32[]{:S(2)}) collective-permute-start(f32[128,256]{1,0:T(8,128)S(1)} %get-tuple-element.16.refs_0_), channel_id=1, source_target_pairs={{0,12},{1,13},{2,14},{3,15},{4,8},{5,9},{6,10},{7,11},{8,4},{9,5},... | collective-permute-start | bytes 393224 | tf_op jit(solution)/shard_map/ppermute | solution.py:29
  24.8 11.1 %collective-permute-start.11 = (f32[128,256]{1,0:T(8,128)S(1)}, f32[128,256]{1,0:T(8,128)S(1)}, u32[]{:S(2)}, u32[]{:S(2)}) collective-permute-start(f32[128,256]{1,0:T(8,128)S(1)} %get-tuple-element.16.refs_0_), channel_id=1, source_target_pairs={{0,8},{1,9},{2,10},{3,11},{4,12},{5,13},{6,14},{7,15},{8,0},{9,1},... | collective-permute-start | bytes 393224 | tf_op jit(solution)/shard_map/ppermute | solution.py:29
  26.0 10.0 %collective-permute-start.10 = (f32[128,256]{1,0:T(8,128)S(1)}, f32[128,256]{1,0:T(8,128)S(1)}, u32[]{:S(2)}, u32[]{:S(2)}) collective-permute-start(f32[128,256]{1,0:T(8,128)S(1)} %get-tuple-element.16.refs_0_), channel_id=1, source_target_pairs={{0,4},{1,5},{2,6},{3,7},{4,0},{5,1},{6,2},{7,3},{8,12},{9,13},{10,... | collective-permute-start | bytes 393224 | tf_op jit(solution)/shard_map/ppermute | solution.py:29
  28.8 1.0 %copy-start.1 = (f32[4,128,256]{2,1,0:T(8,128)S(1)}, f32[4,128,256]{2,1,0:T(8,128)}, u32[]{:S(2)}) copy-start(f32[4,128,256]{2,1,0:T(8,128)} %get-tuple-element.14.kept_ref) | copy-start | bytes 1572868
  31.0 6.7 %collective-permute-start.9 = (f32[4,128,256]{2,1,0:T(8,128)S(1)}, f32[4,128,256]{2,1,0:T(8,128)S(1)}, u32[]{:S(2)}, u32[]{:S(2)}) collective-permute-start(f32[4,128,256]{2,1,0:T(8,128)S(1)} %get-tuple-element.17.share_ref), channel_id=1, source_target_pairs={{0,1},{1,0},{2,3},{3,2},{4,5},{5,4},{6,7},{7,6},{8,9},{9,8},{10,11... | collective-permute-start | bytes 1572872 | tf_op jit(solution)/shard_map/ppermute | solution.py:29
  36.0 1.8 %collective-permute-start.13 = (f32[384,256]{1,0:T(8,128)S(1)}, f32[384,256]{1,0:T(8,128)S(1)}, u32[]{:S(2)}, u32[]{:S(2)}) collective-permute-start(f32[384,256]{1,0:T(8,128)S(1)} %pad_maximum_fusion), channel_id=1, source_target_pairs={{0,1},{1,0},{2,3},{3,2},{4,5},{5,4},{6,7},{7,6},{8,9},{9,8},{10,11... | collective-permute-start | bytes 1179656 | tf_op jit(solution)/shard_map/ppermute | solution.py:29
  39.3 6.6 %collective-permute-start.16 = (f32[64,384]{1,0:T(8,128)S(1)}, f32[64,384]{1,0:T(8,128)S(1)}, u32[]{:S(2)}, u32[]{:S(2)}) collective-permute-start(f32[64,384]{1,0:T(8,128)S(1)} %get-tuple-element.25), channel_id=1, source_target_pairs={{0,18},{1,19},{2,16},{3,17},{4,22},{5,23},{6,20},{7,21},{8,26},{9,... | collective-permute-start | bytes 294920 | tf_op jit(solution)/shard_map/ppermute | solution.py:29
  40.8 6.7 %collective-permute-start.14 = (f32[64,384]{1,0:T(8,128)S(1)}, f32[64,384]{1,0:T(8,128)S(1)}, u32[]{:S(2)}, u32[]{:S(2)}) collective-permute-start(f32[64,384]{1,0:T(8,128)S(1)} %get-tuple-element.23), channel_id=1, source_target_pairs={{0,2},{1,3},{2,0},{3,1},{4,6},{5,7},{6,4},{7,5},{8,10},{9,11},{10,... | collective-permute-start | bytes 294920 | tf_op jit(solution)/shard_map/ppermute | solution.py:29
  42.5 4.9 %collective-permute-start.15 = (f32[64,384]{1,0:T(8,128)S(1)}, f32[64,384]{1,0:T(8,128)S(1)}, u32[]{:S(2)}, u32[]{:S(2)}) collective-permute-start(f32[64,384]{1,0:T(8,128)S(1)} %get-tuple-element.24), channel_id=1, source_target_pairs={{0,16},{1,17},{2,18},{3,19},{4,20},{5,21},{6,22},{7,23},{8,24},{9,... | collective-permute-start | bytes 294920 | tf_op jit(solution)/shard_map/ppermute | solution.py:29
  47.5 7.5 %collective-permute-start.19 = (f32[64,384]{1,0:T(8,128)S(1)}, f32[64,384]{1,0:T(8,128)S(1)}, u32[]{:S(2)}, u32[]{:S(2)}) collective-permute-start(f32[64,384]{1,0:T(8,128)S(1)} %add_add_fusion.1), channel_id=1, source_target_pairs={{0,12},{1,13},{2,14},{3,15},{4,8},{5,9},{6,10},{7,11},{8,4},{9,5},... | collective-permute-start | bytes 294920 | tf_op jit(solution)/shard_map/ppermute | solution.py:29
  49.6 8.0 %collective-permute-start.17 = (f32[64,384]{1,0:T(8,128)S(1)}, f32[64,384]{1,0:T(8,128)S(1)}, u32[]{:S(2)}, u32[]{:S(2)}) collective-permute-start(f32[64,384]{1,0:T(8,128)S(1)} %add_add_fusion.1), channel_id=1, source_target_pairs={{0,4},{1,5},{2,6},{3,7},{4,0},{5,1},{6,2},{7,3},{8,12},{9,13},{10,... | collective-permute-start | bytes 294920 | tf_op jit(solution)/shard_map/ppermute | solution.py:29
  49.6 8.0 %collective-permute-start.18 = (f32[64,384]{1,0:T(8,128)S(1)}, f32[64,384]{1,0:T(8,128)S(1)}, u32[]{:S(2)}, u32[]{:S(2)}) collective-permute-start(f32[64,384]{1,0:T(8,128)S(1)} %add_add_fusion.1), channel_id=1, source_target_pairs={{0,8},{1,9},{2,10},{3,11},{4,12},{5,13},{6,14},{7,15},{8,0},{9,1},... | collective-permute-start | bytes 294920 | tf_op jit(solution)/shard_map/ppermute | solution.py:29
  57.6 6.4 %collective-permute-start.22 = (f32[64,384]{1,0:T(8,128)S(1)}, f32[64,384]{1,0:T(8,128)S(1)}, u32[]{:S(2)}, u32[]{:S(2)}) collective-permute-start(f32[64,384]{1,0:T(8,128)S(1)} %add_add_fusion.refs_0_), channel_id=1, source_target_pairs={{0,18},{1,19},{2,16},{3,17},{4,22},{5,23},{6,20},{7,21},{8,26},{9,... | collective-permute-start | bytes 294920 | tf_op jit(solution)/shard_map/ppermute | solution.py:29
  59.1 6.5 %collective-permute-start.21 = (f32[64,384]{1,0:T(8,128)S(1)}, f32[64,384]{1,0:T(8,128)S(1)}, u32[]{:S(2)}, u32[]{:S(2)}) collective-permute-start(f32[64,384]{1,0:T(8,128)S(1)} %add_add_fusion.refs_0_), channel_id=1, source_target_pairs={{0,16},{1,17},{2,18},{3,19},{4,20},{5,21},{6,22},{7,23},{8,24},{9,... | collective-permute-start | bytes 294920 | tf_op jit(solution)/shard_map/ppermute | solution.py:29
  60.5 5.2 %collective-permute-start.20 = (f32[64,384]{1,0:T(8,128)S(1)}, f32[64,384]{1,0:T(8,128)S(1)}, u32[]{:S(2)}, u32[]{:S(2)}) collective-permute-start(f32[64,384]{1,0:T(8,128)S(1)} %add_add_fusion.refs_0_), channel_id=1, source_target_pairs={{0,2},{1,3},{2,0},{3,1},{4,6},{5,7},{6,4},{7,5},{8,10},{9,11},{10,... | collective-permute-start | bytes 294920 | tf_op jit(solution)/shard_map/ppermute | solution.py:29
  61.2 8.2 %collective-permute-start.8 = (f32[128,256]{1,0:T(8,128)S(1)}, f32[128,256]{1,0:T(8,128)S(1)}, u32[]{:S(2)}, u32[]{:S(2)}) collective-permute-start(f32[128,256]{1,0:T(8,128)S(1)} %get-tuple-element.20), channel_id=1, source_target_pairs={{0,12},{1,13},{2,14},{3,15},{4,8},{5,9},{6,10},{7,11},{8,4},{9,5},... | collective-permute-start | bytes 393224 | tf_op jit(solution)/shard_map/ppermute | solution.py:29
  63.2 8.0 %collective-permute-start.6 = (f32[128,256]{1,0:T(8,128)S(1)}, f32[128,256]{1,0:T(8,128)S(1)}, u32[]{:S(2)}, u32[]{:S(2)}) collective-permute-start(f32[128,256]{1,0:T(8,128)S(1)} %get-tuple-element.18), channel_id=1, source_target_pairs={{0,4},{1,5},{2,6},{3,7},{4,0},{5,1},{6,2},{7,3},{8,12},{9,13},{10,... | collective-permute-start | bytes 393224 | tf_op jit(solution)/shard_map/ppermute | solution.py:29
  64.0 10.6 %collective-permute-start.7 = (f32[128,256]{1,0:T(8,128)S(1)}, f32[128,256]{1,0:T(8,128)S(1)}, u32[]{:S(2)}, u32[]{:S(2)}) collective-permute-start(f32[128,256]{1,0:T(8,128)S(1)} %get-tuple-element.19), channel_id=1, source_target_pairs={{0,8},{1,9},{2,10},{3,11},{4,12},{5,13},{6,14},{7,15},{8,0},{9,1},... | collective-permute-start | bytes 393224 | tf_op jit(solution)/shard_map/ppermute | solution.py:29
  65.6 9.6 %copy-start = (f32[512,256]{1,0:T(8,128)S(1)}, f32[512,256]{1,0:T(8,128)}, u32[]{:S(2)}) copy-start(f32[512,256]{1,0:T(8,128)} %pivot_ref.1) | copy-start | bytes 1572868
  65.7 9.5 %collective-permute-start.23 = (f32[256,128]{1,0:T(8,128)S(1)}, f32[256,128]{1,0:T(8,128)S(1)}, u32[]{:S(2)}, u32[]{:S(2)}) collective-permute-start(f32[256,128]{1,0:T(8,128)S(1)} %pad_maximum_fusion.1), channel_id=1, source_target_pairs={{0,1},{1,0},{2,3},{3,2},{4,5},{5,4},{6,7},{7,6},{8,9},{9,8},{10,11... | collective-permute-start | bytes 393224 | tf_op jit(solution)/shard_map/ppermute | solution.py:29

commit v3 on v2

--- a/solution.py
+++ b/solution.py
@@ -10,7 +10,8 @@
 
 AXES = ("row", "col", "rep")
 PAIR = 2
-ROOM = 56000000
+ROOM_OWN = 56380000
+ROOM_MASK = 56000000
 F32, BF16 = jnp.float32, jnp.bfloat16
 
 
@@ -52,33 +53,43 @@
     return pl.ds(pl.multiple_of(index * size, size), size)
 
 
-def front_kernel(planes, rows, place_ref, marks_ref, factor_ref, normalizer_ref, full_ref, *refs):
-    normed_ref, other_ref, kept_ref, given_ref, *scratch = refs
-    factor_in, normalizer_in, full_in, sems = scratch
+def load_all(loads):
+    copies = [pltpu.make_async_copy(*load) for load in loads]
+    for copy in copies:
+        copy.start()
+    return copies
+
+
+def own_kernel(place_ref, factor_ref, normalizer_ref, normed_ref, factor_in, normalizer_in, sems):
+    columns = tile_at(place_ref[3], normed_ref.shape[1])
+    for copy in load_all(
+        [
+            (factor_ref, factor_in, sems.at[0]),
+            (normalizer_ref.at[:, columns], normalizer_in, sems.at[1]),
+        ]
+    ):
+        copy.wait()
+    normed_ref[...] = split_dot(split(factor_in[...]), split(normalizer_in[...]))
+
+
+def mask_kernel(planes, rows, place_ref, marks_ref, factor_ref, normalizer_ref, full_ref, *refs):
+    other_ref, kept_ref, given_ref, factor_in, normalizer_in, full_in, sems = refs
     row, plane, side, rep = (place_ref[i] for i in range(4))
-    tile, half = normed_ref.shape
+    tile, half = other_ref.shape
     cut = planes // 2
     band = PAIR * tile
-    loads = [
-        pltpu.make_async_copy(factor_ref, factor_in, sems.at[0]),
-    ] + [
-        pltpu.make_async_copy(
-            normalizer_ref.at[:, tile_at(columns, half)], normalizer_in.at[i], sems.at[1 + i]
-        )
-        for i, columns in enumerate((rep, 1 - rep))
-    ] + [
-        pltpu.make_async_copy(full_ref.at[tile_at(plane ^ k, band), :], full_in.at[k], sems.at[3 + k])
-        for k in range(planes)
-    ]
-    for load in loads:
-        load.start()
-    for load in loads[:2]:
-        load.wait()
-    left = split(factor_in[...])
-    normed_ref[...] = split_dot(left, split(normalizer_in[0]))
-    for load in loads[2:]:
-        load.wait()
-    other_ref[...] = split_dot(left, split(normalizer_in[1]))
+    copies = load_all(
+        [
+            (full_ref.at[tile_at(plane ^ k, band), :], full_in.at[k], sems.at[k])
+            for k in range(planes)
+        ]
+        + [
+            (factor_ref, factor_in, sems.at[planes]),
+            (normalizer_ref.at[:, tile_at(1 - rep, half)], normalizer_in, sems.at[planes + 1]),
+        ]
+    )
+    for copy in copies[:planes]:
+        copy.wait()
 
     def masked(k, wanted, m):
         across = row ^ m
@@ -95,6 +106,10 @@
         @pl.loop(0, planes)
         def _(k):
             kept_ref[k, :, columns] = masked(k, side, m)
+
+    for copy in copies[planes:]:
+        copy.wait()
+    other_ref[...] = split_dot(split(factor_in[...]), split(normalizer_in[...]))
 
 
 def product_kernel(planes, members, place_ref, kept_ref, mine_ref, theirs_ref, *refs):
@@ -115,13 +130,17 @@
     strip, outs, total_ref = refs[: planes + 1], refs[planes + 1 : -1], refs[-1]
     place, first = place_ref[4], place_ref[3] == 0
     tile, half = strip[0].shape
-    quarter, step = half // 2, half // members
+    quarter = half // 2
+    step = quarter // members
     own_normed = jnp.concatenate([ref[...] for ref in strip[:planes]], 0)
     other_normed = jnp.concatenate([strip[planes][...], gathered_ref[...]], 0)
     own = share_ref[...].reshape(planes * tile, half)
     other = other_ref[...].reshape(planes * tile, half)
     mixed = split_dot(split(own_normed), split(own), (0, 0))
-    total_ref[:, :half] = mixed + mixed.T
+    lower = mixed[quarter:, :quarter]
+    total_ref[:, :quarter] = mixed[:quarter, :quarter] + mixed[:quarter, :quarter].T
+    total_ref[:, quarter:half] = mixed[:quarter, quarter:] + lower.T
+    total_ref[:, half : half + quarter] = mixed[quarter:, quarter:] + mixed[quarter:, quarter:].T
 
     def left(mine, theirs):
         return split(jnp.where(first, mine, theirs))
@@ -129,9 +148,11 @@
     def right(mine, theirs):
         return split(jnp.where(first, theirs[:, :quarter], mine[:, quarter:]))
 
-    total_ref[:, half:] = split_dot(
+    between = split_dot(
         left(own_normed, other_normed), right(own, other), (0, 0)
     ) + split_dot(left(own, other), right(own_normed, other_normed), (0, 0))
+    total_ref[:, half + quarter : PAIR * half] = between[:quarter]
+    total_ref[:, PAIR * half :] = between[quarter:]
     for k in range(members):
         outs[k][...] = total_ref[tile_at(place ^ k, step), :]
 
@@ -140,23 +161,38 @@
     parts, out_ref, total_ref, between_ref = refs[:members], *refs[members:]
     place, rep = place_ref[4], place_ref[3]
     half = out_ref.shape[1]
-    step = half // members
+    quarter = half // 2
+    step = quarter // members
     for k in range(members):
         rows = tile_at(place ^ k, step)
         total_ref[rows, :] = parts[k][...]
         between_ref[rows, :] = other_ref[k * step : (k + 1) * step, :]
+    blocks = [total_ref[:, i * quarter : (i + 1) * quarter] for i in range(5)]
+    others = [between_ref[:, i * quarter : (i + 1) * quarter] for i in range(2)]
+
+    def put(i, j, block):
+        at = (pl.ds(i * quarter, quarter), pl.ds(j * quarter, quarter))
+        out_ref[at] = pivot_ref[at] + 0.5 * block
+
+    def diagonal(i):
+        put(i, 0, blocks[0])
+        put(i, 1, blocks[1])
+        put(i + 1, 0, blocks[1].T)
+        put(i + 1, 1, blocks[2])
 
     @pl.when(rep == 0)
     def _():
-        across = jnp.concatenate([total_ref[:, half:], between_ref[...]], 1)
-        out_ref[:half, :] = pivot_ref[:half, :] + 0.5 * total_ref[:, :half]
-        out_ref[half:, :] = pivot_ref[half:, :] + 0.5 * across.T
+        diagonal(0)
+        for i in range(2):
+            put(2, i, blocks[3 + i].T)
+            put(3, i, others[i].T)
 
     @pl.when(rep != 0)
     def _():
-        across = jnp.concatenate([between_ref[...], total_ref[:, half:]], 1)
-        out_ref[:half, :] = pivot_ref[:half, :] + 0.5 * across
-        out_ref[half:, :] = pivot_ref[half:, :] + 0.5 * total_ref[:, :half]
+        diagonal(2)
+        for i in range(2):
+            put(i, 0, others[i])
+            put(i, 1, blocks[3 + i])
 
 
 def call(kernel, shapes, spaces, args, scratch=(), flops=0, room=None):
@@ -189,20 +225,28 @@
     place = jnp.stack([row, plane, side, rep, row * PAIR + side]).astype(jnp.int32)
     depth = rows * tile
 
-    cut = planes // 2
+    cut, inner = planes // 2, factor.shape[1]
     inner = factor.shape[1]
-    own_normed, other_normed, kept, given = call(
-        functools.partial(front_kernel, planes, rows),
-        [(tile, half), (tile, half), (planes, tile, depth), (cut, tile, depth)],
+    (own_normed,) = call(
+        own_kernel,
+        [(tile, half)],
+        "shh",
+        [place, factor, factor_normalizer],
+        [(tile, inner), (inner, half), pltpu.SemaphoreType.DMA((2,))],
+        room=ROOM_OWN,
+    )
+    other_normed, kept, given = call(
+        functools.partial(mask_kernel, planes, rows),
+        [(tile, half), (planes, tile, depth), (cut, tile, depth)],
         "sshhh",
         [place, tile_structure.T, factor, factor_normalizer, ancestor_inverse],
         [
             (tile, inner),
-            (PAIR, inner, half),
+            (inner, half),
             (planes, PAIR * tile, depth),
-            pltpu.SemaphoreType.DMA((3 + planes,)),
+            pltpu.SemaphoreType.DMA((2 + planes,)),
         ],
-        room=ROOM,
+        room=ROOM_MASK,
     )
 
     def to_plane(r, c, p):
@@ -238,14 +282,14 @@
     landed = [send(shares[k - 1], along(k)) for k in range(1, planes)]
     ancestor_columns = -(product[0] + sum(landed))
 
-    quarter, step = half // 2, half // members
-    width = half + quarter
+    quarter = half // 2
+    step, width = quarter // members, 5 * quarter
     parts = call(
         functools.partial(coupling_kernel, members, planes),
         [(step, width)] * members,
         "s",
         [place, product, other_product, other_strip, *strip, other_normed],
-        [(half, width)],
+        [(quarter, width)],
         flops=12 * planes * tile * half * half,
     )
 
@@ -259,13 +303,13 @@
     part = parts[0] + sum(send(parts[k], in_plane(k)) for k in range(1, members))
     part = part + sum(send(part, along(k)) for k in range(1, planes))
     parts = [part] + [send(part, in_plane(k)) for k in range(1, members)]
-    other_between = swap_core(jnp.concatenate([one[:, half:] for one in parts], 0))
+    other_between = swap_core(jnp.concatenate([one[:, half + quarter :] for one in parts], 0))
     (diag_block,) = call(
         functools.partial(finish_kernel, members),
         [pivot_inverse.shape],
         "s",
         [place, pivot_inverse, other_between, *parts],
-        [(half, width), (half, quarter)],
+        [(quarter, width), (quarter, half)],
     )
     return ancestor_columns, diag_block
 

time: 77 us -> 75.1 us (0.975)
  waiting for transfers between devices: 34.1 us -> 28 us
  starting transfers between devices: 31.7 us -> 35.6 us
  Pallas kernels: 7.66 us -> 8.99 us
  local copies, waits for them, and re-layouts: 1.82 us -> 0.79 us
    ppermute x24, waiting for transfers between devices: 34.1 us -> 28 us  [send(): return lax.ppermute(block, AXES, route)]
    ppermute x24, starting transfers between devices: 31.7 us -> 35.6 us  [send(): return lax.ppermute(block, AXES, route)]
    pallas_call x4 -> x5, Pallas kernels: 7.66 us -> 8.99 us  [call(): pl.pallas_call(kernel, out_shape=[jax.ShapeDtypeStruct(shape, F32) for sh...]
    unnamed x6, local copies, waits for them, and re-layouts: 1.72 us -> 0.69 us
  transfers between devices with their start and end apart: 24 -> 24, of which waited for: 11 -> 11; matrix products, arithmetic and copies ran while one was open for 1% -> 1% of each run, Pallas kernels for 1% -> 4%
where the time goes in v3:
time: 75.1 us; the launch traced here: 75 us
  starting transfers between devices  35.6 us (47%)
  waiting for transfers between devices  28 us (37%)
  Pallas kernels  8.99 us (12%)
  between operations  0.81 us (1%)
  local copies, waits for them, and re-layouts  0.79 us (1%)
  other arithmetic  0.77 us (1%)
    ppermute x24, starting transfers between devices, send(): return lax.ppermute(block, AXES, route)  35.6 us
    ppermute x24, waiting for transfers between devices, send(): return lax.ppermute(block, AXES, route)  28 us
    pallas_call x5, Pallas kernels, call(): pl.pallas_call(kernel, out_shape=[jax.ShapeDtypeStruct(shape, F32) for sh...  8.99 us
  transfers between devices with their start and end apart: 24, of which 11 were waited for; matrix products, arithmetic and copies ran while one was open for 1% of the time, Pallas kernels for 4%

profile of v3, /device:TPU:0, one launch (start us, length us, event | category | flops | bytes accessed | tf_op | source)
XLA Modules:
  0.0 75.0 jit_solution(18128002394744297717)
XLA Ops:
  0.7 0.1 stack.23.place_ref
  0.7 0.7 copy-done.2
  1.4 2.8 %shard_map.68 = (f32[128,256]{1,0:T(8,128)S(1)}, f32[4,128,256]{2,1,0:T(8,128)}, f32[2,128,256]{2,1,0:T(8,128)S(1)}) custom-call(s32[5]{0:T(128)S(1)} %stack.23.place_ref, s32[2,8]{1,0:T(2,128)S(1)} %bitcast.10, f32[128,512]{1,0:T(8,128)} %factor_ref.3, f32[512,512]{1,0:T(8,128)} %normalizer_ref.3, f32[1024,256]{1,0:T(8,128)} %full_ref.1), custom_call_target="tpu_custom_call" | custom-call | bytes 3276884 | tf_op jit(solution)/shard_map/pallas_call | solution.py:207
  4.3 0.0 copy-start.1
  4.3 3.0 %collective-permute-start = (f32[2,128,256]{2,1,0:T(8,128)S(1)}, f32[2,128,256]{2,1,0:T(8,128)S(1)}, u32[]{:S(2)}, u32[]{:S(2)}) collective-permute-start(f32[2,128,256]{2,1,0:T(8,128)S(1)} %get-tuple-element.14), channel_id=1, source_target_pairs={{0,2},{1,3},{2,0},{3,1},{4,6},{5,7},{6,4},{7,5},{8,10},{9,11},{10,... | collective-permute-start | bytes 786440 | tf_op jit(solution)/shard_map/ppermute | solution.py:30
  7.3 2.0 %shard_map.69.refs_0_ = f32[128,256]{1,0:T(8,128)S(1)} custom-call(s32[5]{0:T(128)S(1)} %stack.23.place_ref, f32[128,512]{1,0:T(8,128)} %factor_ref.3, f32[512,512]{1,0:T(8,128)} %normalizer_ref.3), custom_call_target="tpu_custom_call" | custom-call | bytes 1441812 | tf_op jit(solution)/shard_map/pallas_call | solution.py:207
  9.3 0.7 collective-permute-start.2
  10.0 5.7 %collective-permute-done.mine_ref = f32[2,128,256]{2,1,0:T(8,128)S(1)} collective-permute-done((f32[2,128,256]{2,1,0:T(8,128)S(1)}, f32[2,128,256]{2,1,0:T(8,128)S(1)}, u32[]{:S(2)}, u32[]{:S(2)}) %collective-permute-start) | collective-permute-done | bytes 262176 | tf_op jit(solution)/shard_map/ppermute | solution.py:30
  15.7 0.0 collective-permute-start.1
  15.7 0.0 collective-permute-done.2.refs_0_
  15.7 2.9 %collective-permute-start.3 = (f32[128,256]{1,0:T(8,128)S(1)}, f32[128,256]{1,0:T(8,128)S(1)}, u32[]{:S(2)}, u32[]{:S(2)}) collective-permute-start(f32[128,256]{1,0:T(8,128)S(1)} %collective-permute-done.2.refs_0_), channel_id=1, source_target_pairs={{0,16},{1,17},{2,18},{3,19},{4,20},{5,21},{6,22},{7,23},{8,24},{9,... | collective-permute-start | bytes 393224 | tf_op jit(solution)/shard_map/ppermute | solution.py:30
  18.6 0.7 collective-permute-start.4
  19.3 0.8 %collective-permute-start.5 = (f32[128,256]{1,0:T(8,128)S(1)}, f32[128,256]{1,0:T(8,128)S(1)}, u32[]{:S(2)}, u32[]{:S(2)}) collective-permute-start(f32[128,256]{1,0:T(8,128)S(1)} %collective-permute-done.2.refs_0_), channel_id=1, source_target_pairs={{0,18},{1,19},{2,16},{3,17},{4,22},{5,23},{6,20},{7,21},{8,26},{9,... | collective-permute-start | bytes 393224 | tf_op jit(solution)/shard_map/ppermute | solution.py:30
  20.0 4.2 %collective-permute-start.12 = (f32[128,256]{1,0:T(8,128)S(1)}, f32[128,256]{1,0:T(8,128)S(1)}, u32[]{:S(2)}, u32[]{:S(2)}) collective-permute-start(f32[128,256]{1,0:T(8,128)S(1)} %shard_map.69.refs_0_), channel_id=1, source_target_pairs={{0,12},{1,13},{2,14},{3,15},{4,8},{5,9},{6,10},{7,11},{8,4},{9,5},... | collective-permute-start | bytes 393224 | tf_op jit(solution)/shard_map/ppermute | solution.py:30
  24.2 2.5 %collective-permute-start.11 = (f32[128,256]{1,0:T(8,128)S(1)}, f32[128,256]{1,0:T(8,128)S(1)}, u32[]{:S(2)}, u32[]{:S(2)}) collective-permute-start(f32[128,256]{1,0:T(8,128)S(1)} %shard_map.69.refs_0_), channel_id=1, source_target_pairs={{0,8},{1,9},{2,10},{3,11},{4,12},{5,13},{6,14},{7,15},{8,0},{9,1},... | collective-permute-start | bytes 393224 | tf_op jit(solution)/shard_map/ppermute | solution.py:30
  26.7 3.4 %collective-permute-start.10 = (f32[128,256]{1,0:T(8,128)S(1)}, f32[128,256]{1,0:T(8,128)S(1)}, u32[]{:S(2)}, u32[]{:S(2)}) collective-permute-start(f32[128,256]{1,0:T(8,128)S(1)} %shard_map.69.refs_0_), channel_id=1, source_target_pairs={{0,4},{1,5},{2,6},{3,7},{4,0},{5,1},{6,2},{7,3},{8,12},{9,13},{10,... | collective-permute-start | bytes 393224 | tf_op jit(solution)/shard_map/ppermute | solution.py:30
  30.2 1.2 %shard_map.70 = (f32[4,128,256]{2,1,0:T(8,128)S(1)}, f32[128,256]{1,0:T(8,128)S(1)}, f32[128,256]{1,0:T(8,128)S(1)}, f32[128,256]{1,0:T(8,128)S(1)}) custom-call(s32[5]{0:T(128)S(1)} %stack.23.place_ref, f32[4,128,256]{2,1,0:T(8,128)S(1)} %copy-done.1, f32[2,128,256]{2,1,0:T(8,128)S(1)} %collective-permute-done.mine_ref, ...), custom_call_target="tpu_custom_call" | custom-call | flops 402653184 | bytes 2490388 | tf_op jit(solution)/shard_map/pallas_call | solution.py:207
  31.3 0.1 collective-permute-start.9
  31.4 4.1 %collective-permute-done.11.refs_2_ = f32[128,256]{1,0:T(8,128)S(1)} collective-permute-done((f32[128,256]{1,0:T(8,128)S(1)}, f32[128,256]{1,0:T(8,128)S(1)}, u32[]{:S(2)}, u32[]{:S(2)}) %collective-permute-start.11) | collective-permute-done | bytes 131104 | tf_op jit(solution)/shard_map/ppermute | solution.py:30
  35.6 0.1 collective-permute-start.13
  35.7 1.7 %collective-permute-done.13.gathered_ref = f32[384,256]{1,0:T(8,128)S(1)} collective-permute-done((f32[384,256]{1,0:T(8,128)S(1)}, f32[384,256]{1,0:T(8,128)S(1)}, u32[]{:S(2)}, u32[]{:S(2)}) %collective-permute-start.13) | collective-permute-done | bytes 393248 | tf_op jit(solution)/shard_map/ppermute | solution.py:30
  37.4 0.0 collective-permute-done.9.other_ref
  37.4 1.5 %shard_map.71 = (f32[32,640]{1,0:T(8,128)S(1)}, f32[32,640]{1,0:T(8,128)S(1)}, f32[32,640]{1,0:T(8,128)S(1)}, f32[32,640]{1,0:T(8,128)S(1)}) custom-call(s32[5]{0:T(128)S(1)} %stack.23.place_ref, f32[4,128,256]{2,1,0:T(8,128)S(1)} %get-tuple-element.15.share_ref, f32[4,128,256]{2,1,0:T(8,128)S(1)} %collective-permute-done.9.other_ref, ...), custom_call_target="tpu_custom_call" | custom-call | flops 402653184 | bytes 2424852 | tf_op jit(solution)/shard_map/pallas_call | solution.py:207
  38.9 1.9 %collective-permute-start.16 = (f32[32,640]{1,0:T(8,128)S(1)}, f32[32,640]{1,0:T(8,128)S(1)}, u32[]{:S(2)}, u32[]{:S(2)}) collective-permute-start(f32[32,640]{1,0:T(8,128)S(1)} %get-tuple-element.23), channel_id=1, source_target_pairs={{0,18},{1,19},{2,16},{3,17},{4,22},{5,23},{6,20},{7,21},{8,26},{9,... | collective-permute-start | bytes 245768 | tf_op jit(solution)/shard_map/ppermute | solution.py:30
  40.8 1.3 %collective-permute-start.14 = (f32[32,640]{1,0:T(8,128)S(1)}, f32[32,640]{1,0:T(8,128)S(1)}, u32[]{:S(2)}, u32[]{:S(2)}) collective-permute-start(f32[32,640]{1,0:T(8,128)S(1)} %get-tuple-element.21), channel_id=1, source_target_pairs={{0,2},{1,3},{2,0},{3,1},{4,6},{5,7},{6,4},{7,5},{8,10},{9,11},{10,... | collective-permute-start | bytes 245768 | tf_op jit(solution)/shard_map/ppermute | solution.py:30
  42.1 0.8 %collective-permute-start.15 = (f32[32,640]{1,0:T(8,128)S(1)}, f32[32,640]{1,0:T(8,128)S(1)}, u32[]{:S(2)}, u32[]{:S(2)}) collective-permute-start(f32[32,640]{1,0:T(8,128)S(1)} %get-tuple-element.22), channel_id=1, source_target_pairs={{0,16},{1,17},{2,18},{3,19},{4,20},{5,21},{6,22},{7,23},{8,24},{9,... | collective-permute-start | bytes 245768 | tf_op jit(solution)/shard_map/ppermute | solution.py:30
  42.9 1.5 %collective-permute-done.16 = f32[32,640]{1,0:T(8,128)S(1)} collective-permute-done((f32[32,640]{1,0:T(8,128)S(1)}, f32[32,640]{1,0:T(8,128)S(1)}, u32[]{:S(2)}, u32[]{:S(2)}) %collective-permute-start.16) | collective-permute-done | bytes 81952 | tf_op jit(solution)/shard_map/ppermute | solution.py:30
  44.3 2.0 %collective-permute-done.14 = f32[32,640]{1,0:T(8,128)S(1)} collective-permute-done((f32[32,640]{1,0:T(8,128)S(1)}, f32[32,640]{1,0:T(8,128)S(1)}, u32[]{:S(2)}, u32[]{:S(2)}) %collective-permute-start.14) | collective-permute-done | bytes 81952 | tf_op jit(solution)/shard_map/ppermute | solution.py:30
  46.3 0.2 collective-permute-done.15
  46.6 2.3 %collective-permute-start.19 = (f32[32,640]{1,0:T(8,128)S(1)}, f32[32,640]{1,0:T(8,128)S(1)}, u32[]{:S(2)}, u32[]{:S(2)}) collective-permute-start(f32[32,640]{1,0:T(8,128)S(1)} %add_add_fusion.1), channel_id=1, source_target_pairs={{0,12},{1,13},{2,14},{3,15},{4,8},{5,9},{6,10},{7,11},{8,4},{9,5},... | collective-permute-start | bytes 245768 | tf_op jit(solution)/shard_map/ppermute | solution.py:30
  48.9 0.0 collective-permute-start.17
  48.9 2.1 %collective-permute-start.18 = (f32[32,640]{1,0:T(8,128)S(1)}, f32[32,640]{1,0:T(8,128)S(1)}, u32[]{:S(2)}, u32[]{:S(2)}) collective-permute-start(f32[32,640]{1,0:T(8,128)S(1)} %add_add_fusion.1), channel_id=1, source_target_pairs={{0,8},{1,9},{2,10},{3,11},{4,12},{5,13},{6,14},{7,15},{8,0},{9,1},... | collective-permute-start | bytes 245768 | tf_op jit(solution)/shard_map/ppermute | solution.py:30
  51.0 2.3 %collective-permute-done.19 = f32[32,640]{1,0:T(8,128)S(1)} collective-permute-done((f32[32,640]{1,0:T(8,128)S(1)}, f32[32,640]{1,0:T(8,128)S(1)}, u32[]{:S(2)}, u32[]{:S(2)}) %collective-permute-start.19) | collective-permute-done | bytes 81952 | tf_op jit(solution)/shard_map/ppermute | solution.py:30
  53.4 2.0 %collective-permute-done.17 = f32[32,640]{1,0:T(8,128)S(1)} collective-permute-done((f32[32,640]{1,0:T(8,128)S(1)}, f32[32,640]{1,0:T(8,128)S(1)}, u32[]{:S(2)}, u32[]{:S(2)}) %collective-permute-start.17) | collective-permute-done | bytes 81952 | tf_op jit(solution)/shard_map/ppermute | solution.py:30
  55.4 2.3 %collective-permute-start.22 = (f32[32,640]{1,0:T(8,128)S(1)}, f32[32,640]{1,0:T(8,128)S(1)}, u32[]{:S(2)}, u32[]{:S(2)}) collective-permute-start(f32[32,640]{1,0:T(8,128)S(1)} %add_add_fusion.refs_0_), channel_id=1, source_target_pairs={{0,18},{1,19},{2,16},{3,17},{4,22},{5,23},{6,20},{7,21},{8,26},{9,... | collective-permute-start | bytes 245768 | tf_op jit(solution)/shard_map/ppermute | solution.py:30
  57.7 2.1 %collective-permute-start.21 = (f32[32,640]{1,0:T(8,128)S(1)}, f32[32,640]{1,0:T(8,128)S(1)}, u32[]{:S(2)}, u32[]{:S(2)}) collective-permute-start(f32[32,640]{1,0:T(8,128)S(1)} %add_add_fusion.refs_0_), channel_id=1, source_target_pairs={{0,16},{1,17},{2,18},{3,19},{4,20},{5,21},{6,22},{7,23},{8,24},{9,... | collective-permute-start | bytes 245768 | tf_op jit(solution)/shard_map/ppermute | solution.py:30
  59.8 0.0 collective-permute-start.20
  59.8 1.8 %collective-permute-start.8 = (f32[128,256]{1,0:T(8,128)S(1)}, f32[128,256]{1,0:T(8,128)S(1)}, u32[]{:S(2)}, u32[]{:S(2)}) collective-permute-start(f32[128,256]{1,0:T(8,128)S(1)} %get-tuple-element.18), channel_id=1, source_target_pairs={{0,12},{1,13},{2,14},{3,15},{4,8},{5,9},{6,10},{7,11},{8,4},{9,5},... | collective-permute-start | bytes 393224 | tf_op jit(solution)/shard_map/ppermute | solution.py:30
  61.5 0.0 collective-permute-start.6
  61.5 2.6 %collective-permute-start.7 = (f32[128,256]{1,0:T(8,128)S(1)}, f32[128,256]{1,0:T(8,128)S(1)}, u32[]{:S(2)}, u32[]{:S(2)}) collective-permute-start(f32[128,256]{1,0:T(8,128)S(1)} %get-tuple-element.17), channel_id=1, source_target_pairs={{0,8},{1,9},{2,10},{3,11},{4,12},{5,13},{6,14},{7,15},{8,0},{9,1},... | collective-permute-start | bytes 393224 | tf_op jit(solution)/shard_map/ppermute | solution.py:30
  64.2 0.0 collective-permute-done.21.refs_2_
  64.2 0.0 collective-permute-done.20.refs_1_
  64.2 0.1 collective-permute-start.23
  64.3 3.7 %collective-permute-done.8 = f32[128,256]{1,0:T(8,128)S(1)} collective-permute-done((f32[128,256]{1,0:T(8,128)S(1)}, f32[128,256]{1,0:T(8,128)S(1)}, u32[]{:S(2)}, u32[]{:S(2)}) %collective-permute-start.8) | collective-permute-done | bytes 131104 | tf_op jit(solution)/shard_map/ppermute | solution.py:30
  68.0 1.8 %collective-permute-done.6 = f32[128,256]{1,0:T(8,128)S(1)} collective-permute-done((f32[128,256]{1,0:T(8,128)S(1)}, f32[128,256]{1,0:T(8,128)S(1)}, u32[]{:S(2)}, u32[]{:S(2)}) %collective-permute-start.6) | collective-permute-done | bytes 131104 | tf_op jit(solution)/shard_map/ppermute | solution.py:30
  69.8 2.9 %collective-permute-done.7 = f32[128,256]{1,0:T(8,128)S(1)} collective-permute-done((f32[128,256]{1,0:T(8,128)S(1)}, f32[128,256]{1,0:T(8,128)S(1)}, u32[]{:S(2)}, u32[]{:S(2)}) %collective-permute-start.7) | collective-permute-done | bytes 131104 | tf_op jit(solution)/shard_map/ppermute | solution.py:30
  72.7 0.7 fusion
  73.4 1.5 %shard_map.72 = f32[512,256]{1,0:T(8,128)} custom-call(s32[5]{0:T(128)S(1)} %stack.23.place_ref, f32[512,256]{1,0:T(8,128)S(1)} %copy-done, f32[128,256]{1,0:T(8,128)S(1)} %collective-permute-done.23.other_ref, f32[32,640]{1,0:T(8,128)S(1)} %add_add_fusion.refs_0_, f32[32,640]{1,0:T(8,128)S(1)} %collective-permute-done.20.refs_1_, ...), custom_call_target="tpu_custom_call" | custom-call | bytes 1507348 | tf_op jit(solution)/shard_map/pallas_call | solution.py:207
  (21 shorter events, 0.1 us)
Async XLA Ops:
  0.7 0.7 copy-start.2
  4.3 25.9 %copy-start.1 = (f32[4,128,256]{2,1,0:T(8,128)S(1)}, f32[4,128,256]{2,1,0:T(8,128)}, u32[]{:S(2)}) copy-start(f32[4,128,256]{2,1,0:T(8,128)} %get-tuple-element.13.kept_ref) | copy-start | bytes 1572868
  4.3 11.4 %collective-permute-start = (f32[2,128,256]{2,1,0:T(8,128)S(1)}, f32[2,128,256]{2,1,0:T(8,128)S(1)}, u32[]{:S(2)}, u32[]{:S(2)}) collective-permute-start(f32[2,128,256]{2,1,0:T(8,128)S(1)} %get-tuple-element.14), channel_id=1, source_target_pairs={{0,2},{1,3},{2,0},{3,1},{4,6},{5,7},{6,4},{7,5},{8,10},{9,11},{10,... | collective-permute-start | bytes 786440 | tf_op jit(solution)/shard_map/ppermute | solution.py:30
  9.3 6.4 %collective-permute-start.2 = (f32[128,256]{1,0:T(8,128)S(1)}, f32[128,256]{1,0:T(8,128)S(1)}, u32[]{:S(2)}, u32[]{:S(2)}) collective-permute-start(f32[128,256]{1,0:T(8,128)S(1)} %shard_map.69.refs_0_), channel_id=1, source_target_pairs={{0,0},{1,1},{2,16},{3,17},{4,2},{5,3},{6,18},{7,19},{8,4},{9,5},{1... | collective-permute-start | bytes 393224 | tf_op jit(solution)/shard_map/ppermute | solution.py:30
  15.7 14.5 %collective-permute-start.1 = (f32[2,128,256]{2,1,0:T(8,128)S(1)}, f32[2,128,256]{2,1,0:T(8,128)S(1)}, u32[]{:S(2)}, u32[]{:S(2)}) collective-permute-start(f32[2,128,256]{2,1,0:T(8,128)S(1)} %collective-permute-done.mine_ref), channel_id=1, source_target_pairs={{0,1},{1,0},{2,3},{3,2},{4,5},{5,4},{6,7},{7,6},{8,9},{9,8},{10,11... | collective-permute-start | bytes 786440 | tf_op jit(solution)/shard_map/ppermute | solution.py:30
  15.7 8.5 %collective-permute-start.3 = (f32[128,256]{1,0:T(8,128)S(1)}, f32[128,256]{1,0:T(8,128)S(1)}, u32[]{:S(2)}, u32[]{:S(2)}) collective-permute-start(f32[128,256]{1,0:T(8,128)S(1)} %collective-permute-done.2.refs_0_), channel_id=1, source_target_pairs={{0,16},{1,17},{2,18},{3,19},{4,20},{5,21},{6,22},{7,23},{8,24},{9,... | collective-permute-start | bytes 393224 | tf_op jit(solution)/shard_map/ppermute | solution.py:30
  18.6 8.2 %collective-permute-start.4 = (f32[128,256]{1,0:T(8,128)S(1)}, f32[128,256]{1,0:T(8,128)S(1)}, u32[]{:S(2)}, u32[]{:S(2)}) collective-permute-start(f32[128,256]{1,0:T(8,128)S(1)} %collective-permute-done.2.refs_0_), channel_id=1, source_target_pairs={{0,2},{1,3},{2,0},{3,1},{4,6},{5,7},{6,4},{7,5},{8,10},{9,11},{10,... | collective-permute-start | bytes 393224 | tf_op jit(solution)/shard_map/ppermute | solution.py:30
  19.3 10.9 %collective-permute-start.5 = (f32[128,256]{1,0:T(8,128)S(1)}, f32[128,256]{1,0:T(8,128)S(1)}, u32[]{:S(2)}, u32[]{:S(2)}) collective-permute-start(f32[128,256]{1,0:T(8,128)S(1)} %collective-permute-done.2.refs_0_), channel_id=1, source_target_pairs={{0,18},{1,19},{2,16},{3,17},{4,22},{5,23},{6,20},{7,21},{8,26},{9,... | collective-permute-start | bytes 393224 | tf_op jit(solution)/shard_map/ppermute | solution.py:30
  20.0 11.4 %collective-permute-start.12 = (f32[128,256]{1,0:T(8,128)S(1)}, f32[128,256]{1,0:T(8,128)S(1)}, u32[]{:S(2)}, u32[]{:S(2)}) collective-permute-start(f32[128,256]{1,0:T(8,128)S(1)} %shard_map.69.refs_0_), channel_id=1, source_target_pairs={{0,12},{1,13},{2,14},{3,15},{4,8},{5,9},{6,10},{7,11},{8,4},{9,5},... | collective-permute-start | bytes 393224 | tf_op jit(solution)/shard_map/ppermute | solution.py:30
  24.2 11.4 %collective-permute-start.11 = (f32[128,256]{1,0:T(8,128)S(1)}, f32[128,256]{1,0:T(8,128)S(1)}, u32[]{:S(2)}, u32[]{:S(2)}) collective-permute-start(f32[128,256]{1,0:T(8,128)S(1)} %shard_map.69.refs_0_), channel_id=1, source_target_pairs={{0,8},{1,9},{2,10},{3,11},{4,12},{5,13},{6,14},{7,15},{8,0},{9,1},... | collective-permute-start | bytes 393224 | tf_op jit(solution)/shard_map/ppermute | solution.py:30
  26.7 8.8 %collective-permute-start.10 = (f32[128,256]{1,0:T(8,128)S(1)}, f32[128,256]{1,0:T(8,128)S(1)}, u32[]{:S(2)}, u32[]{:S(2)}) collective-permute-start(f32[128,256]{1,0:T(8,128)S(1)} %shard_map.69.refs_0_), channel_id=1, source_target_pairs={{0,4},{1,5},{2,6},{3,7},{4,0},{5,1},{6,2},{7,3},{8,12},{9,13},{10,... | collective-permute-start | bytes 393224 | tf_op jit(solution)/shard_map/ppermute | solution.py:30
  31.3 6.0 %collective-permute-start.9 = (f32[4,128,256]{2,1,0:T(8,128)S(1)}, f32[4,128,256]{2,1,0:T(8,128)S(1)}, u32[]{:S(2)}, u32[]{:S(2)}) collective-permute-start(f32[4,128,256]{2,1,0:T(8,128)S(1)} %get-tuple-element.15.share_ref), channel_id=1, source_target_pairs={{0,1},{1,0},{2,3},{3,2},{4,5},{5,4},{6,7},{7,6},{8,9},{9,8},{10,11... | collective-permute-start | bytes 1572872 | tf_op jit(solution)/shard_map/ppermute | solution.py:30
  35.6 1.8 %collective-permute-start.13 = (f32[384,256]{1,0:T(8,128)S(1)}, f32[384,256]{1,0:T(8,128)S(1)}, u32[]{:S(2)}, u32[]{:S(2)}) collective-permute-start(f32[384,256]{1,0:T(8,128)S(1)} %pad_maximum_fusion), channel_id=1, source_target_pairs={{0,1},{1,0},{2,3},{3,2},{4,5},{5,4},{6,7},{7,6},{8,9},{9,8},{10,11... | collective-permute-start | bytes 1179656 | tf_op jit(solution)/shard_map/ppermute | solution.py:30
  38.9 5.5 %collective-permute-start.16 = (f32[32,640]{1,0:T(8,128)S(1)}, f32[32,640]{1,0:T(8,128)S(1)}, u32[]{:S(2)}, u32[]{:S(2)}) collective-permute-start(f32[32,640]{1,0:T(8,128)S(1)} %get-tuple-element.23), channel_id=1, source_target_pairs={{0,18},{1,19},{2,16},{3,17},{4,22},{5,23},{6,20},{7,21},{8,26},{9,... | collective-permute-start | bytes 245768 | tf_op jit(solution)/shard_map/ppermute | solution.py:30
  40.8 5.5 %collective-permute-start.14 = (f32[32,640]{1,0:T(8,128)S(1)}, f32[32,640]{1,0:T(8,128)S(1)}, u32[]{:S(2)}, u32[]{:S(2)}) collective-permute-start(f32[32,640]{1,0:T(8,128)S(1)} %get-tuple-element.21), channel_id=1, source_target_pairs={{0,2},{1,3},{2,0},{3,1},{4,6},{5,7},{6,4},{7,5},{8,10},{9,11},{10,... | collective-permute-start | bytes 245768 | tf_op jit(solution)/shard_map/ppermute | solution.py:30
  42.1 4.4 %collective-permute-start.15 = (f32[32,640]{1,0:T(8,128)S(1)}, f32[32,640]{1,0:T(8,128)S(1)}, u32[]{:S(2)}, u32[]{:S(2)}) collective-permute-start(f32[32,640]{1,0:T(8,128)S(1)} %get-tuple-element.22), channel_id=1, source_target_pairs={{0,16},{1,17},{2,18},{3,19},{4,20},{5,21},{6,22},{7,23},{8,24},{9,... | collective-permute-start | bytes 245768 | tf_op jit(solution)/shard_map/ppermute | solution.py:30
  46.6 6.8 %collective-permute-start.19 = (f32[32,640]{1,0:T(8,128)S(1)}, f32[32,640]{1,0:T(8,128)S(1)}, u32[]{:S(2)}, u32[]{:S(2)}) collective-permute-start(f32[32,640]{1,0:T(8,128)S(1)} %add_add_fusion.1), channel_id=1, source_target_pairs={{0,12},{1,13},{2,14},{3,15},{4,8},{5,9},{6,10},{7,11},{8,4},{9,5},... | collective-permute-start | bytes 245768 | tf_op jit(solution)/shard_map/ppermute | solution.py:30
  48.9 6.4 %collective-permute-start.17 = (f32[32,640]{1,0:T(8,128)S(1)}, f32[32,640]{1,0:T(8,128)S(1)}, u32[]{:S(2)}, u32[]{:S(2)}) collective-permute-start(f32[32,640]{1,0:T(8,128)S(1)} %add_add_fusion.1), channel_id=1, source_target_pairs={{0,4},{1,5},{2,6},{3,7},{4,0},{5,1},{6,2},{7,3},{8,12},{9,13},{10,... | collective-permute-start | bytes 245768 | tf_op jit(solution)/shard_map/ppermute | solution.py:30
  48.9 6.4 %collective-permute-start.18 = (f32[32,640]{1,0:T(8,128)S(1)}, f32[32,640]{1,0:T(8,128)S(1)}, u32[]{:S(2)}, u32[]{:S(2)}) collective-permute-start(f32[32,640]{1,0:T(8,128)S(1)} %add_add_fusion.1), channel_id=1, source_target_pairs={{0,8},{1,9},{2,10},{3,11},{4,12},{5,13},{6,14},{7,15},{8,0},{9,1},... | collective-permute-start | bytes 245768 | tf_op jit(solution)/shard_map/ppermute | solution.py:30
  55.4 6.2 %collective-permute-start.22 = (f32[32,640]{1,0:T(8,128)S(1)}, f32[32,640]{1,0:T(8,128)S(1)}, u32[]{:S(2)}, u32[]{:S(2)}) collective-permute-start(f32[32,640]{1,0:T(8,128)S(1)} %add_add_fusion.refs_0_), channel_id=1, source_target_pairs={{0,18},{1,19},{2,16},{3,17},{4,22},{5,23},{6,20},{7,21},{8,26},{9,... | collective-permute-start | bytes 245768 | tf_op jit(solution)/shard_map/ppermute | solution.py:30
  57.7 6.5 %collective-permute-start.21 = (f32[32,640]{1,0:T(8,128)S(1)}, f32[32,640]{1,0:T(8,128)S(1)}, u32[]{:S(2)}, u32[]{:S(2)}) collective-permute-start(f32[32,640]{1,0:T(8,128)S(1)} %add_add_fusion.refs_0_), channel_id=1, source_target_pairs={{0,16},{1,17},{2,18},{3,19},{4,20},{5,21},{6,22},{7,23},{8,24},{9,... | collective-permute-start | bytes 245768 | tf_op jit(solution)/shard_map/ppermute | solution.py:30
  59.8 4.4 %collective-permute-start.20 = (f32[32,640]{1,0:T(8,128)S(1)}, f32[32,640]{1,0:T(8,128)S(1)}, u32[]{:S(2)}, u32[]{:S(2)}) collective-permute-start(f32[32,640]{1,0:T(8,128)S(1)} %add_add_fusion.refs_0_), channel_id=1, source_target_pairs={{0,2},{1,3},{2,0},{3,1},{4,6},{5,7},{6,4},{7,5},{8,10},{9,11},{10,... | collective-permute-start | bytes 245768 | tf_op jit(solution)/shard_map/ppermute | solution.py:30
  59.8 8.3 %collective-permute-start.8 = (f32[128,256]{1,0:T(8,128)S(1)}, f32[128,256]{1,0:T(8,128)S(1)}, u32[]{:S(2)}, u32[]{:S(2)}) collective-permute-start(f32[128,256]{1,0:T(8,128)S(1)} %get-tuple-element.18), channel_id=1, source_target_pairs={{0,12},{1,13},{2,14},{3,15},{4,8},{5,9},{6,10},{7,11},{8,4},{9,5},... | collective-permute-start | bytes 393224 | tf_op jit(solution)/shard_map/ppermute | solution.py:30
  61.5 8.3 %collective-permute-start.6 = (f32[128,256]{1,0:T(8,128)S(1)}, f32[128,256]{1,0:T(8,128)S(1)}, u32[]{:S(2)}, u32[]{:S(2)}) collective-permute-start(f32[128,256]{1,0:T(8,128)S(1)} %get-tuple-element.16), channel_id=1, source_target_pairs={{0,4},{1,5},{2,6},{3,7},{4,0},{5,1},{6,2},{7,3},{8,12},{9,13},{10,... | collective-permute-start | bytes 393224 | tf_op jit(solution)/shard_map/ppermute | solution.py:30
  61.5 11.2 %collective-permute-start.7 = (f32[128,256]{1,0:T(8,128)S(1)}, f32[128,256]{1,0:T(8,128)S(1)}, u32[]{:S(2)}, u32[]{:S(2)}) collective-permute-start(f32[128,256]{1,0:T(8,128)S(1)} %get-tuple-element.17), channel_id=1, source_target_pairs={{0,8},{1,9},{2,10},{3,11},{4,12},{5,13},{6,14},{7,15},{8,0},{9,1},... | collective-permute-start | bytes 393224 | tf_op jit(solution)/shard_map/ppermute | solution.py:30
  64.2 9.3 %copy-start = (f32[512,256]{1,0:T(8,128)S(1)}, f32[512,256]{1,0:T(8,128)}, u32[]{:S(2)}) copy-start(f32[512,256]{1,0:T(8,128)} %pivot_ref.1) | copy-start | bytes 1572868
  64.2 9.2 %collective-permute-start.23 = (f32[128,256]{1,0:T(8,128)S(1)}, f32[128,256]{1,0:T(8,128)S(1)}, u32[]{:S(2)}, u32[]{:S(2)}) collective-permute-start(f32[128,256]{1,0:T(8,128)S(1)} %pad_maximum_fusion.1), channel_id=1, source_target_pairs={{0,1},{1,0},{2,3},{3,2},{4,5},{5,4},{6,7},{7,6},{8,9},{9,8},{10,11... | collective-permute-start | bytes 393224 | tf_op jit(solution)/shard_map/ppermute | solution.py:30

commit v4 on v3

--- a/solution.py
+++ b/solution.py
@@ -11,7 +11,7 @@
 AXES = ("row", "col", "rep")
 PAIR = 2
 ROOM_OWN = 56380000
-ROOM_MASK = 56000000
+ROOM_MASK = 55500000
 F32, BF16 = jnp.float32, jnp.bfloat16
 
 
@@ -49,6 +49,10 @@
     )
 
 
+def here():
+    return (lax.axis_index(name) for name in AXES)
+
+
 def tile_at(index, size):
     return pl.ds(pl.multiple_of(index * size, size), size)
 
@@ -60,62 +64,61 @@
     return copies
 
 
-def own_kernel(place_ref, factor_ref, normalizer_ref, normed_ref, factor_in, normalizer_in, sems):
-    columns = tile_at(place_ref[3], normed_ref.shape[1])
-    for copy in load_all(
-        [
-            (factor_ref, factor_in, sems.at[0]),
-            (normalizer_ref.at[:, columns], normalizer_in, sems.at[1]),
+def normed_half(other, factor_ref, normalizer_ref, normed_ref, factor_in, normalizer_in, sems):
+    rep = lax.axis_index("rep")
+    half = normed_ref.shape[1]
+    columns = tile_at(1 - rep if other else rep, half)
+    chunks, depth = normalizer_in.shape[:2]
+    copies = load_all(
+        [(factor_ref, factor_in, sems.at[chunks])]
+        + [
+            (normalizer_ref.at[pl.ds(i * depth, depth), columns], normalizer_in.at[i], sems.at[i])
+            for i in range(chunks)
         ]
-    ):
+    )
+    total = None
+    for i, copy in enumerate(copies):
         copy.wait()
-    normed_ref[...] = split_dot(split(factor_in[...]), split(normalizer_in[...]))
-
-
-def mask_kernel(planes, rows, place_ref, marks_ref, factor_ref, normalizer_ref, full_ref, *refs):
-    other_ref, kept_ref, given_ref, factor_in, normalizer_in, full_in, sems = refs
-    row, plane, side, rep = (place_ref[i] for i in range(4))
-    tile, half = other_ref.shape
+        if i:
+            left = factor_in[:, (i - 1) * depth : i * depth]
+            term = split_dot(split(left), split(normalizer_in[i - 1]))
+            total = term if total is None else total + term
+    normed_ref[...] = total
+
+
+def mask_kernel(planes, rows, marks_ref, full_ref, kept_ref, given_ref, full_in, sems):
+    row, col, rep = here()
+    plane, side = col // PAIR, col % PAIR
     cut = planes // 2
+    tile = kept_ref.shape[1]
     band = PAIR * tile
     copies = load_all(
         [
             (full_ref.at[tile_at(plane ^ k, band), :], full_in.at[k], sems.at[k])
             for k in range(planes)
         ]
-        + [
-            (factor_ref, factor_in, sems.at[planes]),
-            (normalizer_ref.at[:, tile_at(1 - rep, half)], normalizer_in, sems.at[planes + 1]),
-        ]
-    )
-    for copy in copies[:planes]:
-        copy.wait()
+    )
 
     def masked(k, wanted, m):
         across = row ^ m
         mark = marks_ref[across, (plane ^ k) * PAIR + wanted].astype(F32)
         return full_in[k, tile_at(wanted, tile), tile_at(across, tile)] * mark
 
+    for k in range(planes):
+        copies[k].wait()
+        for m in range(rows):
+            kept_ref[k, :, m * tile : (m + 1) * tile] = masked(k, side, m)
     for m in range(rows):
-        columns = pl.ds(m * tile, tile)
 
         @pl.loop(0, cut)
         def _(k):
-            given_ref[k, :, columns] = masked(k + rep * cut, 1 - side, m)
-
-        @pl.loop(0, planes)
-        def _(k):
-            kept_ref[k, :, columns] = masked(k, side, m)
-
-    for copy in copies[planes:]:
-        copy.wait()
-    other_ref[...] = split_dot(split(factor_in[...]), split(normalizer_in[...]))
-
-
-def product_kernel(planes, members, place_ref, kept_ref, mine_ref, theirs_ref, *refs):
+            given_ref[k, :, m * tile : (m + 1) * tile] = masked(k + rep * cut, 1 - side, m)
+
+
+def product_kernel(planes, members, kept_ref, mine_ref, theirs_ref, *refs):
     arrived, outs = refs[:members], refs[members:]
     cut = planes // 2
-    rep = place_ref[3]
+    rep = lax.axis_index("rep")
     right = split(jnp.concatenate([ref[...] for ref in arrived], 0))
     for k in range(planes):
         taken = jnp.where(rep == k // cut, mine_ref[k % cut], theirs_ref[k % cut])
@@ -126,9 +129,10 @@
             outs[k][...] = share
 
 
-def coupling_kernel(members, planes, place_ref, share_ref, other_ref, gathered_ref, *refs):
+def coupling_kernel(members, planes, share_ref, other_ref, gathered_ref, *refs):
     strip, outs, total_ref = refs[: planes + 1], refs[planes + 1 : -1], refs[-1]
-    place, first = place_ref[4], place_ref[3] == 0
+    row, col, rep = here()
+    place, first = row * PAIR + col % PAIR, rep == 0
     tile, half = strip[0].shape
     quarter = half // 2
     step = quarter // members
@@ -157,9 +161,10 @@
         outs[k][...] = total_ref[tile_at(place ^ k, step), :]
 
 
-def finish_kernel(members, place_ref, pivot_ref, other_ref, *refs):
+def finish_kernel(members, pivot_ref, other_ref, *refs):
     parts, out_ref, total_ref, between_ref = refs[:members], *refs[members:]
-    place, rep = place_ref[4], place_ref[3]
+    row, col, rep = here()
+    place = row * PAIR + col % PAIR
     half = out_ref.shape[1]
     quarter = half // 2
     step = quarter // members
@@ -219,35 +224,33 @@
     tile = factor.shape[0]
     half = pivot_inverse.shape[1]
     rows, cols = lax.axis_size("row"), lax.axis_size("col")
-    row, col, rep = (lax.axis_index(name) for name in AXES)
     planes, members = cols // PAIR, rows * PAIR
-    plane, side = col // PAIR, col % PAIR
-    place = jnp.stack([row, plane, side, rep, row * PAIR + side]).astype(jnp.int32)
     depth = rows * tile
 
     cut, inner = planes // 2, factor.shape[1]
     inner = factor.shape[1]
-    (own_normed,) = call(
-        own_kernel,
-        [(tile, half)],
-        "shh",
-        [place, factor, factor_normalizer],
-        [(tile, inner), (inner, half), pltpu.SemaphoreType.DMA((2,))],
-        room=ROOM_OWN,
-    )
-    other_normed, kept, given = call(
+    chunks = inner // tile
+
+    def normed(other):
+        return call(
+            functools.partial(normed_half, other),
+            [(tile, half)],
+            "hh",
+            [factor, factor_normalizer],
+            [(tile, inner), (chunks, tile, half), pltpu.SemaphoreType.DMA((chunks + 1,))],
+            room=ROOM_OWN,
+        )[0]
+
+    own_normed = normed(False)
+    kept, given = call(
         functools.partial(mask_kernel, planes, rows),
-        [(tile, half), (planes, tile, depth), (cut, tile, depth)],
-        "sshhh",
-        [place, tile_structure.T, factor, factor_normalizer, ancestor_inverse],
-        [
-            (tile, inner),
-            (inner, half),
-            (planes, PAIR * tile, depth),
-            pltpu.SemaphoreType.DMA((2 + planes,)),
-        ],
+        [(planes, tile, depth), (cut, tile, depth)],
+        "sh",
+        [tile_structure.T, ancestor_inverse],
+        [(planes, PAIR * tile, depth), pltpu.SemaphoreType.DMA((planes,))],
         room=ROOM_MASK,
     )
+    other_normed = normed(True)
 
     def to_plane(r, c, p):
         block = r * cols + c
@@ -274,8 +277,8 @@
     product, *shares = call(
         functools.partial(product_kernel, planes, members),
         [(planes, tile, half)] + [(tile, half)] * (planes - 1),
-        "s",
-        [place, kept, mine, theirs, *arrived],
+        "",
+        [kept, mine, theirs, *arrived],
         flops=12 * planes * tile * depth * half,
     )
     other_product = swap_core(product)
@@ -287,8 +290,8 @@
     parts = call(
         functools.partial(coupling_kernel, members, planes),
         [(step, width)] * members,
-        "s",
-        [place, product, other_product, other_strip, *strip, other_normed],
+        "",
+        [product, other_product, other_strip, *strip, other_normed],
         [(quarter, width)],
         flops=12 * planes * tile * half * half,
     )
@@ -307,8 +310,8 @@
     (diag_block,) = call(
         functools.partial(finish_kernel, members),
         [pivot_inverse.shape],
-        "s",
-        [place, pivot_inverse, other_between, *parts],
+        "",
+        [pivot_inverse, other_between, *parts],
         [(quarter, width), (quarter, half)],
     )
     return ancestor_columns, diag_block

time: 75.1 us -> 73.6 us (0.980)
  starting transfers between devices: 35.6 us -> 34.2 us
  Pallas kernels: 8.99 us -> 7.89 us
  waiting for transfers between devices: 28 us -> 29 us
    ppermute x24, starting transfers between devices: 35.6 us -> 34.2 us  [send(): return lax.ppermute(block, AXES, route)]
    pallas_call x5 -> x6, Pallas kernels: 8.99 us -> 7.89 us  [call(): pl.pallas_call(kernel, out_shape=[jax.ShapeDtypeStruct(shape, F32) for sh...]
    ppermute x24, waiting for transfers between devices: 28 us -> 29 us  [send(): return lax.ppermute(block, AXES, route)]
  transfers between devices with their start and end apart: 24 -> 24, of which waited for: 11 -> 10; matrix products, arithmetic and copies ran while one was open for 1% -> 1% of each run, Pallas kernels for 4% -> 6%
where the time goes in v4:
time: 73.6 us; the launch traced here: 73.4 us
  starting transfers between devices  34.2 us (46%)
  waiting for transfers between devices  29 us (39%)
  Pallas kernels  7.89 us (11%)
  between operations  0.81 us (1%)
  other arithmetic  0.76 us (1%)
    ppermute x24, starting transfers between devices, send(): return lax.ppermute(block, AXES, route)  34.2 us
    ppermute x24, waiting for transfers between devices, send(): return lax.ppermute(block, AXES, route)  29 us
    pallas_call x6, Pallas kernels, call(): pl.pallas_call(kernel, out_shape=[jax.ShapeDtypeStruct(shape, F32) for sh...  7.89 us
  transfers between devices with their start and end apart: 24, of which 10 were waited for; matrix products, arithmetic and copies ran while one was open for 1% of the time, Pallas kernels for 6%

profile of v4, /device:TPU:0, one launch (start us, length us, event | category | flops | bytes accessed | tf_op | source)
XLA Modules:
  0.0 73.4 jit_solution(13371548119426591492)
XLA Ops:
  0.6 0.7 copy-done.1
  1.3 1.9 %shard_map.68 = (f32[4,128,256]{2,1,0:T(8,128)S(1)}, f32[2,128,256]{2,1,0:T(8,128)S(1)}) custom-call(s32[2,8]{1,0:T(2,128)S(1)} %bitcast.5, f32[1024,256]{1,0:T(8,128)} %full_ref.1), custom_call_target="tpu_custom_call" | custom-call | bytes 1835072 | tf_op jit(solution)/shard_map/pallas_call | solution.py:212
  3.2 3.0 %collective-permute-start = (f32[2,128,256]{2,1,0:T(8,128)S(1)}, f32[2,128,256]{2,1,0:T(8,128)S(1)}, u32[]{:S(2)}, u32[]{:S(2)}) collective-permute-start(f32[2,128,256]{2,1,0:T(8,128)S(1)} %get-tuple-element.13), channel_id=1, source_target_pairs={{0,2},{1,3},{2,0},{3,1},{4,6},{5,7},{6,4},{7,5},{8,10},{9,11},{10,... | collective-permute-start | bytes 786440 | tf_op jit(solution)/shard_map/ppermute | solution.py:30
  6.2 1.7 %shard_map.69.refs_0_ = f32[128,256]{1,0:T(8,128)S(1)} custom-call(f32[128,512]{1,0:T(8,128)} %factor_ref.3, f32[512,512]{1,0:T(8,128)} %normalizer_ref.3), custom_call_target="tpu_custom_call" | custom-call | bytes 1441792 | tf_op jit(solution)/shard_map/pallas_call | solution.py:212
  7.9 0.7 collective-permute-start.2
  8.6 6.0 %collective-permute-done.mine_ref = f32[2,128,256]{2,1,0:T(8,128)S(1)} collective-permute-done((f32[2,128,256]{2,1,0:T(8,128)S(1)}, f32[2,128,256]{2,1,0:T(8,128)S(1)}, u32[]{:S(2)}, u32[]{:S(2)}) %collective-permute-start) | collective-permute-done | bytes 262176 | tf_op jit(solution)/shard_map/ppermute | solution.py:30
  14.6 0.0 collective-permute-start.1
  14.6 0.0 collective-permute-done.2.refs_0_
  14.6 2.6 %collective-permute-start.3 = (f32[128,256]{1,0:T(8,128)S(1)}, f32[128,256]{1,0:T(8,128)S(1)}, u32[]{:S(2)}, u32[]{:S(2)}) collective-permute-start(f32[128,256]{1,0:T(8,128)S(1)} %collective-permute-done.2.refs_0_), channel_id=1, source_target_pairs={{0,16},{1,17},{2,18},{3,19},{4,20},{5,21},{6,22},{7,23},{8,24},{9,... | collective-permute-start | bytes 393224 | tf_op jit(solution)/shard_map/ppermute | solution.py:30
  17.2 0.7 collective-permute-start.4
  17.9 0.8 %collective-permute-start.5 = (f32[128,256]{1,0:T(8,128)S(1)}, f32[128,256]{1,0:T(8,128)S(1)}, u32[]{:S(2)}, u32[]{:S(2)}) collective-permute-start(f32[128,256]{1,0:T(8,128)S(1)} %collective-permute-done.2.refs_0_), channel_id=1, source_target_pairs={{0,18},{1,19},{2,16},{3,17},{4,22},{5,23},{6,20},{7,21},{8,26},{9,... | collective-permute-start | bytes 393224 | tf_op jit(solution)/shard_map/ppermute | solution.py:30
  18.7 4.4 %collective-permute-start.12 = (f32[128,256]{1,0:T(8,128)S(1)}, f32[128,256]{1,0:T(8,128)S(1)}, u32[]{:S(2)}, u32[]{:S(2)}) collective-permute-start(f32[128,256]{1,0:T(8,128)S(1)} %shard_map.69.refs_0_), channel_id=1, source_target_pairs={{0,12},{1,13},{2,14},{3,15},{4,8},{5,9},{6,10},{7,11},{8,4},{9,5},... | collective-permute-start | bytes 393224 | tf_op jit(solution)/shard_map/ppermute | solution.py:30
  23.1 2.3 %collective-permute-start.11 = (f32[128,256]{1,0:T(8,128)S(1)}, f32[128,256]{1,0:T(8,128)S(1)}, u32[]{:S(2)}, u32[]{:S(2)}) collective-permute-start(f32[128,256]{1,0:T(8,128)S(1)} %shard_map.69.refs_0_), channel_id=1, source_target_pairs={{0,8},{1,9},{2,10},{3,11},{4,12},{5,13},{6,14},{7,15},{8,0},{9,1},... | collective-permute-start | bytes 393224 | tf_op jit(solution)/shard_map/ppermute | solution.py:30
  25.4 0.0 collective-permute-done.4.refs_2_
  25.4 3.4 %collective-permute-start.10 = (f32[128,256]{1,0:T(8,128)S(1)}, f32[128,256]{1,0:T(8,128)S(1)}, u32[]{:S(2)}, u32[]{:S(2)}) collective-permute-start(f32[128,256]{1,0:T(8,128)S(1)} %shard_map.69.refs_0_), channel_id=1, source_target_pairs={{0,4},{1,5},{2,6},{3,7},{4,0},{5,1},{6,2},{7,3},{8,12},{9,13},{10,... | collective-permute-start | bytes 393224 | tf_op jit(solution)/shard_map/ppermute | solution.py:30
  28.8 0.0 collective-permute-done.5.refs_3_
  28.8 0.0 collective-permute-done.1.theirs_ref
  28.8 0.6 shard_map.70
  29.5 0.1 collective-permute-start.9
  29.6 0.0 collective-permute-done.12.refs_3_
  29.6 4.9 %collective-permute-done.11.refs_2_ = f32[128,256]{1,0:T(8,128)S(1)} collective-permute-done((f32[128,256]{1,0:T(8,128)S(1)}, f32[128,256]{1,0:T(8,128)S(1)}, u32[]{:S(2)}, u32[]{:S(2)}) %collective-permute-start.11) | collective-permute-done | bytes 131104 | tf_op jit(solution)/shard_map/ppermute | solution.py:30
  34.5 0.0 collective-permute-done.10.refs_1_
  34.5 0.1 collective-permute-start.13
  34.6 1.7 %shard_map.71.refs_4_ = f32[128,256]{1,0:T(8,128)S(1)} custom-call(f32[128,512]{1,0:T(8,128)} %factor_ref.3, f32[512,512]{1,0:T(8,128)} %normalizer_ref.3), custom_call_target="tpu_custom_call" | custom-call | bytes 1441792 | tf_op jit(solution)/shard_map/pallas_call | solution.py:212
  36.3 0.9 %shard_map.72 = (f32[32,640]{1,0:T(8,128)S(1)}, f32[32,640]{1,0:T(8,128)S(1)}, f32[32,640]{1,0:T(8,128)S(1)}, f32[32,640]{1,0:T(8,128)S(1)}) custom-call(f32[4,128,256]{2,1,0:T(8,128)S(1)} %get-tuple-element.14.share_ref, f32[4,128,256]{2,1,0:T(8,128)S(1)} %collective-permute-done.9.other_ref, f32[384,256]{1,0:T(8,128)S(1)} %collective-permute-done.13.gathered_ref, ...), custom_call_target="tpu_custom_call" | custom-call | flops 402653184 | bytes 2424832 | tf_op jit(solution)/shard_map/pallas_call | solution.py:212
  37.3 1.7 %collective-permute-start.16 = (f32[32,640]{1,0:T(8,128)S(1)}, f32[32,640]{1,0:T(8,128)S(1)}, u32[]{:S(2)}, u32[]{:S(2)}) collective-permute-start(f32[32,640]{1,0:T(8,128)S(1)} %get-tuple-element.21), channel_id=1, source_target_pairs={{0,18},{1,19},{2,16},{3,17},{4,22},{5,23},{6,20},{7,21},{8,26},{9,... | collective-permute-start | bytes 245768 | tf_op jit(solution)/shard_map/ppermute | solution.py:30
  38.9 1.3 %collective-permute-start.14 = (f32[32,640]{1,0:T(8,128)S(1)}, f32[32,640]{1,0:T(8,128)S(1)}, u32[]{:S(2)}, u32[]{:S(2)}) collective-permute-start(f32[32,640]{1,0:T(8,128)S(1)} %get-tuple-element.19), channel_id=1, source_target_pairs={{0,2},{1,3},{2,0},{3,1},{4,6},{5,7},{6,4},{7,5},{8,10},{9,11},{10,... | collective-permute-start | bytes 245768 | tf_op jit(solution)/shard_map/ppermute | solution.py:30
  40.3 0.7 collective-permute-start.15
  41.0 2.2 %collective-permute-done.16 = f32[32,640]{1,0:T(8,128)S(1)} collective-permute-done((f32[32,640]{1,0:T(8,128)S(1)}, f32[32,640]{1,0:T(8,128)S(1)}, u32[]{:S(2)}, u32[]{:S(2)}) %collective-permute-start.16) | collective-permute-done | bytes 81952 | tf_op jit(solution)/shard_map/ppermute | solution.py:30
  43.1 1.7 %collective-permute-done.14 = f32[32,640]{1,0:T(8,128)S(1)} collective-permute-done((f32[32,640]{1,0:T(8,128)S(1)}, f32[32,640]{1,0:T(8,128)S(1)}, u32[]{:S(2)}, u32[]{:S(2)}) %collective-permute-start.14) | collective-permute-done | bytes 81952 | tf_op jit(solution)/shard_map/ppermute | solution.py:30
  44.8 0.0 collective-permute-done.15
  44.9 2.7 %collective-permute-start.19 = (f32[32,640]{1,0:T(8,128)S(1)}, f32[32,640]{1,0:T(8,128)S(1)}, u32[]{:S(2)}, u32[]{:S(2)}) collective-permute-start(f32[32,640]{1,0:T(8,128)S(1)} %add_add_fusion.1), channel_id=1, source_target_pairs={{0,12},{1,13},{2,14},{3,15},{4,8},{5,9},{6,10},{7,11},{8,4},{9,5},... | collective-permute-start | bytes 245768 | tf_op jit(solution)/shard_map/ppermute | solution.py:30
  47.6 1.7 %collective-permute-start.18 = (f32[32,640]{1,0:T(8,128)S(1)}, f32[32,640]{1,0:T(8,128)S(1)}, u32[]{:S(2)}, u32[]{:S(2)}) collective-permute-start(f32[32,640]{1,0:T(8,128)S(1)} %add_add_fusion.1), channel_id=1, source_target_pairs={{0,8},{1,9},{2,10},{3,11},{4,12},{5,13},{6,14},{7,15},{8,0},{9,1},... | collective-permute-start | bytes 245768 | tf_op jit(solution)/shard_map/ppermute | solution.py:30
  49.3 2.5 %collective-permute-done.19 = f32[32,640]{1,0:T(8,128)S(1)} collective-permute-done((f32[32,640]{1,0:T(8,128)S(1)}, f32[32,640]{1,0:T(8,128)S(1)}, u32[]{:S(2)}, u32[]{:S(2)}) %collective-permute-start.19) | collective-permute-done | bytes 81952 | tf_op jit(solution)/shard_map/ppermute | solution.py:30
  51.8 2.0 %collective-permute-done.17 = f32[32,640]{1,0:T(8,128)S(1)} collective-permute-done((f32[32,640]{1,0:T(8,128)S(1)}, f32[32,640]{1,0:T(8,128)S(1)}, u32[]{:S(2)}, u32[]{:S(2)}) %collective-permute-start.17) | collective-permute-done | bytes 81952 | tf_op jit(solution)/shard_map/ppermute | solution.py:30
  53.7 1.1 %collective-permute-done.18 = f32[32,640]{1,0:T(8,128)S(1)} collective-permute-done((f32[32,640]{1,0:T(8,128)S(1)}, f32[32,640]{1,0:T(8,128)S(1)}, u32[]{:S(2)}, u32[]{:S(2)}) %collective-permute-start.18) | collective-permute-done | bytes 81952 | tf_op jit(solution)/shard_map/ppermute | solution.py:30
  54.9 1.8 %collective-permute-start.22 = (f32[32,640]{1,0:T(8,128)S(1)}, f32[32,640]{1,0:T(8,128)S(1)}, u32[]{:S(2)}, u32[]{:S(2)}) collective-permute-start(f32[32,640]{1,0:T(8,128)S(1)} %add_add_fusion.refs_0_), channel_id=1, source_target_pairs={{0,18},{1,19},{2,16},{3,17},{4,22},{5,23},{6,20},{7,21},{8,26},{9,... | collective-permute-start | bytes 245768 | tf_op jit(solution)/shard_map/ppermute | solution.py:30
  56.7 1.8 %collective-permute-start.21 = (f32[32,640]{1,0:T(8,128)S(1)}, f32[32,640]{1,0:T(8,128)S(1)}, u32[]{:S(2)}, u32[]{:S(2)}) collective-permute-start(f32[32,640]{1,0:T(8,128)S(1)} %add_add_fusion.refs_0_), channel_id=1, source_target_pairs={{0,16},{1,17},{2,18},{3,19},{4,20},{5,21},{6,22},{7,23},{8,24},{9,... | collective-permute-start | bytes 245768 | tf_op jit(solution)/shard_map/ppermute | solution.py:30
  58.4 0.0 collective-permute-start.20
  58.5 2.2 %collective-permute-start.8 = (f32[128,256]{1,0:T(8,128)S(1)}, f32[128,256]{1,0:T(8,128)S(1)}, u32[]{:S(2)}, u32[]{:S(2)}) collective-permute-start(f32[128,256]{1,0:T(8,128)S(1)} %get-tuple-element.17), channel_id=1, source_target_pairs={{0,12},{1,13},{2,14},{3,15},{4,8},{5,9},{6,10},{7,11},{8,4},{9,5},... | collective-permute-start | bytes 393224 | tf_op jit(solution)/shard_map/ppermute | solution.py:30
  60.7 0.0 collective-permute-done.22.refs_3_
  60.7 2.2 %collective-permute-start.7 = (f32[128,256]{1,0:T(8,128)S(1)}, f32[128,256]{1,0:T(8,128)S(1)}, u32[]{:S(2)}, u32[]{:S(2)}) collective-permute-start(f32[128,256]{1,0:T(8,128)S(1)} %get-tuple-element.16), channel_id=1, source_target_pairs={{0,8},{1,9},{2,10},{3,11},{4,12},{5,13},{6,14},{7,15},{8,0},{9,1},... | collective-permute-start | bytes 393224 | tf_op jit(solution)/shard_map/ppermute | solution.py:30
  62.9 0.1 collective-permute-start.23
  63.0 3.6 %collective-permute-done.8 = f32[128,256]{1,0:T(8,128)S(1)} collective-permute-done((f32[128,256]{1,0:T(8,128)S(1)}, f32[128,256]{1,0:T(8,128)S(1)}, u32[]{:S(2)}, u32[]{:S(2)}) %collective-permute-start.8) | collective-permute-done | bytes 131104 | tf_op jit(solution)/shard_map/ppermute | solution.py:30
  66.6 0.9 %collective-permute-done.6 = f32[128,256]{1,0:T(8,128)S(1)} collective-permute-done((f32[128,256]{1,0:T(8,128)S(1)}, f32[128,256]{1,0:T(8,128)S(1)}, u32[]{:S(2)}, u32[]{:S(2)}) %collective-permute-start.6) | collective-permute-done | bytes 131104 | tf_op jit(solution)/shard_map/ppermute | solution.py:30
  67.5 4.2 %collective-permute-done.7 = f32[128,256]{1,0:T(8,128)S(1)} collective-permute-done((f32[128,256]{1,0:T(8,128)S(1)}, f32[128,256]{1,0:T(8,128)S(1)}, u32[]{:S(2)}, u32[]{:S(2)}) %collective-permute-start.7) | collective-permute-done | bytes 131104 | tf_op jit(solution)/shard_map/ppermute | solution.py:30
  71.7 0.7 fusion
  72.4 1.0 %shard_map.73 = f32[512,256]{1,0:T(8,128)} custom-call(f32[512,256]{1,0:T(8,128)S(1)} %copy-done, f32[128,256]{1,0:T(8,128)S(1)} %collective-permute-done.23.other_ref, f32[32,640]{1,0:T(8,128)S(1)} %add_add_fusion.refs_0_, f32[32,640]{1,0:T(8,128)S(1)} %collective-permute-done.20.refs_1_, f32[32,640]{1,0:T(8,128)S(1)} %collective-permute-done.21.refs_2_, ...), custom_call_target="tpu_custom_call" | custom-call | bytes 1507328 | tf_op jit(solution)/shard_map/pallas_call | solution.py:212
  (19 shorter events, 0.1 us)
Async XLA Ops:
  0.6 0.7 copy-start.1
  3.2 11.4 %collective-permute-start = (f32[2,128,256]{2,1,0:T(8,128)S(1)}, f32[2,128,256]{2,1,0:T(8,128)S(1)}, u32[]{:S(2)}, u32[]{:S(2)}) collective-permute-start(f32[2,128,256]{2,1,0:T(8,128)S(1)} %get-tuple-element.13), channel_id=1, source_target_pairs={{0,2},{1,3},{2,0},{3,1},{4,6},{5,7},{6,4},{7,5},{8,10},{9,11},{10,... | collective-permute-start | bytes 786440 | tf_op jit(solution)/shard_map/ppermute | solution.py:30
  7.9 6.6 %collective-permute-start.2 = (f32[128,256]{1,0:T(8,128)S(1)}, f32[128,256]{1,0:T(8,128)S(1)}, u32[]{:S(2)}, u32[]{:S(2)}) collective-permute-start(f32[128,256]{1,0:T(8,128)S(1)} %shard_map.69.refs_0_), channel_id=1, source_target_pairs={{0,0},{1,1},{2,16},{3,17},{4,2},{5,3},{6,18},{7,19},{8,4},{9,5},{1... | collective-permute-start | bytes 393224 | tf_op jit(solution)/shard_map/ppermute | solution.py:30
  14.6 14.3 %collective-permute-start.1 = (f32[2,128,256]{2,1,0:T(8,128)S(1)}, f32[2,128,256]{2,1,0:T(8,128)S(1)}, u32[]{:S(2)}, u32[]{:S(2)}) collective-permute-start(f32[2,128,256]{2,1,0:T(8,128)S(1)} %collective-permute-done.mine_ref), channel_id=1, source_target_pairs={{0,1},{1,0},{2,3},{3,2},{4,5},{5,4},{6,7},{7,6},{8,9},{9,8},{10,11... | collective-permute-start | bytes 786440 | tf_op jit(solution)/shard_map/ppermute | solution.py:30
  14.6 8.5 %collective-permute-start.3 = (f32[128,256]{1,0:T(8,128)S(1)}, f32[128,256]{1,0:T(8,128)S(1)}, u32[]{:S(2)}, u32[]{:S(2)}) collective-permute-start(f32[128,256]{1,0:T(8,128)S(1)} %collective-permute-done.2.refs_0_), channel_id=1, source_target_pairs={{0,16},{1,17},{2,18},{3,19},{4,20},{5,21},{6,22},{7,23},{8,24},{9,... | collective-permute-start | bytes 393224 | tf_op jit(solution)/shard_map/ppermute | solution.py:30
  17.2 8.2 %collective-permute-start.4 = (f32[128,256]{1,0:T(8,128)S(1)}, f32[128,256]{1,0:T(8,128)S(1)}, u32[]{:S(2)}, u32[]{:S(2)}) collective-permute-start(f32[128,256]{1,0:T(8,128)S(1)} %collective-permute-done.2.refs_0_), channel_id=1, source_target_pairs={{0,2},{1,3},{2,0},{3,1},{4,6},{5,7},{6,4},{7,5},{8,10},{9,11},{10,... | collective-permute-start | bytes 393224 | tf_op jit(solution)/shard_map/ppermute | solution.py:30
  17.9 10.9 %collective-permute-start.5 = (f32[128,256]{1,0:T(8,128)S(1)}, f32[128,256]{1,0:T(8,128)S(1)}, u32[]{:S(2)}, u32[]{:S(2)}) collective-permute-start(f32[128,256]{1,0:T(8,128)S(1)} %collective-permute-done.2.refs_0_), channel_id=1, source_target_pairs={{0,18},{1,19},{2,16},{3,17},{4,22},{5,23},{6,20},{7,21},{8,26},{9,... | collective-permute-start | bytes 393224 | tf_op jit(solution)/shard_map/ppermute | solution.py:30
  18.7 10.9 %collective-permute-start.12 = (f32[128,256]{1,0:T(8,128)S(1)}, f32[128,256]{1,0:T(8,128)S(1)}, u32[]{:S(2)}, u32[]{:S(2)}) collective-permute-start(f32[128,256]{1,0:T(8,128)S(1)} %shard_map.69.refs_0_), channel_id=1, source_target_pairs={{0,12},{1,13},{2,14},{3,15},{4,8},{5,9},{6,10},{7,11},{8,4},{9,5},... | collective-permute-start | bytes 393224 | tf_op jit(solution)/shard_map/ppermute | solution.py:30
  23.1 11.4 %collective-permute-start.11 = (f32[128,256]{1,0:T(8,128)S(1)}, f32[128,256]{1,0:T(8,128)S(1)}, u32[]{:S(2)}, u32[]{:S(2)}) collective-permute-start(f32[128,256]{1,0:T(8,128)S(1)} %shard_map.69.refs_0_), channel_id=1, source_target_pairs={{0,8},{1,9},{2,10},{3,11},{4,12},{5,13},{6,14},{7,15},{8,0},{9,1},... | collective-permute-start | bytes 393224 | tf_op jit(solution)/shard_map/ppermute | solution.py:30
  25.4 9.1 %collective-permute-start.10 = (f32[128,256]{1,0:T(8,128)S(1)}, f32[128,256]{1,0:T(8,128)S(1)}, u32[]{:S(2)}, u32[]{:S(2)}) collective-permute-start(f32[128,256]{1,0:T(8,128)S(1)} %shard_map.69.refs_0_), channel_id=1, source_target_pairs={{0,4},{1,5},{2,6},{3,7},{4,0},{5,1},{6,2},{7,3},{8,12},{9,13},{10,... | collective-permute-start | bytes 393224 | tf_op jit(solution)/shard_map/ppermute | solution.py:30
  29.5 6.9 %collective-permute-start.9 = (f32[4,128,256]{2,1,0:T(8,128)S(1)}, f32[4,128,256]{2,1,0:T(8,128)S(1)}, u32[]{:S(2)}, u32[]{:S(2)}) collective-permute-start(f32[4,128,256]{2,1,0:T(8,128)S(1)} %get-tuple-element.14.share_ref), channel_id=1, source_target_pairs={{0,1},{1,0},{2,3},{3,2},{4,5},{5,4},{6,7},{7,6},{8,9},{9,8},{10,11... | collective-permute-start | bytes 1572872 | tf_op jit(solution)/shard_map/ppermute | solution.py:30
  34.5 1.8 %collective-permute-start.13 = (f32[384,256]{1,0:T(8,128)S(1)}, f32[384,256]{1,0:T(8,128)S(1)}, u32[]{:S(2)}, u32[]{:S(2)}) collective-permute-start(f32[384,256]{1,0:T(8,128)S(1)} %pad_maximum_fusion), channel_id=1, source_target_pairs={{0,1},{1,0},{2,3},{3,2},{4,5},{5,4},{6,7},{7,6},{8,9},{9,8},{10,11... | collective-permute-start | bytes 1179656 | tf_op jit(solution)/shard_map/ppermute | solution.py:30
  37.3 5.8 %collective-permute-start.16 = (f32[32,640]{1,0:T(8,128)S(1)}, f32[32,640]{1,0:T(8,128)S(1)}, u32[]{:S(2)}, u32[]{:S(2)}) collective-permute-start(f32[32,640]{1,0:T(8,128)S(1)} %get-tuple-element.21), channel_id=1, source_target_pairs={{0,18},{1,19},{2,16},{3,17},{4,22},{5,23},{6,20},{7,21},{8,26},{9,... | collective-permute-start | bytes 245768 | tf_op jit(solution)/shard_map/ppermute | solution.py:30
  38.9 5.9 %collective-permute-start.14 = (f32[32,640]{1,0:T(8,128)S(1)}, f32[32,640]{1,0:T(8,128)S(1)}, u32[]{:S(2)}, u32[]{:S(2)}) collective-permute-start(f32[32,640]{1,0:T(8,128)S(1)} %get-tuple-element.19), channel_id=1, source_target_pairs={{0,2},{1,3},{2,0},{3,1},{4,6},{5,7},{6,4},{7,5},{8,10},{9,11},{10,... | collective-permute-start | bytes 245768 | tf_op jit(solution)/shard_map/ppermute | solution.py:30
  40.3 4.6 %collective-permute-start.15 = (f32[32,640]{1,0:T(8,128)S(1)}, f32[32,640]{1,0:T(8,128)S(1)}, u32[]{:S(2)}, u32[]{:S(2)}) collective-permute-start(f32[32,640]{1,0:T(8,128)S(1)} %get-tuple-element.20), channel_id=1, source_target_pairs={{0,16},{1,17},{2,18},{3,19},{4,20},{5,21},{6,22},{7,23},{8,24},{9,... | collective-permute-start | bytes 245768 | tf_op jit(solution)/shard_map/ppermute | solution.py:30
  44.9 6.9 %collective-permute-start.19 = (f32[32,640]{1,0:T(8,128)S(1)}, f32[32,640]{1,0:T(8,128)S(1)}, u32[]{:S(2)}, u32[]{:S(2)}) collective-permute-start(f32[32,640]{1,0:T(8,128)S(1)} %add_add_fusion.1), channel_id=1, source_target_pairs={{0,12},{1,13},{2,14},{3,15},{4,8},{5,9},{6,10},{7,11},{8,4},{9,5},... | collective-permute-start | bytes 245768 | tf_op jit(solution)/shard_map/ppermute | solution.py:30
  47.6 6.1 %collective-permute-start.17 = (f32[32,640]{1,0:T(8,128)S(1)}, f32[32,640]{1,0:T(8,128)S(1)}, u32[]{:S(2)}, u32[]{:S(2)}) collective-permute-start(f32[32,640]{1,0:T(8,128)S(1)} %add_add_fusion.1), channel_id=1, source_target_pairs={{0,4},{1,5},{2,6},{3,7},{4,0},{5,1},{6,2},{7,3},{8,12},{9,13},{10,... | collective-permute-start | bytes 245768 | tf_op jit(solution)/shard_map/ppermute | solution.py:30
  47.6 7.3 %collective-permute-start.18 = (f32[32,640]{1,0:T(8,128)S(1)}, f32[32,640]{1,0:T(8,128)S(1)}, u32[]{:S(2)}, u32[]{:S(2)}) collective-permute-start(f32[32,640]{1,0:T(8,128)S(1)} %add_add_fusion.1), channel_id=1, source_target_pairs={{0,8},{1,9},{2,10},{3,11},{4,12},{5,13},{6,14},{7,15},{8,0},{9,1},... | collective-permute-start | bytes 245768 | tf_op jit(solution)/shard_map/ppermute | solution.py:30
  54.9 5.8 %collective-permute-start.22 = (f32[32,640]{1,0:T(8,128)S(1)}, f32[32,640]{1,0:T(8,128)S(1)}, u32[]{:S(2)}, u32[]{:S(2)}) collective-permute-start(f32[32,640]{1,0:T(8,128)S(1)} %add_add_fusion.refs_0_), channel_id=1, source_target_pairs={{0,18},{1,19},{2,16},{3,17},{4,22},{5,23},{6,20},{7,21},{8,26},{9,... | collective-permute-start | bytes 245768 | tf_op jit(solution)/shard_map/ppermute | solution.py:30
  56.7 6.2 %collective-permute-start.21 = (f32[32,640]{1,0:T(8,128)S(1)}, f32[32,640]{1,0:T(8,128)S(1)}, u32[]{:S(2)}, u32[]{:S(2)}) collective-permute-start(f32[32,640]{1,0:T(8,128)S(1)} %add_add_fusion.refs_0_), channel_id=1, source_target_pairs={{0,16},{1,17},{2,18},{3,19},{4,20},{5,21},{6,22},{7,23},{8,24},{9,... | collective-permute-start | bytes 245768 | tf_op jit(solution)/shard_map/ppermute | solution.py:30
  58.4 4.4 %collective-permute-start.20 = (f32[32,640]{1,0:T(8,128)S(1)}, f32[32,640]{1,0:T(8,128)S(1)}, u32[]{:S(2)}, u32[]{:S(2)}) collective-permute-start(f32[32,640]{1,0:T(8,128)S(1)} %add_add_fusion.refs_0_), channel_id=1, source_target_pairs={{0,2},{1,3},{2,0},{3,1},{4,6},{5,7},{6,4},{7,5},{8,10},{9,11},{10,... | collective-permute-start | bytes 245768 | tf_op jit(solution)/shard_map/ppermute | solution.py:30
  58.5 8.2 %collective-permute-start.8 = (f32[128,256]{1,0:T(8,128)S(1)}, f32[128,256]{1,0:T(8,128)S(1)}, u32[]{:S(2)}, u32[]{:S(2)}) collective-permute-start(f32[128,256]{1,0:T(8,128)S(1)} %get-tuple-element.17), channel_id=1, source_target_pairs={{0,12},{1,13},{2,14},{3,15},{4,8},{5,9},{6,10},{7,11},{8,4},{9,5},... | collective-permute-start | bytes 393224 | tf_op jit(solution)/shard_map/ppermute | solution.py:30
  60.7 6.9 %collective-permute-start.6 = (f32[128,256]{1,0:T(8,128)S(1)}, f32[128,256]{1,0:T(8,128)S(1)}, u32[]{:S(2)}, u32[]{:S(2)}) collective-permute-start(f32[128,256]{1,0:T(8,128)S(1)} %get-tuple-element.15), channel_id=1, source_target_pairs={{0,4},{1,5},{2,6},{3,7},{4,0},{5,1},{6,2},{7,3},{8,12},{9,13},{10,... | collective-permute-start | bytes 393224 | tf_op jit(solution)/shard_map/ppermute | solution.py:30
  60.7 11.0 %collective-permute-start.7 = (f32[128,256]{1,0:T(8,128)S(1)}, f32[128,256]{1,0:T(8,128)S(1)}, u32[]{:S(2)}, u32[]{:S(2)}) collective-permute-start(f32[128,256]{1,0:T(8,128)S(1)} %get-tuple-element.16), channel_id=1, source_target_pairs={{0,8},{1,9},{2,10},{3,11},{4,12},{5,13},{6,14},{7,15},{8,0},{9,1},... | collective-permute-start | bytes 393224 | tf_op jit(solution)/shard_map/ppermute | solution.py:30
  62.9 9.6 %copy-start = (f32[512,256]{1,0:T(8,128)S(1)}, f32[512,256]{1,0:T(8,128)}, u32[]{:S(2)}) copy-start(f32[512,256]{1,0:T(8,128)} %pivot_ref.1) | copy-start | bytes 1572868
  62.9 9.5 %collective-permute-start.23 = (f32[128,256]{1,0:T(8,128)S(1)}, f32[128,256]{1,0:T(8,128)S(1)}, u32[]{:S(2)}, u32[]{:S(2)}) collective-permute-start(f32[128,256]{1,0:T(8,128)S(1)} %pad_maximum_fusion.1), channel_id=1, source_target_pairs={{0,1},{1,0},{2,3},{3,2},{4,5},{5,4},{6,7},{7,6},{8,9},{9,8},{10,11... | collective-permute-start | bytes 393224 | tf_op jit(solution)/shard_map/ppermute | solution.py:30

commit v5 on v4

--- a/solution.py
+++ b/solution.py
@@ -125,8 +125,8 @@
         left = jnp.concatenate([kept_ref[k], taken], 1)
         share = split_dot(split(left), right)
         outs[0][k] = share
-        if k:
-            outs[k][...] = share
+        if k % PAIR:
+            outs[1][k // PAIR] = share
 
 
 def coupling_kernel(members, planes, share_ref, other_ref, gathered_ref, *refs):
@@ -274,16 +274,18 @@
     other_strip = swap_core(packed)
     mine = send(given, lambda r, c, p: (r, c ^ 1, p))
     theirs = swap_core(mine)
-    product, *shares = call(
+    product, given_shares = call(
         functools.partial(product_kernel, planes, members),
-        [(planes, tile, half)] + [(tile, half)] * (planes - 1),
+        [(planes, tile, half), (planes // PAIR, tile, half)],
         "",
         [kept, mine, theirs, *arrived],
         flops=12 * planes * tile * depth * half,
     )
     other_product = swap_core(product)
-    landed = [send(shares[k - 1], along(k)) for k in range(1, planes)]
-    ancestor_columns = -(product[0] + sum(landed))
+    taken_shares = send(given_shares, along(1))
+    halved = [product[k] + taken_shares[k // PAIR] for k in range(0, planes, PAIR)]
+    landed = [send(halved[k], along(k * PAIR)) for k in range(1, planes // PAIR)]
+    ancestor_columns = -(halved[0] + sum(landed))
 
     quarter = half // 2
     step, width = quarter // members, 5 * quarter

time: 73.6 us -> 70.3 us (0.955)
  starting transfers between devices: 34.2 us -> 31.3 us
    ppermute x24 -> x23, starting transfers between devices: 34.2 us -> 31.3 us  [send(): return lax.ppermute(block, AXES, route)]
    ppermute x24 -> x23, waiting for transfers between devices: 29 us -> 28.7 us  [send(): return lax.ppermute(block, AXES, route)]
  transfers between devices with their start and end apart: 24 -> 23, of which waited for: 10 -> 10; matrix products, arithmetic and copies ran while one was open for 1% -> 1% of each run, Pallas kernels for 6% -> 6%
where the time goes in v5:
time: 70.3 us; the launch traced here: 70.1 us
  starting transfers between devices  31.3 us (45%)
  waiting for transfers between devices  28.7 us (41%)
  Pallas kernels  7.89 us (11%)
  between operations  0.78 us (1%)
  other arithmetic  0.77 us (1%)
    ppermute x23, starting transfers between devices, send(): return lax.ppermute(block, AXES, route)  31.3 us
    ppermute x23, waiting for transfers between devices, send(): return lax.ppermute(block, AXES, route)  28.7 us
    pallas_call x6, Pallas kernels, call(): pl.pallas_call(kernel, out_shape=[jax.ShapeDtypeStruct(shape, F32) for sh...  7.89 us
  transfers between devices with their start and end apart: 23, of which 10 were waited for; matrix products, arithmetic and copies ran while one was open for 1% of the time, Pallas kernels for 6%

profile of v5, /device:TPU:0, one launch (start us, length us, event | category | flops | bytes accessed | tf_op | source)
XLA Modules:
  0.0 70.1 jit_solution(1481050676747073466)
XLA Ops:
  0.6 0.7 copy-done.1
  1.3 1.9 %shard_map.68 = (f32[4,128,256]{2,1,0:T(8,128)S(1)}, f32[2,128,256]{2,1,0:T(8,128)S(1)}) custom-call(s32[2,8]{1,0:T(2,128)S(1)} %bitcast.9, f32[1024,256]{1,0:T(8,128)} %full_ref.1), custom_call_target="tpu_custom_call" | custom-call | bytes 1835072 | tf_op jit(solution)/shard_map/pallas_call | solution.py:212
  3.2 3.0 %collective-permute-start = (f32[2,128,256]{2,1,0:T(8,128)S(1)}, f32[2,128,256]{2,1,0:T(8,128)S(1)}, u32[]{:S(2)}, u32[]{:S(2)}) collective-permute-start(f32[2,128,256]{2,1,0:T(8,128)S(1)} %get-tuple-element.11), channel_id=1, source_target_pairs={{0,2},{1,3},{2,0},{3,1},{4,6},{5,7},{6,4},{7,5},{8,10},{9,11},{10,... | collective-permute-start | bytes 786440 | tf_op jit(solution)/shard_map/ppermute | solution.py:30
  6.2 1.7 %shard_map.69.refs_0_ = f32[128,256]{1,0:T(8,128)S(1)} custom-call(f32[128,512]{1,0:T(8,128)} %factor_ref.3, f32[512,512]{1,0:T(8,128)} %normalizer_ref.3), custom_call_target="tpu_custom_call" | custom-call | bytes 1441792 | tf_op jit(solution)/shard_map/pallas_call | solution.py:212
  7.9 0.7 collective-permute-start.2
  8.6 6.0 %collective-permute-done.mine_ref = f32[2,128,256]{2,1,0:T(8,128)S(1)} collective-permute-done((f32[2,128,256]{2,1,0:T(8,128)S(1)}, f32[2,128,256]{2,1,0:T(8,128)S(1)}, u32[]{:S(2)}, u32[]{:S(2)}) %collective-permute-start) | collective-permute-done | bytes 262176 | tf_op jit(solution)/shard_map/ppermute | solution.py:30
  14.6 0.0 collective-permute-start.1
  14.6 0.0 collective-permute-done.2.refs_0_
  14.6 2.6 %collective-permute-start.3 = (f32[128,256]{1,0:T(8,128)S(1)}, f32[128,256]{1,0:T(8,128)S(1)}, u32[]{:S(2)}, u32[]{:S(2)}) collective-permute-start(f32[128,256]{1,0:T(8,128)S(1)} %collective-permute-done.2.refs_0_), channel_id=1, source_target_pairs={{0,16},{1,17},{2,18},{3,19},{4,20},{5,21},{6,22},{7,23},{8,24},{9,... | collective-permute-start | bytes 393224 | tf_op jit(solution)/shard_map/ppermute | solution.py:30
  17.2 0.7 %collective-permute-start.4 = (f32[128,256]{1,0:T(8,128)S(1)}, f32[128,256]{1,0:T(8,128)S(1)}, u32[]{:S(2)}, u32[]{:S(2)}) collective-permute-start(f32[128,256]{1,0:T(8,128)S(1)} %collective-permute-done.2.refs_0_), channel_id=1, source_target_pairs={{0,2},{1,3},{2,0},{3,1},{4,6},{5,7},{6,4},{7,5},{8,10},{9,11},{10,... | collective-permute-start | bytes 393224 | tf_op jit(solution)/shard_map/ppermute | solution.py:30
  17.9 0.8 %collective-permute-start.5 = (f32[128,256]{1,0:T(8,128)S(1)}, f32[128,256]{1,0:T(8,128)S(1)}, u32[]{:S(2)}, u32[]{:S(2)}) collective-permute-start(f32[128,256]{1,0:T(8,128)S(1)} %collective-permute-done.2.refs_0_), channel_id=1, source_target_pairs={{0,18},{1,19},{2,16},{3,17},{4,22},{5,23},{6,20},{7,21},{8,26},{9,... | collective-permute-start | bytes 393224 | tf_op jit(solution)/shard_map/ppermute | solution.py:30
  18.7 4.4 %collective-permute-start.11 = (f32[128,256]{1,0:T(8,128)S(1)}, f32[128,256]{1,0:T(8,128)S(1)}, u32[]{:S(2)}, u32[]{:S(2)}) collective-permute-start(f32[128,256]{1,0:T(8,128)S(1)} %shard_map.69.refs_0_), channel_id=1, source_target_pairs={{0,12},{1,13},{2,14},{3,15},{4,8},{5,9},{6,10},{7,11},{8,4},{9,5},... | collective-permute-start | bytes 393224 | tf_op jit(solution)/shard_map/ppermute | solution.py:30
  23.1 2.3 %collective-permute-start.10 = (f32[128,256]{1,0:T(8,128)S(1)}, f32[128,256]{1,0:T(8,128)S(1)}, u32[]{:S(2)}, u32[]{:S(2)}) collective-permute-start(f32[128,256]{1,0:T(8,128)S(1)} %shard_map.69.refs_0_), channel_id=1, source_target_pairs={{0,8},{1,9},{2,10},{3,11},{4,12},{5,13},{6,14},{7,15},{8,0},{9,1},... | collective-permute-start | bytes 393224 | tf_op jit(solution)/shard_map/ppermute | solution.py:30
  25.4 0.0 collective-permute-done.4.refs_2_
  25.4 3.4 %collective-permute-start.9 = (f32[128,256]{1,0:T(8,128)S(1)}, f32[128,256]{1,0:T(8,128)S(1)}, u32[]{:S(2)}, u32[]{:S(2)}) collective-permute-start(f32[128,256]{1,0:T(8,128)S(1)} %shard_map.69.refs_0_), channel_id=1, source_target_pairs={{0,4},{1,5},{2,6},{3,7},{4,0},{5,1},{6,2},{7,3},{8,12},{9,13},{10,... | collective-permute-start | bytes 393224 | tf_op jit(solution)/shard_map/ppermute | solution.py:30
  28.8 0.0 collective-permute-done.5.refs_3_
  28.8 0.0 collective-permute-done.1.theirs_ref
  28.8 0.6 shard_map.70
  29.5 0.1 collective-permute-start.8
  29.6 0.0 collective-permute-done.11.refs_3_
  29.6 4.9 %collective-permute-done.10.refs_2_ = f32[128,256]{1,0:T(8,128)S(1)} collective-permute-done((f32[128,256]{1,0:T(8,128)S(1)}, f32[128,256]{1,0:T(8,128)S(1)}, u32[]{:S(2)}, u32[]{:S(2)}) %collective-permute-start.10) | collective-permute-done | bytes 131104 | tf_op jit(solution)/shard_map/ppermute | solution.py:30
  34.5 0.0 collective-permute-done.9.refs_1_
  34.5 0.1 collective-permute-start.12
  34.6 1.7 %shard_map.71.refs_4_ = f32[128,256]{1,0:T(8,128)S(1)} custom-call(f32[128,512]{1,0:T(8,128)} %factor_ref.3, f32[512,512]{1,0:T(8,128)} %normalizer_ref.3), custom_call_target="tpu_custom_call" | custom-call | bytes 1441792 | tf_op jit(solution)/shard_map/pallas_call | solution.py:212
  36.3 0.9 %shard_map.72 = (f32[32,640]{1,0:T(8,128)S(1)}, f32[32,640]{1,0:T(8,128)S(1)}, f32[32,640]{1,0:T(8,128)S(1)}, f32[32,640]{1,0:T(8,128)S(1)}) custom-call(f32[4,128,256]{2,1,0:T(8,128)S(1)} %get-tuple-element.12.share_ref, f32[4,128,256]{2,1,0:T(8,128)S(1)} %collective-permute-done.8.other_ref, f32[384,256]{1,0:T(8,128)S(1)} %collective-permute-done.12.gathered_ref, ...), custom_call_target="tpu_custom_call" | custom-call | flops 402653184 | bytes 2424832 | tf_op jit(solution)/shard_map/pallas_call | solution.py:212
  37.3 1.7 %collective-permute-start.15 = (f32[32,640]{1,0:T(8,128)S(1)}, f32[32,640]{1,0:T(8,128)S(1)}, u32[]{:S(2)}, u32[]{:S(2)}) collective-permute-start(f32[32,640]{1,0:T(8,128)S(1)} %get-tuple-element.17), channel_id=1, source_target_pairs={{0,18},{1,19},{2,16},{3,17},{4,22},{5,23},{6,20},{7,21},{8,26},{9,... | collective-permute-start | bytes 245768 | tf_op jit(solution)/shard_map/ppermute | solution.py:30
  38.9 1.3 %collective-permute-start.13 = (f32[32,640]{1,0:T(8,128)S(1)}, f32[32,640]{1,0:T(8,128)S(1)}, u32[]{:S(2)}, u32[]{:S(2)}) collective-permute-start(f32[32,640]{1,0:T(8,128)S(1)} %get-tuple-element.15), channel_id=1, source_target_pairs={{0,2},{1,3},{2,0},{3,1},{4,6},{5,7},{6,4},{7,5},{8,10},{9,11},{10,... | collective-permute-start | bytes 245768 | tf_op jit(solution)/shard_map/ppermute | solution.py:30
  40.3 0.7 collective-permute-start.14
  41.0 2.2 %collective-permute-done.15 = f32[32,640]{1,0:T(8,128)S(1)} collective-permute-done((f32[32,640]{1,0:T(8,128)S(1)}, f32[32,640]{1,0:T(8,128)S(1)}, u32[]{:S(2)}, u32[]{:S(2)}) %collective-permute-start.15) | collective-permute-done | bytes 81952 | tf_op jit(solution)/shard_map/ppermute | solution.py:30
  43.1 1.7 %collective-permute-done.13 = f32[32,640]{1,0:T(8,128)S(1)} collective-permute-done((f32[32,640]{1,0:T(8,128)S(1)}, f32[32,640]{1,0:T(8,128)S(1)}, u32[]{:S(2)}, u32[]{:S(2)}) %collective-permute-start.13) | collective-permute-done | bytes 81952 | tf_op jit(solution)/shard_map/ppermute | solution.py:30
  44.8 0.0 collective-permute-done.14
  44.9 2.7 %collective-permute-start.18 = (f32[32,640]{1,0:T(8,128)S(1)}, f32[32,640]{1,0:T(8,128)S(1)}, u32[]{:S(2)}, u32[]{:S(2)}) collective-permute-start(f32[32,640]{1,0:T(8,128)S(1)} %add_add_fusion.1), channel_id=1, source_target_pairs={{0,12},{1,13},{2,14},{3,15},{4,8},{5,9},{6,10},{7,11},{8,4},{9,5},... | collective-permute-start | bytes 245768 | tf_op jit(solution)/shard_map/ppermute | solution.py:30
  47.6 1.7 %collective-permute-start.17 = (f32[32,640]{1,0:T(8,128)S(1)}, f32[32,640]{1,0:T(8,128)S(1)}, u32[]{:S(2)}, u32[]{:S(2)}) collective-permute-start(f32[32,640]{1,0:T(8,128)S(1)} %add_add_fusion.1), channel_id=1, source_target_pairs={{0,8},{1,9},{2,10},{3,11},{4,12},{5,13},{6,14},{7,15},{8,0},{9,1},... | collective-permute-start | bytes 245768 | tf_op jit(solution)/shard_map/ppermute | solution.py:30
  49.3 0.3 collective-permute-start.6
  49.6 2.1 %collective-permute-done.18 = f32[32,640]{1,0:T(8,128)S(1)} collective-permute-done((f32[32,640]{1,0:T(8,128)S(1)}, f32[32,640]{1,0:T(8,128)S(1)}, u32[]{:S(2)}, u32[]{:S(2)}) %collective-permute-start.18) | collective-permute-done | bytes 81952 | tf_op jit(solution)/shard_map/ppermute | solution.py:30
  51.8 3.1 %collective-permute-done.16 = f32[32,640]{1,0:T(8,128)S(1)} collective-permute-done((f32[32,640]{1,0:T(8,128)S(1)}, f32[32,640]{1,0:T(8,128)S(1)}, u32[]{:S(2)}, u32[]{:S(2)}) %collective-permute-start.16) | collective-permute-done | bytes 81952 | tf_op jit(solution)/shard_map/ppermute | solution.py:30
  55.0 1.7 %collective-permute-start.21 = (f32[32,640]{1,0:T(8,128)S(1)}, f32[32,640]{1,0:T(8,128)S(1)}, u32[]{:S(2)}, u32[]{:S(2)}) collective-permute-start(f32[32,640]{1,0:T(8,128)S(1)} %add_add_fusion.refs_0_), channel_id=1, source_target_pairs={{0,18},{1,19},{2,16},{3,17},{4,22},{5,23},{6,20},{7,21},{8,26},{9,... | collective-permute-start | bytes 245768 | tf_op jit(solution)/shard_map/ppermute | solution.py:30
  56.7 1.8 %collective-permute-start.20 = (f32[32,640]{1,0:T(8,128)S(1)}, f32[32,640]{1,0:T(8,128)S(1)}, u32[]{:S(2)}, u32[]{:S(2)}) collective-permute-start(f32[32,640]{1,0:T(8,128)S(1)} %add_add_fusion.refs_0_), channel_id=1, source_target_pairs={{0,16},{1,17},{2,18},{3,19},{4,20},{5,21},{6,22},{7,23},{8,24},{9,... | collective-permute-start | bytes 245768 | tf_op jit(solution)/shard_map/ppermute | solution.py:30
  58.4 0.1 collective-permute-start.19
  58.5 1.3 %collective-permute-done.6 = f32[2,128,256]{2,1,0:T(8,128)S(1)} collective-permute-done((f32[2,128,256]{2,1,0:T(8,128)S(1)}, f32[2,128,256]{2,1,0:T(8,128)S(1)}, u32[]{:S(2)}, u32[]{:S(2)}) %collective-permute-start.6) | collective-permute-done | bytes 262176 | tf_op jit(solution)/shard_map/ppermute | solution.py:30
  59.8 0.0 copy-start
  59.9 1.1 %collective-permute-start.7 = (f32[128,256]{1,0:T(8,128)S(1)}, f32[128,256]{1,0:T(8,128)S(1)}, u32[]{:S(2)}, u32[]{:S(2)}) collective-permute-start(f32[128,256]{1,0:T(8,128)S(1)} %fusion), channel_id=1, source_target_pairs={{0,8},{1,9},{2,10},{3,11},{4,12},{5,13},{6,14},{7,15},{8,0},{9,1},... | collective-permute-start | bytes 393224 | tf_op jit(solution)/shard_map/ppermute | solution.py:30
  61.0 0.5 collective-permute-done.20.refs_2_
  61.5 1.4 %collective-permute-done.19.refs_1_ = f32[32,640]{1,0:T(8,128)S(1)} collective-permute-done((f32[32,640]{1,0:T(8,128)S(1)}, f32[32,640]{1,0:T(8,128)S(1)}, u32[]{:S(2)}, u32[]{:S(2)}) %collective-permute-start.19) | collective-permute-done | bytes 81952 | tf_op jit(solution)/shard_map/ppermute | solution.py:30
  62.9 0.1 collective-permute-start.22
  63.0 5.5 %collective-permute-done.7 = f32[128,256]{1,0:T(8,128)S(1)} collective-permute-done((f32[128,256]{1,0:T(8,128)S(1)}, f32[128,256]{1,0:T(8,128)S(1)}, u32[]{:S(2)}, u32[]{:S(2)}) %collective-permute-start.7) | collective-permute-done | bytes 131104 | tf_op jit(solution)/shard_map/ppermute | solution.py:30
  68.4 0.7 fusion.3
  69.1 1.0 %shard_map.73 = f32[512,256]{1,0:T(8,128)} custom-call(f32[512,256]{1,0:T(8,128)S(1)} %copy-done, f32[128,256]{1,0:T(8,128)S(1)} %collective-permute-done.22.other_ref, f32[32,640]{1,0:T(8,128)S(1)} %add_add_fusion.refs_0_, f32[32,640]{1,0:T(8,128)S(1)} %collective-permute-done.19.refs_1_, f32[32,640]{1,0:T(8,128)S(1)} %collective-permute-done.20.refs_2_, ...), custom_call_target="tpu_custom_call" | custom-call | bytes 1507328 | tf_op jit(solution)/shard_map/pallas_call | solution.py:212
  (18 shorter events, 0.1 us)
Async XLA Ops:
  0.6 0.7 copy-start.1
  3.2 11.4 %collective-permute-start = (f32[2,128,256]{2,1,0:T(8,128)S(1)}, f32[2,128,256]{2,1,0:T(8,128)S(1)}, u32[]{:S(2)}, u32[]{:S(2)}) collective-permute-start(f32[2,128,256]{2,1,0:T(8,128)S(1)} %get-tuple-element.11), channel_id=1, source_target_pairs={{0,2},{1,3},{2,0},{3,1},{4,6},{5,7},{6,4},{7,5},{8,10},{9,11},{10,... | collective-permute-start | bytes 786440 | tf_op jit(solution)/shard_map/ppermute | solution.py:30
  7.9 6.6 %collective-permute-start.2 = (f32[128,256]{1,0:T(8,128)S(1)}, f32[128,256]{1,0:T(8,128)S(1)}, u32[]{:S(2)}, u32[]{:S(2)}) collective-permute-start(f32[128,256]{1,0:T(8,128)S(1)} %shard_map.69.refs_0_), channel_id=1, source_target_pairs={{0,0},{1,1},{2,16},{3,17},{4,2},{5,3},{6,18},{7,19},{8,4},{9,5},{1... | collective-permute-start | bytes 393224 | tf_op jit(solution)/shard_map/ppermute | solution.py:30
  14.6 14.3 %collective-permute-start.1 = (f32[2,128,256]{2,1,0:T(8,128)S(1)}, f32[2,128,256]{2,1,0:T(8,128)S(1)}, u32[]{:S(2)}, u32[]{:S(2)}) collective-permute-start(f32[2,128,256]{2,1,0:T(8,128)S(1)} %collective-permute-done.mine_ref), channel_id=1, source_target_pairs={{0,1},{1,0},{2,3},{3,2},{4,5},{5,4},{6,7},{7,6},{8,9},{9,8},{10,11... | collective-permute-start | bytes 786440 | tf_op jit(solution)/shard_map/ppermute | solution.py:30
  14.6 8.5 %collective-permute-start.3 = (f32[128,256]{1,0:T(8,128)S(1)}, f32[128,256]{1,0:T(8,128)S(1)}, u32[]{:S(2)}, u32[]{:S(2)}) collective-permute-start(f32[128,256]{1,0:T(8,128)S(1)} %collective-permute-done.2.refs_0_), channel_id=1, source_target_pairs={{0,16},{1,17},{2,18},{3,19},{4,20},{5,21},{6,22},{7,23},{8,24},{9,... | collective-permute-start | bytes 393224 | tf_op jit(solution)/shard_map/ppermute | solution.py:30
  17.2 8.2 %collective-permute-start.4 = (f32[128,256]{1,0:T(8,128)S(1)}, f32[128,256]{1,0:T(8,128)S(1)}, u32[]{:S(2)}, u32[]{:S(2)}) collective-permute-start(f32[128,256]{1,0:T(8,128)S(1)} %collective-permute-done.2.refs_0_), channel_id=1, source_target_pairs={{0,2},{1,3},{2,0},{3,1},{4,6},{5,7},{6,4},{7,5},{8,10},{9,11},{10,... | collective-permute-start | bytes 393224 | tf_op jit(solution)/shard_map/ppermute | solution.py:30
  17.9 10.9 %collective-permute-start.5 = (f32[128,256]{1,0:T(8,128)S(1)}, f32[128,256]{1,0:T(8,128)S(1)}, u32[]{:S(2)}, u32[]{:S(2)}) collective-permute-start(f32[128,256]{1,0:T(8,128)S(1)} %collective-permute-done.2.refs_0_), channel_id=1, source_target_pairs={{0,18},{1,19},{2,16},{3,17},{4,22},{5,23},{6,20},{7,21},{8,26},{9,... | collective-permute-start | bytes 393224 | tf_op jit(solution)/shard_map/ppermute | solution.py:30
  18.7 10.9 %collective-permute-start.11 = (f32[128,256]{1,0:T(8,128)S(1)}, f32[128,256]{1,0:T(8,128)S(1)}, u32[]{:S(2)}, u32[]{:S(2)}) collective-permute-start(f32[128,256]{1,0:T(8,128)S(1)} %shard_map.69.refs_0_), channel_id=1, source_target_pairs={{0,12},{1,13},{2,14},{3,15},{4,8},{5,9},{6,10},{7,11},{8,4},{9,5},... | collective-permute-start | bytes 393224 | tf_op jit(solution)/shard_map/ppermute | solution.py:30
  23.1 11.4 %collective-permute-start.10 = (f32[128,256]{1,0:T(8,128)S(1)}, f32[128,256]{1,0:T(8,128)S(1)}, u32[]{:S(2)}, u32[]{:S(2)}) collective-permute-start(f32[128,256]{1,0:T(8,128)S(1)} %shard_map.69.refs_0_), channel_id=1, source_target_pairs={{0,8},{1,9},{2,10},{3,11},{4,12},{5,13},{6,14},{7,15},{8,0},{9,1},... | collective-permute-start | bytes 393224 | tf_op jit(solution)/shard_map/ppermute | solution.py:30
  25.4 9.1 %collective-permute-start.9 = (f32[128,256]{1,0:T(8,128)S(1)}, f32[128,256]{1,0:T(8,128)S(1)}, u32[]{:S(2)}, u32[]{:S(2)}) collective-permute-start(f32[128,256]{1,0:T(8,128)S(1)} %shard_map.69.refs_0_), channel_id=1, source_target_pairs={{0,4},{1,5},{2,6},{3,7},{4,0},{5,1},{6,2},{7,3},{8,12},{9,13},{10,... | collective-permute-start | bytes 393224 | tf_op jit(solution)/shard_map/ppermute | solution.py:30
  29.5 6.9 %collective-permute-start.8 = (f32[4,128,256]{2,1,0:T(8,128)S(1)}, f32[4,128,256]{2,1,0:T(8,128)S(1)}, u32[]{:S(2)}, u32[]{:S(2)}) collective-permute-start(f32[4,128,256]{2,1,0:T(8,128)S(1)} %get-tuple-element.12.share_ref), channel_id=1, source_target_pairs={{0,1},{1,0},{2,3},{3,2},{4,5},{5,4},{6,7},{7,6},{8,9},{9,8},{10,11... | collective-permute-start | bytes 1572872 | tf_op jit(solution)/shard_map/ppermute | solution.py:30
  34.5 1.8 %collective-permute-start.12 = (f32[384,256]{1,0:T(8,128)S(1)}, f32[384,256]{1,0:T(8,128)S(1)}, u32[]{:S(2)}, u32[]{:S(2)}) collective-permute-start(f32[384,256]{1,0:T(8,128)S(1)} %pad_maximum_fusion), channel_id=1, source_target_pairs={{0,1},{1,0},{2,3},{3,2},{4,5},{5,4},{6,7},{7,6},{8,9},{9,8},{10,11... | collective-permute-start | bytes 1179656 | tf_op jit(solution)/shard_map/ppermute | solution.py:30
  37.3 5.8 %collective-permute-start.15 = (f32[32,640]{1,0:T(8,128)S(1)}, f32[32,640]{1,0:T(8,128)S(1)}, u32[]{:S(2)}, u32[]{:S(2)}) collective-permute-start(f32[32,640]{1,0:T(8,128)S(1)} %get-tuple-element.17), channel_id=1, source_target_pairs={{0,18},{1,19},{2,16},{3,17},{4,22},{5,23},{6,20},{7,21},{8,26},{9,... | collective-permute-start | bytes 245768 | tf_op jit(solution)/shard_map/ppermute | solution.py:30
  38.9 5.9 %collective-permute-start.13 = (f32[32,640]{1,0:T(8,128)S(1)}, f32[32,640]{1,0:T(8,128)S(1)}, u32[]{:S(2)}, u32[]{:S(2)}) collective-permute-start(f32[32,640]{1,0:T(8,128)S(1)} %get-tuple-element.15), channel_id=1, source_target_pairs={{0,2},{1,3},{2,0},{3,1},{4,6},{5,7},{6,4},{7,5},{8,10},{9,11},{10,... | collective-permute-start | bytes 245768 | tf_op jit(solution)/shard_map/ppermute | solution.py:30
  40.3 4.6 %collective-permute-start.14 = (f32[32,640]{1,0:T(8,128)S(1)}, f32[32,640]{1,0:T(8,128)S(1)}, u32[]{:S(2)}, u32[]{:S(2)}) collective-permute-start(f32[32,640]{1,0:T(8,128)S(1)} %get-tuple-element.16), channel_id=1, source_target_pairs={{0,16},{1,17},{2,18},{3,19},{4,20},{5,21},{6,22},{7,23},{8,24},{9,... | collective-permute-start | bytes 245768 | tf_op jit(solution)/shard_map/ppermute | solution.py:30
  44.9 6.9 %collective-permute-start.18 = (f32[32,640]{1,0:T(8,128)S(1)}, f32[32,640]{1,0:T(8,128)S(1)}, u32[]{:S(2)}, u32[]{:S(2)}) collective-permute-start(f32[32,640]{1,0:T(8,128)S(1)} %add_add_fusion.1), channel_id=1, source_target_pairs={{0,12},{1,13},{2,14},{3,15},{4,8},{5,9},{6,10},{7,11},{8,4},{9,5},... | collective-permute-start | bytes 245768 | tf_op jit(solution)/shard_map/ppermute | solution.py:30
  47.6 7.3 %collective-permute-start.16 = (f32[32,640]{1,0:T(8,128)S(1)}, f32[32,640]{1,0:T(8,128)S(1)}, u32[]{:S(2)}, u32[]{:S(2)}) collective-permute-start(f32[32,640]{1,0:T(8,128)S(1)} %add_add_fusion.1), channel_id=1, source_target_pairs={{0,4},{1,5},{2,6},{3,7},{4,0},{5,1},{6,2},{7,3},{8,12},{9,13},{10,... | collective-permute-start | bytes 245768 | tf_op jit(solution)/shard_map/ppermute | solution.py:30
  47.6 7.3 %collective-permute-start.17 = (f32[32,640]{1,0:T(8,128)S(1)}, f32[32,640]{1,0:T(8,128)S(1)}, u32[]{:S(2)}, u32[]{:S(2)}) collective-permute-start(f32[32,640]{1,0:T(8,128)S(1)} %add_add_fusion.1), channel_id=1, source_target_pairs={{0,8},{1,9},{2,10},{3,11},{4,12},{5,13},{6,14},{7,15},{8,0},{9,1},... | collective-permute-start | bytes 245768 | tf_op jit(solution)/shard_map/ppermute | solution.py:30
  49.3 10.5 %collective-permute-start.6 = (f32[2,128,256]{2,1,0:T(8,128)S(1)}, f32[2,128,256]{2,1,0:T(8,128)S(1)}, u32[]{:S(2)}, u32[]{:S(2)}) collective-permute-start(f32[2,128,256]{2,1,0:T(8,128)S(1)} %get-tuple-element.13), channel_id=1, source_target_pairs={{0,4},{1,5},{2,6},{3,7},{4,0},{5,1},{6,2},{7,3},{8,12},{9,13},{10,... | collective-permute-start | bytes 786440 | tf_op jit(solution)/shard_map/ppermute | solution.py:30
  55.0 6.1 %collective-permute-start.21 = (f32[32,640]{1,0:T(8,128)S(1)}, f32[32,640]{1,0:T(8,128)S(1)}, u32[]{:S(2)}, u32[]{:S(2)}) collective-permute-start(f32[32,640]{1,0:T(8,128)S(1)} %add_add_fusion.refs_0_), channel_id=1, source_target_pairs={{0,18},{1,19},{2,16},{3,17},{4,22},{5,23},{6,20},{7,21},{8,26},{9,... | collective-permute-start | bytes 245768 | tf_op jit(solution)/shard_map/ppermute | solution.py:30
  56.7 4.8 %collective-permute-start.20 = (f32[32,640]{1,0:T(8,128)S(1)}, f32[32,640]{1,0:T(8,128)S(1)}, u32[]{:S(2)}, u32[]{:S(2)}) collective-permute-start(f32[32,640]{1,0:T(8,128)S(1)} %add_add_fusion.refs_0_), channel_id=1, source_target_pairs={{0,16},{1,17},{2,18},{3,19},{4,20},{5,21},{6,22},{7,23},{8,24},{9,... | collective-permute-start | bytes 245768 | tf_op jit(solution)/shard_map/ppermute | solution.py:30
  58.4 4.4 %collective-permute-start.19 = (f32[32,640]{1,0:T(8,128)S(1)}, f32[32,640]{1,0:T(8,128)S(1)}, u32[]{:S(2)}, u32[]{:S(2)}) collective-permute-start(f32[32,640]{1,0:T(8,128)S(1)} %add_add_fusion.refs_0_), channel_id=1, source_target_pairs={{0,2},{1,3},{2,0},{3,1},{4,6},{5,7},{6,4},{7,5},{8,10},{9,11},{10,... | collective-permute-start | bytes 245768 | tf_op jit(solution)/shard_map/ppermute | solution.py:30
  59.8 9.3 %copy-start = (f32[512,256]{1,0:T(8,128)S(1)}, f32[512,256]{1,0:T(8,128)}, u32[]{:S(2)}) copy-start(f32[512,256]{1,0:T(8,128)} %pivot_ref.1) | copy-start | bytes 1572868
  59.9 8.6 %collective-permute-start.7 = (f32[128,256]{1,0:T(8,128)S(1)}, f32[128,256]{1,0:T(8,128)S(1)}, u32[]{:S(2)}, u32[]{:S(2)}) collective-permute-start(f32[128,256]{1,0:T(8,128)S(1)} %fusion), channel_id=1, source_target_pairs={{0,8},{1,9},{2,10},{3,11},{4,12},{5,13},{6,14},{7,15},{8,0},{9,1},... | collective-permute-start | bytes 393224 | tf_op jit(solution)/shard_map/ppermute | solution.py:30
  62.9 6.2 %collective-permute-start.22 = (f32[128,256]{1,0:T(8,128)S(1)}, f32[128,256]{1,0:T(8,128)S(1)}, u32[]{:S(2)}, u32[]{:S(2)}) collective-permute-start(f32[128,256]{1,0:T(8,128)S(1)} %pad_maximum_fusion.1), channel_id=1, source_target_pairs={{0,1},{1,0},{2,3},{3,2},{4,5},{5,4},{6,7},{7,6},{8,9},{9,8},{10,11... | collective-permute-start | bytes 393224 | tf_op jit(solution)/shard_map/ppermute | solution.py:30

commit v6 on v5

--- a/solution.py
+++ b/solution.py
@@ -129,15 +129,16 @@
             outs[1][k // PAIR] = share
 
 
-def coupling_kernel(members, planes, share_ref, other_ref, gathered_ref, *refs):
-    strip, outs, total_ref = refs[: planes + 1], refs[planes + 1 : -1], refs[-1]
+def coupling_kernel(members, planes, share_ref, other_ref, *refs):
+    strip, other_strip = refs[:planes], refs[planes : 2 * planes]
+    outs, total_ref = refs[2 * planes : -1], refs[-1]
     row, col, rep = here()
     place, first = row * PAIR + col % PAIR, rep == 0
     tile, half = strip[0].shape
     quarter = half // 2
     step = quarter // members
-    own_normed = jnp.concatenate([ref[...] for ref in strip[:planes]], 0)
-    other_normed = jnp.concatenate([strip[planes][...], gathered_ref[...]], 0)
+    own_normed = jnp.concatenate([ref[...] for ref in strip], 0)
+    other_normed = jnp.concatenate([ref[...] for ref in other_strip], 0)
     own = share_ref[...].reshape(planes * tile, half)
     other = other_ref[...].reshape(planes * tile, half)
     mixed = split_dot(split(own_normed), split(own), (0, 0))
@@ -270,8 +271,7 @@
     arrived = [send(own_normed, to_plane)]
     arrived += [send(arrived[0], beside(k)) for k in range(1, members)]
     strip = [own_normed] + [send(own_normed, along(k)) for k in range(1, planes)]
-    packed = jnp.concatenate(strip[1:], 0)
-    other_strip = swap_core(packed)
+    other_strip = [swap_core(strip[k]) for k in range(1, planes)]
     mine = send(given, lambda r, c, p: (r, c ^ 1, p))
     theirs = swap_core(mine)
     product, given_shares = call(
@@ -293,7 +293,7 @@
         functools.partial(coupling_kernel, members, planes),
         [(step, width)] * members,
         "",
-        [product, other_product, other_strip, *strip, other_normed],
+        [product, other_product, *strip, other_normed, *other_strip],
         [(quarter, width)],
         flops=12 * planes * tile * half * half,
     )

time: 70.3 us -> 78.1 us (1.11)
  waiting for transfers between devices: 28.7 us -> 36.9 us
    ppermute x23 -> x25, waiting for transfers between devices: 28.7 us -> 36.9 us  [send(): return lax.ppermute(block, AXES, route)]
    ppermute x23 -> x25, starting transfers between devices: 31.3 us -> 30.9 us  [send(): return lax.ppermute(block, AXES, route)]
  transfers between devices with their start and end apart: 23 -> 25, of which waited for: 10 -> 16; matrix products, arithmetic and copies ran while one was open for 1% -> 1% of each run, Pallas kernels for 6% -> 4%
where the time goes in v6:
time: 78.1 us; the launch traced here: 77.9 us
  waiting for transfers between devices  36.9 us (47%)
  starting transfers between devices  30.9 us (40%)
  Pallas kernels  7.88 us (10%)
    ppermute x25, waiting for transfers between devices, send(): return lax.ppermute(block, AXES, route)  36.9 us
    ppermute x25, starting transfers between devices, send(): return lax.ppermute(block, AXES, route)  30.9 us
    pallas_call x6, Pallas kernels, call(): pl.pallas_call(kernel, out_shape=[jax.ShapeDtypeStruct(shape, F32) for sh...  7.88 us
  transfers between devices with their start and end apart: 25, of which 16 were waited for; matrix products, arithmetic and copies ran while one was open for 1% of the time, Pallas kernels for 4%

profile of v6, /device:TPU:0, one launch (start us, length us, event | category | flops | bytes accessed | tf_op | source)
XLA Modules:
  0.0 77.9 jit_solution(12259673822382966584)
XLA Ops:
  0.6 0.7 copy-done.1
  1.3 1.9 %shard_map.68 = (f32[4,128,256]{2,1,0:T(8,128)S(1)}, f32[2,128,256]{2,1,0:T(8,128)S(1)}) custom-call(s32[2,8]{1,0:T(2,128)S(1)} %bitcast.9, f32[1024,256]{1,0:T(8,128)} %full_ref.1), custom_call_target="tpu_custom_call" | custom-call | bytes 1835072 | tf_op jit(solution)/shard_map/pallas_call | solution.py:213
  3.2 3.0 %collective-permute-start = (f32[2,128,256]{2,1,0:T(8,128)S(1)}, f32[2,128,256]{2,1,0:T(8,128)S(1)}, u32[]{:S(2)}, u32[]{:S(2)}) collective-permute-start(f32[2,128,256]{2,1,0:T(8,128)S(1)} %get-tuple-element.11), channel_id=1, source_target_pairs={{0,2},{1,3},{2,0},{3,1},{4,6},{5,7},{6,4},{7,5},{8,10},{9,11},{10,... | collective-permute-start | bytes 786440 | tf_op jit(solution)/shard_map/ppermute | solution.py:30
  6.2 1.7 %shard_map.69.refs_0_ = f32[128,256]{1,0:T(8,128)S(1)} custom-call(f32[128,512]{1,0:T(8,128)} %factor_ref.3, f32[512,512]{1,0:T(8,128)} %normalizer_ref.3), custom_call_target="tpu_custom_call" | custom-call | bytes 1441792 | tf_op jit(solution)/shard_map/pallas_call | solution.py:213
  7.9 0.7 collective-permute-start.2
  8.6 6.0 %collective-permute-done.mine_ref = f32[2,128,256]{2,1,0:T(8,128)S(1)} collective-permute-done((f32[2,128,256]{2,1,0:T(8,128)S(1)}, f32[2,128,256]{2,1,0:T(8,128)S(1)}, u32[]{:S(2)}, u32[]{:S(2)}) %collective-permute-start) | collective-permute-done | bytes 262176 | tf_op jit(solution)/shard_map/ppermute | solution.py:30
  14.6 0.0 collective-permute-start.1
  14.6 0.0 collective-permute-done.2.refs_0_
  14.6 2.6 %collective-permute-start.3 = (f32[128,256]{1,0:T(8,128)S(1)}, f32[128,256]{1,0:T(8,128)S(1)}, u32[]{:S(2)}, u32[]{:S(2)}) collective-permute-start(f32[128,256]{1,0:T(8,128)S(1)} %collective-permute-done.2.refs_0_), channel_id=1, source_target_pairs={{0,16},{1,17},{2,18},{3,19},{4,20},{5,21},{6,22},{7,23},{8,24},{9,... | collective-permute-start | bytes 393224 | tf_op jit(solution)/shard_map/ppermute | solution.py:30
  17.2 0.7 collective-permute-start.4
  17.9 0.8 collective-permute-start.5
  18.7 1.8 %collective-permute-done.3.refs_1_ = f32[128,256]{1,0:T(8,128)S(1)} collective-permute-done((f32[128,256]{1,0:T(8,128)S(1)}, f32[128,256]{1,0:T(8,128)S(1)}, u32[]{:S(2)}, u32[]{:S(2)}) %collective-permute-start.3) | collective-permute-done | bytes 131104 | tf_op jit(solution)/shard_map/ppermute | solution.py:30
  20.5 2.8 %collective-permute-done.4.refs_2_ = f32[128,256]{1,0:T(8,128)S(1)} collective-permute-done((f32[128,256]{1,0:T(8,128)S(1)}, f32[128,256]{1,0:T(8,128)S(1)}, u32[]{:S(2)}, u32[]{:S(2)}) %collective-permute-start.4) | collective-permute-done | bytes 131104 | tf_op jit(solution)/shard_map/ppermute | solution.py:30
  23.3 1.9 %collective-permute-done.5.refs_3_ = f32[128,256]{1,0:T(8,128)S(1)} collective-permute-done((f32[128,256]{1,0:T(8,128)S(1)}, f32[128,256]{1,0:T(8,128)S(1)}, u32[]{:S(2)}, u32[]{:S(2)}) %collective-permute-start.5) | collective-permute-done | bytes 131104 | tf_op jit(solution)/shard_map/ppermute | solution.py:30
  25.2 0.6 shard_map.70
  25.8 0.1 collective-permute-start.8
  25.9 5.0 %collective-permute-start.9 = (f32[128,256]{1,0:T(8,128)S(1)}, f32[128,256]{1,0:T(8,128)S(1)}, u32[]{:S(2)}, u32[]{:S(2)}) collective-permute-start(f32[128,256]{1,0:T(8,128)S(1)} %shard_map.69.refs_0_), channel_id=1, source_target_pairs={{0,4},{1,5},{2,6},{3,7},{4,0},{5,1},{6,2},{7,3},{8,12},{9,13},{10,... | collective-permute-start | bytes 393224 | tf_op jit(solution)/shard_map/ppermute | solution.py:30
  30.9 2.4 %collective-permute-start.11 = (f32[128,256]{1,0:T(8,128)S(1)}, f32[128,256]{1,0:T(8,128)S(1)}, u32[]{:S(2)}, u32[]{:S(2)}) collective-permute-start(f32[128,256]{1,0:T(8,128)S(1)} %shard_map.69.refs_0_), channel_id=1, source_target_pairs={{0,12},{1,13},{2,14},{3,15},{4,8},{5,9},{6,10},{7,11},{8,4},{9,5},... | collective-permute-start | bytes 393224 | tf_op jit(solution)/shard_map/ppermute | solution.py:30
  33.3 2.3 %collective-permute-done.9.refs_1_ = f32[128,256]{1,0:T(8,128)S(1)} collective-permute-done((f32[128,256]{1,0:T(8,128)S(1)}, f32[128,256]{1,0:T(8,128)S(1)}, u32[]{:S(2)}, u32[]{:S(2)}) %collective-permute-start.9) | collective-permute-done | bytes 131104 | tf_op jit(solution)/shard_map/ppermute | solution.py:30
  35.7 7.8 %collective-permute-done.10.refs_2_ = f32[128,256]{1,0:T(8,128)S(1)} collective-permute-done((f32[128,256]{1,0:T(8,128)S(1)}, f32[128,256]{1,0:T(8,128)S(1)}, u32[]{:S(2)}, u32[]{:S(2)}) %collective-permute-start.10) | collective-permute-done | bytes 131104 | tf_op jit(solution)/shard_map/ppermute | solution.py:30
  43.5 0.5 collective-permute-start.14
  44.0 1.7 %shard_map.71.refs_4_ = f32[128,256]{1,0:T(8,128)S(1)} custom-call(f32[128,512]{1,0:T(8,128)} %factor_ref.3, f32[512,512]{1,0:T(8,128)} %normalizer_ref.3), custom_call_target="tpu_custom_call" | custom-call | bytes 1441792 | tf_op jit(solution)/shard_map/pallas_call | solution.py:213
  45.8 0.9 %shard_map.72 = (f32[32,640]{1,0:T(8,128)S(1)}, f32[32,640]{1,0:T(8,128)S(1)}, f32[32,640]{1,0:T(8,128)S(1)}, f32[32,640]{1,0:T(8,128)S(1)}) custom-call(f32[4,128,256]{2,1,0:T(8,128)S(1)} %get-tuple-element.12.share_ref, f32[4,128,256]{2,1,0:T(8,128)S(1)} %collective-permute-done.8.other_ref, f32[128,256]{1,0:T(8,128)S(1)} %shard_map.69.refs_0_, ...), custom_call_target="tpu_custom_call" | custom-call | flops 402653184 | bytes 2424832 | tf_op jit(solution)/shard_map/pallas_call | solution.py:213
  46.7 1.5 %collective-permute-start.17 = (f32[32,640]{1,0:T(8,128)S(1)}, f32[32,640]{1,0:T(8,128)S(1)}, u32[]{:S(2)}, u32[]{:S(2)}) collective-permute-start(f32[32,640]{1,0:T(8,128)S(1)} %get-tuple-element.17), channel_id=1, source_target_pairs={{0,18},{1,19},{2,16},{3,17},{4,22},{5,23},{6,20},{7,21},{8,26},{9,... | collective-permute-start | bytes 245768 | tf_op jit(solution)/shard_map/ppermute | solution.py:30
  48.3 1.5 %collective-permute-start.15 = (f32[32,640]{1,0:T(8,128)S(1)}, f32[32,640]{1,0:T(8,128)S(1)}, u32[]{:S(2)}, u32[]{:S(2)}) collective-permute-start(f32[32,640]{1,0:T(8,128)S(1)} %get-tuple-element.15), channel_id=1, source_target_pairs={{0,2},{1,3},{2,0},{3,1},{4,6},{5,7},{6,4},{7,5},{8,10},{9,11},{10,... | collective-permute-start | bytes 245768 | tf_op jit(solution)/shard_map/ppermute | solution.py:30
  49.7 0.5 collective-permute-start.16
  50.3 2.7 %collective-permute-done.17 = f32[32,640]{1,0:T(8,128)S(1)} collective-permute-done((f32[32,640]{1,0:T(8,128)S(1)}, f32[32,640]{1,0:T(8,128)S(1)}, u32[]{:S(2)}, u32[]{:S(2)}) %collective-permute-start.17) | collective-permute-done | bytes 81952 | tf_op jit(solution)/shard_map/ppermute | solution.py:30
  53.0 0.8 %collective-permute-done.15 = f32[32,640]{1,0:T(8,128)S(1)} collective-permute-done((f32[32,640]{1,0:T(8,128)S(1)}, f32[32,640]{1,0:T(8,128)S(1)}, u32[]{:S(2)}, u32[]{:S(2)}) %collective-permute-start.15) | collective-permute-done | bytes 81952 | tf_op jit(solution)/shard_map/ppermute | solution.py:30
  53.8 0.4 collective-permute-done.16
  54.2 0.7 collective-permute-start.20
  55.0 2.0 %collective-permute-start.18 = (f32[32,640]{1,0:T(8,128)S(1)}, f32[32,640]{1,0:T(8,128)S(1)}, u32[]{:S(2)}, u32[]{:S(2)}) collective-permute-start(f32[32,640]{1,0:T(8,128)S(1)} %add_add_fusion.1), channel_id=1, source_target_pairs={{0,4},{1,5},{2,6},{3,7},{4,0},{5,1},{6,2},{7,3},{8,12},{9,13},{10,... | collective-permute-start | bytes 245768 | tf_op jit(solution)/shard_map/ppermute | solution.py:30
  57.0 1.7 %collective-permute-start.19 = (f32[32,640]{1,0:T(8,128)S(1)}, f32[32,640]{1,0:T(8,128)S(1)}, u32[]{:S(2)}, u32[]{:S(2)}) collective-permute-start(f32[32,640]{1,0:T(8,128)S(1)} %add_add_fusion.1), channel_id=1, source_target_pairs={{0,8},{1,9},{2,10},{3,11},{4,12},{5,13},{6,14},{7,15},{8,0},{9,1},... | collective-permute-start | bytes 245768 | tf_op jit(solution)/shard_map/ppermute | solution.py:30
  58.7 1.7 %collective-permute-start.6 = (f32[2,128,256]{2,1,0:T(8,128)S(1)}, f32[2,128,256]{2,1,0:T(8,128)S(1)}, u32[]{:S(2)}, u32[]{:S(2)}) collective-permute-start(f32[2,128,256]{2,1,0:T(8,128)S(1)} %get-tuple-element.13), channel_id=1, source_target_pairs={{0,4},{1,5},{2,6},{3,7},{4,0},{5,1},{6,2},{7,3},{8,12},{9,13},{10,... | collective-permute-start | bytes 786440 | tf_op jit(solution)/shard_map/ppermute | solution.py:30
  60.4 0.9 %collective-permute-done.20 = f32[32,640]{1,0:T(8,128)S(1)} collective-permute-done((f32[32,640]{1,0:T(8,128)S(1)}, f32[32,640]{1,0:T(8,128)S(1)}, u32[]{:S(2)}, u32[]{:S(2)}) %collective-permute-start.20) | collective-permute-done | bytes 81952 | tf_op jit(solution)/shard_map/ppermute | solution.py:30
  61.3 0.7 collective-permute-done.18
  61.9 3.0 %collective-permute-done.19 = f32[32,640]{1,0:T(8,128)S(1)} collective-permute-done((f32[32,640]{1,0:T(8,128)S(1)}, f32[32,640]{1,0:T(8,128)S(1)}, u32[]{:S(2)}, u32[]{:S(2)}) %collective-permute-start.19) | collective-permute-done | bytes 81952 | tf_op jit(solution)/shard_map/ppermute | solution.py:30
  65.0 1.5 %collective-permute-start.23 = (f32[32,640]{1,0:T(8,128)S(1)}, f32[32,640]{1,0:T(8,128)S(1)}, u32[]{:S(2)}, u32[]{:S(2)}) collective-permute-start(f32[32,640]{1,0:T(8,128)S(1)} %add_add_fusion.refs_0_), channel_id=1, source_target_pairs={{0,18},{1,19},{2,16},{3,17},{4,22},{5,23},{6,20},{7,21},{8,26},{9,... | collective-permute-start | bytes 245768 | tf_op jit(solution)/shard_map/ppermute | solution.py:30
  66.5 0.5 collective-permute-start.22
  67.1 1.5 %collective-permute-start.21 = (f32[32,640]{1,0:T(8,128)S(1)}, f32[32,640]{1,0:T(8,128)S(1)}, u32[]{:S(2)}, u32[]{:S(2)}) collective-permute-start(f32[32,640]{1,0:T(8,128)S(1)} %add_add_fusion.refs_0_), channel_id=1, source_target_pairs={{0,2},{1,3},{2,0},{3,1},{4,6},{5,7},{6,4},{7,5},{8,10},{9,11},{10,... | collective-permute-start | bytes 245768 | tf_op jit(solution)/shard_map/ppermute | solution.py:30
  68.5 0.0 copy-start
  68.6 1.7 %collective-permute-start.7 = (f32[128,256]{1,0:T(8,128)S(1)}, f32[128,256]{1,0:T(8,128)S(1)}, u32[]{:S(2)}, u32[]{:S(2)}) collective-permute-start(f32[128,256]{1,0:T(8,128)S(1)} %fusion), channel_id=1, source_target_pairs={{0,8},{1,9},{2,10},{3,11},{4,12},{5,13},{6,14},{7,15},{8,0},{9,1},... | collective-permute-start | bytes 393224 | tf_op jit(solution)/shard_map/ppermute | solution.py:30
  70.3 0.8 %collective-permute-done.23.refs_3_ = f32[32,640]{1,0:T(8,128)S(1)} collective-permute-done((f32[32,640]{1,0:T(8,128)S(1)}, f32[32,640]{1,0:T(8,128)S(1)}, u32[]{:S(2)}, u32[]{:S(2)}) %collective-permute-start.23) | collective-permute-done | bytes 81952 | tf_op jit(solution)/shard_map/ppermute | solution.py:30
  71.1 0.4 collective-permute-done.22.refs_2_
  71.5 0.1 collective-permute-done.21.refs_1_
  71.6 0.1 collective-permute-start.24
  71.7 4.5 %collective-permute-done.7 = f32[128,256]{1,0:T(8,128)S(1)} collective-permute-done((f32[128,256]{1,0:T(8,128)S(1)}, f32[128,256]{1,0:T(8,128)S(1)}, u32[]{:S(2)}, u32[]{:S(2)}) %collective-permute-start.7) | collective-permute-done | bytes 131104 | tf_op jit(solution)/shard_map/ppermute | solution.py:30
  76.2 0.7 fusion.3
  76.9 1.0 %shard_map.73 = f32[512,256]{1,0:T(8,128)} custom-call(f32[512,256]{1,0:T(8,128)S(1)} %copy-done, f32[128,256]{1,0:T(8,128)S(1)} %collective-permute-done.24.other_ref, f32[32,640]{1,0:T(8,128)S(1)} %add_add_fusion.refs_0_, f32[32,640]{1,0:T(8,128)S(1)} %collective-permute-done.21.refs_1_, f32[32,640]{1,0:T(8,128)S(1)} %collective-permute-done.22.refs_2_, ...), custom_call_target="tpu_custom_call" | custom-call | bytes 1507328 | tf_op jit(solution)/shard_map/pallas_call | solution.py:213
  (21 shorter events, 0.1 us)
Async XLA Ops:
  0.6 0.7 copy-start.1
  3.2 11.4 %collective-permute-start = (f32[2,128,256]{2,1,0:T(8,128)S(1)}, f32[2,128,256]{2,1,0:T(8,128)S(1)}, u32[]{:S(2)}, u32[]{:S(2)}) collective-permute-start(f32[2,128,256]{2,1,0:T(8,128)S(1)} %get-tuple-element.11), channel_id=1, source_target_pairs={{0,2},{1,3},{2,0},{3,1},{4,6},{5,7},{6,4},{7,5},{8,10},{9,11},{10,... | collective-permute-start | bytes 786440 | tf_op jit(solution)/shard_map/ppermute | solution.py:30
  7.9 6.6 %collective-permute-start.2 = (f32[128,256]{1,0:T(8,128)S(1)}, f32[128,256]{1,0:T(8,128)S(1)}, u32[]{:S(2)}, u32[]{:S(2)}) collective-permute-start(f32[128,256]{1,0:T(8,128)S(1)} %shard_map.69.refs_0_), channel_id=1, source_target_pairs={{0,0},{1,1},{2,16},{3,17},{4,2},{5,3},{6,18},{7,19},{8,4},{9,5},{1... | collective-permute-start | bytes 393224 | tf_op jit(solution)/shard_map/ppermute | solution.py:30
  14.6 10.6 %collective-permute-start.1 = (f32[2,128,256]{2,1,0:T(8,128)S(1)}, f32[2,128,256]{2,1,0:T(8,128)S(1)}, u32[]{:S(2)}, u32[]{:S(2)}) collective-permute-start(f32[2,128,256]{2,1,0:T(8,128)S(1)} %collective-permute-done.mine_ref), channel_id=1, source_target_pairs={{0,1},{1,0},{2,3},{3,2},{4,5},{5,4},{6,7},{7,6},{8,9},{9,8},{10,11... | collective-permute-start | bytes 786440 | tf_op jit(solution)/shard_map/ppermute | solution.py:30
  14.6 5.9 %collective-permute-start.3 = (f32[128,256]{1,0:T(8,128)S(1)}, f32[128,256]{1,0:T(8,128)S(1)}, u32[]{:S(2)}, u32[]{:S(2)}) collective-permute-start(f32[128,256]{1,0:T(8,128)S(1)} %collective-permute-done.2.refs_0_), channel_id=1, source_target_pairs={{0,16},{1,17},{2,18},{3,19},{4,20},{5,21},{6,22},{7,23},{8,24},{9,... | collective-permute-start | bytes 393224 | tf_op jit(solution)/shard_map/ppermute | solution.py:30
  17.2 6.1 %collective-permute-start.4 = (f32[128,256]{1,0:T(8,128)S(1)}, f32[128,256]{1,0:T(8,128)S(1)}, u32[]{:S(2)}, u32[]{:S(2)}) collective-permute-start(f32[128,256]{1,0:T(8,128)S(1)} %collective-permute-done.2.refs_0_), channel_id=1, source_target_pairs={{0,2},{1,3},{2,0},{3,1},{4,6},{5,7},{6,4},{7,5},{8,10},{9,11},{10,... | collective-permute-start | bytes 393224 | tf_op jit(solution)/shard_map/ppermute | solution.py:30
  17.9 7.3 %collective-permute-start.5 = (f32[128,256]{1,0:T(8,128)S(1)}, f32[128,256]{1,0:T(8,128)S(1)}, u32[]{:S(2)}, u32[]{:S(2)}) collective-permute-start(f32[128,256]{1,0:T(8,128)S(1)} %collective-permute-done.2.refs_0_), channel_id=1, source_target_pairs={{0,18},{1,19},{2,16},{3,17},{4,22},{5,23},{6,20},{7,21},{8,26},{9,... | collective-permute-start | bytes 393224 | tf_op jit(solution)/shard_map/ppermute | solution.py:30
  25.8 19.9 %collective-permute-start.8 = (f32[4,128,256]{2,1,0:T(8,128)S(1)}, f32[4,128,256]{2,1,0:T(8,128)S(1)}, u32[]{:S(2)}, u32[]{:S(2)}) collective-permute-start(f32[4,128,256]{2,1,0:T(8,128)S(1)} %get-tuple-element.12.share_ref), channel_id=1, source_target_pairs={{0,1},{1,0},{2,3},{3,2},{4,5},{5,4},{6,7},{7,6},{8,9},{9,8},{10,11... | collective-permute-start | bytes 1572872 | tf_op jit(solution)/shard_map/ppermute | solution.py:30
  25.9 9.7 %collective-permute-start.9 = (f32[128,256]{1,0:T(8,128)S(1)}, f32[128,256]{1,0:T(8,128)S(1)}, u32[]{:S(2)}, u32[]{:S(2)}) collective-permute-start(f32[128,256]{1,0:T(8,128)S(1)} %shard_map.69.refs_0_), channel_id=1, source_target_pairs={{0,4},{1,5},{2,6},{3,7},{4,0},{5,1},{6,2},{7,3},{8,12},{9,13},{10,... | collective-permute-start | bytes 393224 | tf_op jit(solution)/shard_map/ppermute | solution.py:30
  30.9 12.6 %collective-permute-start.10 = (f32[128,256]{1,0:T(8,128)S(1)}, f32[128,256]{1,0:T(8,128)S(1)}, u32[]{:S(2)}, u32[]{:S(2)}) collective-permute-start(f32[128,256]{1,0:T(8,128)S(1)} %shard_map.69.refs_0_), channel_id=1, source_target_pairs={{0,8},{1,9},{2,10},{3,11},{4,12},{5,13},{6,14},{7,15},{8,0},{9,1},... | collective-permute-start | bytes 393224 | tf_op jit(solution)/shard_map/ppermute | solution.py:30
  30.9 12.6 %collective-permute-start.11 = (f32[128,256]{1,0:T(8,128)S(1)}, f32[128,256]{1,0:T(8,128)S(1)}, u32[]{:S(2)}, u32[]{:S(2)}) collective-permute-start(f32[128,256]{1,0:T(8,128)S(1)} %shard_map.69.refs_0_), channel_id=1, source_target_pairs={{0,12},{1,13},{2,14},{3,15},{4,8},{5,9},{6,10},{7,11},{8,4},{9,5},... | collective-permute-start | bytes 393224 | tf_op jit(solution)/shard_map/ppermute | solution.py:30
  35.7 10.1 %collective-permute-start.12 = (f32[128,256]{1,0:T(8,128)S(1)}, f32[128,256]{1,0:T(8,128)S(1)}, u32[]{:S(2)}, u32[]{:S(2)}) collective-permute-start(f32[128,256]{1,0:T(8,128)S(1)} %collective-permute-done.9.refs_1_), channel_id=1, source_target_pairs={{0,1},{1,0},{2,3},{3,2},{4,5},{5,4},{6,7},{7,6},{8,9},{9,8},{10,11... | collective-permute-start | bytes 393224 | tf_op jit(solution)/shard_map/ppermute | solution.py:30
  43.5 2.3 %collective-permute-start.13 = (f32[128,256]{1,0:T(8,128)S(1)}, f32[128,256]{1,0:T(8,128)S(1)}, u32[]{:S(2)}, u32[]{:S(2)}) collective-permute-start(f32[128,256]{1,0:T(8,128)S(1)} %collective-permute-done.10.refs_2_), channel_id=1, source_target_pairs={{0,1},{1,0},{2,3},{3,2},{4,5},{5,4},{6,7},{7,6},{8,9},{9,8},{10,11... | collective-permute-start | bytes 393224 | tf_op jit(solution)/shard_map/ppermute | solution.py:30
  43.5 2.3 %collective-permute-start.14 = (f32[128,256]{1,0:T(8,128)S(1)}, f32[128,256]{1,0:T(8,128)S(1)}, u32[]{:S(2)}, u32[]{:S(2)}) collective-permute-start(f32[128,256]{1,0:T(8,128)S(1)} %collective-permute-done.11.refs_3_), channel_id=1, source_target_pairs={{0,1},{1,0},{2,3},{3,2},{4,5},{5,4},{6,7},{7,6},{8,9},{9,8},{10,11... | collective-permute-start | bytes 393224 | tf_op jit(solution)/shard_map/ppermute | solution.py:30
  46.7 6.3 %collective-permute-start.17 = (f32[32,640]{1,0:T(8,128)S(1)}, f32[32,640]{1,0:T(8,128)S(1)}, u32[]{:S(2)}, u32[]{:S(2)}) collective-permute-start(f32[32,640]{1,0:T(8,128)S(1)} %get-tuple-element.17), channel_id=1, source_target_pairs={{0,18},{1,19},{2,16},{3,17},{4,22},{5,23},{6,20},{7,21},{8,26},{9,... | collective-permute-start | bytes 245768 | tf_op jit(solution)/shard_map/ppermute | solution.py:30
  48.3 5.6 %collective-permute-start.15 = (f32[32,640]{1,0:T(8,128)S(1)}, f32[32,640]{1,0:T(8,128)S(1)}, u32[]{:S(2)}, u32[]{:S(2)}) collective-permute-start(f32[32,640]{1,0:T(8,128)S(1)} %get-tuple-element.15), channel_id=1, source_target_pairs={{0,2},{1,3},{2,0},{3,1},{4,6},{5,7},{6,4},{7,5},{8,10},{9,11},{10,... | collective-permute-start | bytes 245768 | tf_op jit(solution)/shard_map/ppermute | solution.py:30
  49.7 4.4 %collective-permute-start.16 = (f32[32,640]{1,0:T(8,128)S(1)}, f32[32,640]{1,0:T(8,128)S(1)}, u32[]{:S(2)}, u32[]{:S(2)}) collective-permute-start(f32[32,640]{1,0:T(8,128)S(1)} %get-tuple-element.16), channel_id=1, source_target_pairs={{0,16},{1,17},{2,18},{3,19},{4,20},{5,21},{6,22},{7,23},{8,24},{9,... | collective-permute-start | bytes 245768 | tf_op jit(solution)/shard_map/ppermute | solution.py:30
  54.2 7.1 %collective-permute-start.20 = (f32[32,640]{1,0:T(8,128)S(1)}, f32[32,640]{1,0:T(8,128)S(1)}, u32[]{:S(2)}, u32[]{:S(2)}) collective-permute-start(f32[32,640]{1,0:T(8,128)S(1)} %add_add_fusion.1), channel_id=1, source_target_pairs={{0,12},{1,13},{2,14},{3,15},{4,8},{5,9},{6,10},{7,11},{8,4},{9,5},... | collective-permute-start | bytes 245768 | tf_op jit(solution)/shard_map/ppermute | solution.py:30
  55.0 7.0 %collective-permute-start.18 = (f32[32,640]{1,0:T(8,128)S(1)}, f32[32,640]{1,0:T(8,128)S(1)}, u32[]{:S(2)}, u32[]{:S(2)}) collective-permute-start(f32[32,640]{1,0:T(8,128)S(1)} %add_add_fusion.1), channel_id=1, source_target_pairs={{0,4},{1,5},{2,6},{3,7},{4,0},{5,1},{6,2},{7,3},{8,12},{9,13},{10,... | collective-permute-start | bytes 245768 | tf_op jit(solution)/shard_map/ppermute | solution.py:30
  57.0 8.0 %collective-permute-start.19 = (f32[32,640]{1,0:T(8,128)S(1)}, f32[32,640]{1,0:T(8,128)S(1)}, u32[]{:S(2)}, u32[]{:S(2)}) collective-permute-start(f32[32,640]{1,0:T(8,128)S(1)} %add_add_fusion.1), channel_id=1, source_target_pairs={{0,8},{1,9},{2,10},{3,11},{4,12},{5,13},{6,14},{7,15},{8,0},{9,1},... | collective-permute-start | bytes 245768 | tf_op jit(solution)/shard_map/ppermute | solution.py:30
  58.7 9.9 %collective-permute-start.6 = (f32[2,128,256]{2,1,0:T(8,128)S(1)}, f32[2,128,256]{2,1,0:T(8,128)S(1)}, u32[]{:S(2)}, u32[]{:S(2)}) collective-permute-start(f32[2,128,256]{2,1,0:T(8,128)S(1)} %get-tuple-element.13), channel_id=1, source_target_pairs={{0,4},{1,5},{2,6},{3,7},{4,0},{5,1},{6,2},{7,3},{8,12},{9,13},{10,... | collective-permute-start | bytes 786440 | tf_op jit(solution)/shard_map/ppermute | solution.py:30
  65.0 6.2 %collective-permute-start.23 = (f32[32,640]{1,0:T(8,128)S(1)}, f32[32,640]{1,0:T(8,128)S(1)}, u32[]{:S(2)}, u32[]{:S(2)}) collective-permute-start(f32[32,640]{1,0:T(8,128)S(1)} %add_add_fusion.refs_0_), channel_id=1, source_target_pairs={{0,18},{1,19},{2,16},{3,17},{4,22},{5,23},{6,20},{7,21},{8,26},{9,... | collective-permute-start | bytes 245768 | tf_op jit(solution)/shard_map/ppermute | solution.py:30
  66.5 5.0 %collective-permute-start.22 = (f32[32,640]{1,0:T(8,128)S(1)}, f32[32,640]{1,0:T(8,128)S(1)}, u32[]{:S(2)}, u32[]{:S(2)}) collective-permute-start(f32[32,640]{1,0:T(8,128)S(1)} %add_add_fusion.refs_0_), channel_id=1, source_target_pairs={{0,16},{1,17},{2,18},{3,19},{4,20},{5,21},{6,22},{7,23},{8,24},{9,... | collective-permute-start | bytes 245768 | tf_op jit(solution)/shard_map/ppermute | solution.py:30
  67.1 4.5 %collective-permute-start.21 = (f32[32,640]{1,0:T(8,128)S(1)}, f32[32,640]{1,0:T(8,128)S(1)}, u32[]{:S(2)}, u32[]{:S(2)}) collective-permute-start(f32[32,640]{1,0:T(8,128)S(1)} %add_add_fusion.refs_0_), channel_id=1, source_target_pairs={{0,2},{1,3},{2,0},{3,1},{4,6},{5,7},{6,4},{7,5},{8,10},{9,11},{10,... | collective-permute-start | bytes 245768 | tf_op jit(solution)/shard_map/ppermute | solution.py:30
  68.5 8.4 %copy-start = (f32[512,256]{1,0:T(8,128)S(1)}, f32[512,256]{1,0:T(8,128)}, u32[]{:S(2)}) copy-start(f32[512,256]{1,0:T(8,128)} %pivot_ref.1) | copy-start | bytes 1572868
  68.6 7.7 %collective-permute-start.7 = (f32[128,256]{1,0:T(8,128)S(1)}, f32[128,256]{1,0:T(8,128)S(1)}, u32[]{:S(2)}, u32[]{:S(2)}) collective-permute-start(f32[128,256]{1,0:T(8,128)S(1)} %fusion), channel_id=1, source_target_pairs={{0,8},{1,9},{2,10},{3,11},{4,12},{5,13},{6,14},{7,15},{8,0},{9,1},... | collective-permute-start | bytes 393224 | tf_op jit(solution)/shard_map/ppermute | solution.py:30
  71.6 5.3 %collective-permute-start.24 = (f32[128,256]{1,0:T(8,128)S(1)}, f32[128,256]{1,0:T(8,128)S(1)}, u32[]{:S(2)}, u32[]{:S(2)}) collective-permute-start(f32[128,256]{1,0:T(8,128)S(1)} %pad_maximum_fusion), channel_id=1, source_target_pairs={{0,1},{1,0},{2,3},{3,2},{4,5},{5,4},{6,7},{7,6},{8,9},{9,8},{10,11... | collective-permute-start | bytes 393224 | tf_op jit(solution)/shard_map/ppermute | solution.py:30

commit v7 on v6

--- a/solution.py
+++ b/solution.py
@@ -10,6 +10,7 @@
 
 AXES = ("row", "col", "rep")
 PAIR = 2
+SUBLANES = 8
 ROOM_OWN = 56380000
 ROOM_MASK = 55500000
 F32, BF16 = jnp.float32, jnp.bfloat16
@@ -55,6 +56,11 @@
 
 def tile_at(index, size):
     return pl.ds(pl.multiple_of(index * size, size), size)
+
+
+def square(size):
+    shape = (size, size)
+    return lax.broadcasted_iota(jnp.int32, shape, 0), lax.broadcasted_iota(jnp.int32, shape, 1)
 
 
 def load_all(loads):
@@ -142,10 +148,12 @@
     own = share_ref[...].reshape(planes * tile, half)
     other = other_ref[...].reshape(planes * tile, half)
     mixed = split_dot(split(own_normed), split(own), (0, 0))
-    lower = mixed[quarter:, :quarter]
-    total_ref[:, :quarter] = mixed[:quarter, :quarter] + mixed[:quarter, :quarter].T
-    total_ref[:, quarter:half] = mixed[:quarter, quarter:] + lower.T
-    total_ref[:, half : half + quarter] = mixed[quarter:, quarter:] + mixed[quarter:, quarter:].T
+    first_block = mixed[:quarter, :quarter] + mixed[:quarter, :quarter].T
+    second_block = mixed[quarter:, quarter:] + mixed[quarter:, quarter:].T
+    down, across = square(quarter)
+    total_ref[0] = jnp.where(down >= across, first_block, second_block)
+    total_ref[1] = mixed[:quarter, quarter:] + mixed[quarter:, :quarter].T
+    trace = jnp.sum(jnp.where(down == across, second_block, 0.0), 0, keepdims=True)
 
     def left(mine, theirs):
         return split(jnp.where(first, mine, theirs))
@@ -156,10 +164,15 @@
     between = split_dot(
         left(own_normed, other_normed), right(own, other), (0, 0)
     ) + split_dot(left(own, other), right(own_normed, other_normed), (0, 0))
-    total_ref[:, half + quarter : PAIR * half] = between[:quarter]
-    total_ref[:, PAIR * half :] = between[quarter:]
+    total_ref[2] = between[:quarter]
+    total_ref[3] = between[quarter:]
+    down, across = down[:SUBLANES], across[:SUBLANES]
     for k in range(members):
-        outs[k][...] = total_ref[tile_at(place ^ k, step), :]
+        peer = place ^ k
+        for i in range(4):
+            outs[k][i * step : (i + 1) * step, :] = total_ref[i, tile_at(peer, step), :]
+        inside = (down == 0) & (across >= peer * step) & (across < (peer + 1) * step)
+        outs[k][4 * step :, :] = jnp.where(inside, trace, 0.0)
 
 
 def finish_kernel(members, pivot_ref, other_ref, *refs):
@@ -169,12 +182,27 @@
     half = out_ref.shape[1]
     quarter = half // 2
     step = quarter // members
+    trace = parts[0][4 * step : 4 * step + 1, :]
     for k in range(members):
         rows = tile_at(place ^ k, step)
-        total_ref[rows, :] = parts[k][...]
-        between_ref[rows, :] = other_ref[k * step : (k + 1) * step, :]
-    blocks = [total_ref[:, i * quarter : (i + 1) * quarter] for i in range(5)]
-    others = [between_ref[:, i * quarter : (i + 1) * quarter] for i in range(2)]
+        for i in range(4):
+            total_ref[i, rows, :] = parts[k][i * step : (i + 1) * step, :]
+        for i in range(2):
+            start = (2 * k + i) * step
+            between_ref[i, rows, :] = other_ref[start : start + step, :]
+        if k:
+            trace = trace + parts[k][4 * step : 4 * step + 1, :]
+    down, across = square(quarter)
+    packed = total_ref[0]
+    below, above = (jnp.where(side, packed, 0.0) for side in (down > across, down < across))
+    blocks = [
+        jnp.where(down == across, packed, below + below.T),
+        total_ref[1],
+        jnp.where(down == across, trace, above + above.T),
+        total_ref[2],
+        total_ref[3],
+    ]
+    others = [between_ref[0], between_ref[1]]
 
     def put(i, j, block):
         at = (pl.ds(i * quarter, quarter), pl.ds(j * quarter, quarter))
@@ -288,13 +316,13 @@
     ancestor_columns = -(halved[0] + sum(landed))
 
     quarter = half // 2
-    step, width = quarter // members, 5 * quarter
+    step = quarter // members
     parts = call(
         functools.partial(coupling_kernel, members, planes),
-        [(step, width)] * members,
+        [(4 * step + SUBLANES, quarter)] * members,
         "",
         [product, other_product, *strip, other_normed, *other_strip],
-        [(quarter, width)],
+        [(4, quarter, quarter)],
         flops=12 * planes * tile * half * half,
     )
 
@@ -308,13 +336,13 @@
     part = parts[0] + sum(send(parts[k], in_plane(k)) for k in range(1, members))
     part = part + sum(send(part, along(k)) for k in range(1, planes))
     parts = [part] + [send(part, in_plane(k)) for k in range(1, members)]
-    other_between = swap_core(jnp.concatenate([one[:, half + quarter :] for one in parts], 0))
+    other_between = swap_core(jnp.concatenate([one[2 * step : 4 * step] for one in parts], 0))
     (diag_block,) = call(
         functools.partial(finish_kernel, members),
         [pivot_inverse.shape],
         "",
         [pivot_inverse, other_between, *parts],
-        [(quarter, width), (quarter, half)],
+        [(4, quarter, quarter), (2, quarter, quarter)],
     )
     return ancestor_columns, diag_block
 

time: 78.1 us -> 76.8 us (0.983)
  waiting for transfers between devices: 36.9 us -> 35.3 us
    ppermute x25, waiting for transfers between devices: 36.9 us -> 35.3 us  [send(): return lax.ppermute(block, AXES, route)]
  transfers between devices with their start and end apart: 25 -> 25, of which waited for: 16 -> 15; matrix products, arithmetic and copies ran while one was open for 1% -> 1% of each run, Pallas kernels for 4% -> 5%
where the time goes in v7:
time: 76.8 us; the launch traced here: 76.6 us
  waiting for transfers between devices  35.3 us (46%)
  starting transfers between devices  31 us (40%)
  Pallas kernels  7.96 us (10%)
  between operations  0.78 us (1%)
    ppermute x25, waiting for transfers between devices, send(): return lax.ppermute(block, AXES, route)  35.3 us
    ppermute x25, starting transfers between devices, send(): return lax.ppermute(block, AXES, route)  31 us
    pallas_call x6, Pallas kernels, call(): pl.pallas_call(kernel, out_shape=[jax.ShapeDtypeStruct(shape, F32) for sh...  7.96 us
  transfers between devices with their start and end apart: 25, of which 15 were waited for; matrix products, arithmetic and copies ran while one was open for 1% of the time, Pallas kernels for 5%

profile of v7, /device:TPU:0, one launch (start us, length us, event | category | flops | bytes accessed | tf_op | source)
XLA Modules:
  0.0 76.6 jit_solution(5899408158640742355)
XLA Ops:
  0.6 0.7 copy-done.1
  1.3 1.9 %shard_map.68 = (f32[4,128,256]{2,1,0:T(8,128)S(1)}, f32[2,128,256]{2,1,0:T(8,128)S(1)}) custom-call(s32[2,8]{1,0:T(2,128)S(1)} %bitcast.9, f32[1024,256]{1,0:T(8,128)} %full_ref.1), custom_call_target="tpu_custom_call" | custom-call | bytes 1835072 | tf_op jit(solution)/shard_map/pallas_call | solution.py:241
  3.2 3.0 %collective-permute-start = (f32[2,128,256]{2,1,0:T(8,128)S(1)}, f32[2,128,256]{2,1,0:T(8,128)S(1)}, u32[]{:S(2)}, u32[]{:S(2)}) collective-permute-start(f32[2,128,256]{2,1,0:T(8,128)S(1)} %get-tuple-element.11), channel_id=1, source_target_pairs={{0,2},{1,3},{2,0},{3,1},{4,6},{5,7},{6,4},{7,5},{8,10},{9,11},{10,... | collective-permute-start | bytes 786440 | tf_op jit(solution)/shard_map/ppermute | solution.py:31
  6.2 1.7 %shard_map.69.refs_0_ = f32[128,256]{1,0:T(8,128)S(1)} custom-call(f32[128,512]{1,0:T(8,128)} %factor_ref.3, f32[512,512]{1,0:T(8,128)} %normalizer_ref.3), custom_call_target="tpu_custom_call" | custom-call | bytes 1441792 | tf_op jit(solution)/shard_map/pallas_call | solution.py:241
  7.9 0.7 collective-permute-start.2
  8.6 6.0 %collective-permute-done.mine_ref = f32[2,128,256]{2,1,0:T(8,128)S(1)} collective-permute-done((f32[2,128,256]{2,1,0:T(8,128)S(1)}, f32[2,128,256]{2,1,0:T(8,128)S(1)}, u32[]{:S(2)}, u32[]{:S(2)}) %collective-permute-start) | collective-permute-done | bytes 262176 | tf_op jit(solution)/shard_map/ppermute | solution.py:31
  14.6 0.0 collective-permute-start.1
  14.6 0.0 collective-permute-done.2.refs_0_
  14.6 2.6 %collective-permute-start.3 = (f32[128,256]{1,0:T(8,128)S(1)}, f32[128,256]{1,0:T(8,128)S(1)}, u32[]{:S(2)}, u32[]{:S(2)}) collective-permute-start(f32[128,256]{1,0:T(8,128)S(1)} %collective-permute-done.2.refs_0_), channel_id=1, source_target_pairs={{0,16},{1,17},{2,18},{3,19},{4,20},{5,21},{6,22},{7,23},{8,24},{9,... | collective-permute-start | bytes 393224 | tf_op jit(solution)/shard_map/ppermute | solution.py:31
  17.2 0.7 collective-permute-start.4
  17.9 0.8 collective-permute-start.5
  18.7 1.8 %collective-permute-done.3.refs_1_ = f32[128,256]{1,0:T(8,128)S(1)} collective-permute-done((f32[128,256]{1,0:T(8,128)S(1)}, f32[128,256]{1,0:T(8,128)S(1)}, u32[]{:S(2)}, u32[]{:S(2)}) %collective-permute-start.3) | collective-permute-done | bytes 131104 | tf_op jit(solution)/shard_map/ppermute | solution.py:31
  20.5 2.8 %collective-permute-done.4.refs_2_ = f32[128,256]{1,0:T(8,128)S(1)} collective-permute-done((f32[128,256]{1,0:T(8,128)S(1)}, f32[128,256]{1,0:T(8,128)S(1)}, u32[]{:S(2)}, u32[]{:S(2)}) %collective-permute-start.4) | collective-permute-done | bytes 131104 | tf_op jit(solution)/shard_map/ppermute | solution.py:31
  23.3 1.9 %collective-permute-done.5.refs_3_ = f32[128,256]{1,0:T(8,128)S(1)} collective-permute-done((f32[128,256]{1,0:T(8,128)S(1)}, f32[128,256]{1,0:T(8,128)S(1)}, u32[]{:S(2)}, u32[]{:S(2)}) %collective-permute-start.5) | collective-permute-done | bytes 131104 | tf_op jit(solution)/shard_map/ppermute | solution.py:31
  25.2 0.6 shard_map.70
  25.8 0.1 collective-permute-start.8
  25.9 5.0 %collective-permute-start.9 = (f32[128,256]{1,0:T(8,128)S(1)}, f32[128,256]{1,0:T(8,128)S(1)}, u32[]{:S(2)}, u32[]{:S(2)}) collective-permute-start(f32[128,256]{1,0:T(8,128)S(1)} %shard_map.69.refs_0_), channel_id=1, source_target_pairs={{0,4},{1,5},{2,6},{3,7},{4,0},{5,1},{6,2},{7,3},{8,12},{9,13},{10,... | collective-permute-start | bytes 393224 | tf_op jit(solution)/shard_map/ppermute | solution.py:31
  30.9 0.0 collective-permute-start.10
  30.9 2.4 %collective-permute-start.11 = (f32[128,256]{1,0:T(8,128)S(1)}, f32[128,256]{1,0:T(8,128)S(1)}, u32[]{:S(2)}, u32[]{:S(2)}) collective-permute-start(f32[128,256]{1,0:T(8,128)S(1)} %shard_map.69.refs_0_), channel_id=1, source_target_pairs={{0,12},{1,13},{2,14},{3,15},{4,8},{5,9},{6,10},{7,11},{8,4},{9,5},... | collective-permute-start | bytes 393224 | tf_op jit(solution)/shard_map/ppermute | solution.py:31
  33.3 2.3 %collective-permute-done.9.refs_1_ = f32[128,256]{1,0:T(8,128)S(1)} collective-permute-done((f32[128,256]{1,0:T(8,128)S(1)}, f32[128,256]{1,0:T(8,128)S(1)}, u32[]{:S(2)}, u32[]{:S(2)}) %collective-permute-start.9) | collective-permute-done | bytes 131104 | tf_op jit(solution)/shard_map/ppermute | solution.py:31
  35.7 7.8 %collective-permute-done.10.refs_2_ = f32[128,256]{1,0:T(8,128)S(1)} collective-permute-done((f32[128,256]{1,0:T(8,128)S(1)}, f32[128,256]{1,0:T(8,128)S(1)}, u32[]{:S(2)}, u32[]{:S(2)}) %collective-permute-start.10) | collective-permute-done | bytes 131104 | tf_op jit(solution)/shard_map/ppermute | solution.py:31
  43.5 0.5 collective-permute-start.14
  44.0 1.7 %shard_map.71.refs_4_ = f32[128,256]{1,0:T(8,128)S(1)} custom-call(f32[128,512]{1,0:T(8,128)} %factor_ref.3, f32[512,512]{1,0:T(8,128)} %normalizer_ref.3), custom_call_target="tpu_custom_call" | custom-call | bytes 1441792 | tf_op jit(solution)/shard_map/pallas_call | solution.py:241
  45.8 0.9 %shard_map.72 = (f32[136,128]{1,0:T(8,128)S(1)}, f32[136,128]{1,0:T(8,128)S(1)}, f32[136,128]{1,0:T(8,128)S(1)}, f32[136,128]{1,0:T(8,128)S(1)}) custom-call(f32[4,128,256]{2,1,0:T(8,128)S(1)} %get-tuple-element.12.share_ref, f32[4,128,256]{2,1,0:T(8,128)S(1)} %collective-permute-done.8.other_ref, f32[128,256]{1,0:T(8,128)S(1)} %shard_map.69.refs_0_, ...), custom_call_target="tpu_custom_call" | custom-call | flops 402653184 | bytes 2375680 | tf_op jit(solution)/shard_map/pallas_call | solution.py:241
  46.7 1.5 %collective-permute-start.17 = (f32[136,128]{1,0:T(8,128)S(1)}, f32[136,128]{1,0:T(8,128)S(1)}, u32[]{:S(2)}, u32[]{:S(2)}) collective-permute-start(f32[136,128]{1,0:T(8,128)S(1)} %get-tuple-element.17), channel_id=1, source_target_pairs={{0,18},{1,19},{2,16},{3,17},{4,22},{5,23},{6,20},{7,21},{8,26},{9,... | collective-permute-start | bytes 208904 | tf_op jit(solution)/shard_map/ppermute | solution.py:31
  48.3 1.5 %collective-permute-start.15 = (f32[136,128]{1,0:T(8,128)S(1)}, f32[136,128]{1,0:T(8,128)S(1)}, u32[]{:S(2)}, u32[]{:S(2)}) collective-permute-start(f32[136,128]{1,0:T(8,128)S(1)} %get-tuple-element.15), channel_id=1, source_target_pairs={{0,2},{1,3},{2,0},{3,1},{4,6},{5,7},{6,4},{7,5},{8,10},{9,11},{10,... | collective-permute-start | bytes 208904 | tf_op jit(solution)/shard_map/ppermute | solution.py:31
  49.7 0.5 collective-permute-start.16
  50.3 2.3 %collective-permute-done.17 = f32[136,128]{1,0:T(8,128)S(1)} collective-permute-done((f32[136,128]{1,0:T(8,128)S(1)}, f32[136,128]{1,0:T(8,128)S(1)}, u32[]{:S(2)}, u32[]{:S(2)}) %collective-permute-start.17) | collective-permute-done | bytes 69664 | tf_op jit(solution)/shard_map/ppermute | solution.py:31
  52.6 0.7 collective-permute-done.15
  53.3 0.8 collective-permute-done.16
  54.1 0.6 collective-permute-start.20
  54.6 2.0 %collective-permute-start.18 = (f32[136,128]{1,0:T(8,128)S(1)}, f32[136,128]{1,0:T(8,128)S(1)}, u32[]{:S(2)}, u32[]{:S(2)}) collective-permute-start(f32[136,128]{1,0:T(8,128)S(1)} %add_add_fusion.1), channel_id=1, source_target_pairs={{0,4},{1,5},{2,6},{3,7},{4,0},{5,1},{6,2},{7,3},{8,12},{9,13},{10,... | collective-permute-start | bytes 208904 | tf_op jit(solution)/shard_map/ppermute | solution.py:31
  56.7 1.8 %collective-permute-start.19 = (f32[136,128]{1,0:T(8,128)S(1)}, f32[136,128]{1,0:T(8,128)S(1)}, u32[]{:S(2)}, u32[]{:S(2)}) collective-permute-start(f32[136,128]{1,0:T(8,128)S(1)} %add_add_fusion.1), channel_id=1, source_target_pairs={{0,8},{1,9},{2,10},{3,11},{4,12},{5,13},{6,14},{7,15},{8,0},{9,1},... | collective-permute-start | bytes 208904 | tf_op jit(solution)/shard_map/ppermute | solution.py:31
  58.5 1.6 %collective-permute-start.6 = (f32[2,128,256]{2,1,0:T(8,128)S(1)}, f32[2,128,256]{2,1,0:T(8,128)S(1)}, u32[]{:S(2)}, u32[]{:S(2)}) collective-permute-start(f32[2,128,256]{2,1,0:T(8,128)S(1)} %get-tuple-element.13), channel_id=1, source_target_pairs={{0,4},{1,5},{2,6},{3,7},{4,0},{5,1},{6,2},{7,3},{8,12},{9,13},{10,... | collective-permute-start | bytes 786440 | tf_op jit(solution)/shard_map/ppermute | solution.py:31
  60.1 1.0 %collective-permute-done.20 = f32[136,128]{1,0:T(8,128)S(1)} collective-permute-done((f32[136,128]{1,0:T(8,128)S(1)}, f32[136,128]{1,0:T(8,128)S(1)}, u32[]{:S(2)}, u32[]{:S(2)}) %collective-permute-start.20) | collective-permute-done | bytes 69664 | tf_op jit(solution)/shard_map/ppermute | solution.py:31
  61.1 2.4 %collective-permute-done.19 = f32[136,128]{1,0:T(8,128)S(1)} collective-permute-done((f32[136,128]{1,0:T(8,128)S(1)}, f32[136,128]{1,0:T(8,128)S(1)}, u32[]{:S(2)}, u32[]{:S(2)}) %collective-permute-start.19) | collective-permute-done | bytes 69664 | tf_op jit(solution)/shard_map/ppermute | solution.py:31
  63.5 1.3 %collective-permute-start.23 = (f32[136,128]{1,0:T(8,128)S(1)}, f32[136,128]{1,0:T(8,128)S(1)}, u32[]{:S(2)}, u32[]{:S(2)}) collective-permute-start(f32[136,128]{1,0:T(8,128)S(1)} %add_add_fusion.refs_0_), channel_id=1, source_target_pairs={{0,18},{1,19},{2,16},{3,17},{4,22},{5,23},{6,20},{7,21},{8,26},{9,... | collective-permute-start | bytes 208904 | tf_op jit(solution)/shard_map/ppermute | solution.py:31
  64.9 1.1 %collective-permute-start.22 = (f32[136,128]{1,0:T(8,128)S(1)}, f32[136,128]{1,0:T(8,128)S(1)}, u32[]{:S(2)}, u32[]{:S(2)}) collective-permute-start(f32[136,128]{1,0:T(8,128)S(1)} %add_add_fusion.refs_0_), channel_id=1, source_target_pairs={{0,16},{1,17},{2,18},{3,19},{4,20},{5,21},{6,22},{7,23},{8,24},{9,... | collective-permute-start | bytes 208904 | tf_op jit(solution)/shard_map/ppermute | solution.py:31
  66.0 1.1 %collective-permute-start.21 = (f32[136,128]{1,0:T(8,128)S(1)}, f32[136,128]{1,0:T(8,128)S(1)}, u32[]{:S(2)}, u32[]{:S(2)}) collective-permute-start(f32[136,128]{1,0:T(8,128)S(1)} %add_add_fusion.refs_0_), channel_id=1, source_target_pairs={{0,2},{1,3},{2,0},{3,1},{4,6},{5,7},{6,4},{7,5},{8,10},{9,11},{10,... | collective-permute-start | bytes 208904 | tf_op jit(solution)/shard_map/ppermute | solution.py:31
  67.1 0.1 collective-permute-done.6
  67.2 0.0 copy-start
  67.2 2.0 %collective-permute-start.7 = (f32[128,256]{1,0:T(8,128)S(1)}, f32[128,256]{1,0:T(8,128)S(1)}, u32[]{:S(2)}, u32[]{:S(2)}) collective-permute-start(f32[128,256]{1,0:T(8,128)S(1)} %fusion), channel_id=1, source_target_pairs={{0,8},{1,9},{2,10},{3,11},{4,12},{5,13},{6,14},{7,15},{8,0},{9,1},... | collective-permute-start | bytes 393224 | tf_op jit(solution)/shard_map/ppermute | solution.py:31
  69.2 0.4 collective-permute-done.22.refs_2_
  69.6 0.7 collective-permute-done.21.refs_1_
  70.3 0.1 collective-permute-start.24
  70.4 4.4 %collective-permute-done.7 = f32[128,256]{1,0:T(8,128)S(1)} collective-permute-done((f32[128,256]{1,0:T(8,128)S(1)}, f32[128,256]{1,0:T(8,128)S(1)}, u32[]{:S(2)}, u32[]{:S(2)}) %collective-permute-start.7) | collective-permute-done | bytes 131104 | tf_op jit(solution)/shard_map/ppermute | solution.py:31
  74.8 0.7 fusion.3
  75.5 1.1 %shard_map.73 = f32[512,256]{1,0:T(8,128)} custom-call(f32[512,256]{1,0:T(8,128)S(1)} %copy-done, f32[256,128]{1,0:T(8,128)S(1)} %collective-permute-done.24.other_ref, f32[136,128]{1,0:T(8,128)S(1)} %add_add_fusion.refs_0_, f32[136,128]{1,0:T(8,128)S(1)} %collective-permute-done.21.refs_1_, f32[136,128]{1,0:T(8,128)S(1)} %collective-permute-done.22.refs_2_, ...), custom_call_target="tpu_custom_call" | custom-call | bytes 1458176 | tf_op jit(solution)/shard_map/pallas_call | solution.py:241
  (21 shorter events, 0.1 us)
Async XLA Ops:
  0.6 0.7 copy-start.1
  3.2 11.4 %collective-permute-start = (f32[2,128,256]{2,1,0:T(8,128)S(1)}, f32[2,128,256]{2,1,0:T(8,128)S(1)}, u32[]{:S(2)}, u32[]{:S(2)}) collective-permute-start(f32[2,128,256]{2,1,0:T(8,128)S(1)} %get-tuple-element.11), channel_id=1, source_target_pairs={{0,2},{1,3},{2,0},{3,1},{4,6},{5,7},{6,4},{7,5},{8,10},{9,11},{10,... | collective-permute-start | bytes 786440 | tf_op jit(solution)/shard_map/ppermute | solution.py:31
  7.9 6.6 %collective-permute-start.2 = (f32[128,256]{1,0:T(8,128)S(1)}, f32[128,256]{1,0:T(8,128)S(1)}, u32[]{:S(2)}, u32[]{:S(2)}) collective-permute-start(f32[128,256]{1,0:T(8,128)S(1)} %shard_map.69.refs_0_), channel_id=1, source_target_pairs={{0,0},{1,1},{2,16},{3,17},{4,2},{5,3},{6,18},{7,19},{8,4},{9,5},{1... | collective-permute-start | bytes 393224 | tf_op jit(solution)/shard_map/ppermute | solution.py:31
  14.6 10.6 %collective-permute-start.1 = (f32[2,128,256]{2,1,0:T(8,128)S(1)}, f32[2,128,256]{2,1,0:T(8,128)S(1)}, u32[]{:S(2)}, u32[]{:S(2)}) collective-permute-start(f32[2,128,256]{2,1,0:T(8,128)S(1)} %collective-permute-done.mine_ref), channel_id=1, source_target_pairs={{0,1},{1,0},{2,3},{3,2},{4,5},{5,4},{6,7},{7,6},{8,9},{9,8},{10,11... | collective-permute-start | bytes 786440 | tf_op jit(solution)/shard_map/ppermute | solution.py:31
  14.6 5.9 %collective-permute-start.3 = (f32[128,256]{1,0:T(8,128)S(1)}, f32[128,256]{1,0:T(8,128)S(1)}, u32[]{:S(2)}, u32[]{:S(2)}) collective-permute-start(f32[128,256]{1,0:T(8,128)S(1)} %collective-permute-done.2.refs_0_), channel_id=1, source_target_pairs={{0,16},{1,17},{2,18},{3,19},{4,20},{5,21},{6,22},{7,23},{8,24},{9,... | collective-permute-start | bytes 393224 | tf_op jit(solution)/shard_map/ppermute | solution.py:31
  17.2 6.1 %collective-permute-start.4 = (f32[128,256]{1,0:T(8,128)S(1)}, f32[128,256]{1,0:T(8,128)S(1)}, u32[]{:S(2)}, u32[]{:S(2)}) collective-permute-start(f32[128,256]{1,0:T(8,128)S(1)} %collective-permute-done.2.refs_0_), channel_id=1, source_target_pairs={{0,2},{1,3},{2,0},{3,1},{4,6},{5,7},{6,4},{7,5},{8,10},{9,11},{10,... | collective-permute-start | bytes 393224 | tf_op jit(solution)/shard_map/ppermute | solution.py:31
  17.9 7.3 %collective-permute-start.5 = (f32[128,256]{1,0:T(8,128)S(1)}, f32[128,256]{1,0:T(8,128)S(1)}, u32[]{:S(2)}, u32[]{:S(2)}) collective-permute-start(f32[128,256]{1,0:T(8,128)S(1)} %collective-permute-done.2.refs_0_), channel_id=1, source_target_pairs={{0,18},{1,19},{2,16},{3,17},{4,22},{5,23},{6,20},{7,21},{8,26},{9,... | collective-permute-start | bytes 393224 | tf_op jit(solution)/shard_map/ppermute | solution.py:31
  25.8 19.9 %collective-permute-start.8 = (f32[4,128,256]{2,1,0:T(8,128)S(1)}, f32[4,128,256]{2,1,0:T(8,128)S(1)}, u32[]{:S(2)}, u32[]{:S(2)}) collective-permute-start(f32[4,128,256]{2,1,0:T(8,128)S(1)} %get-tuple-element.12.share_ref), channel_id=1, source_target_pairs={{0,1},{1,0},{2,3},{3,2},{4,5},{5,4},{6,7},{7,6},{8,9},{9,8},{10,11... | collective-permute-start | bytes 1572872 | tf_op jit(solution)/shard_map/ppermute | solution.py:31
  25.9 9.7 %collective-permute-start.9 = (f32[128,256]{1,0:T(8,128)S(1)}, f32[128,256]{1,0:T(8,128)S(1)}, u32[]{:S(2)}, u32[]{:S(2)}) collective-permute-start(f32[128,256]{1,0:T(8,128)S(1)} %shard_map.69.refs_0_), channel_id=1, source_target_pairs={{0,4},{1,5},{2,6},{3,7},{4,0},{5,1},{6,2},{7,3},{8,12},{9,13},{10,... | collective-permute-start | bytes 393224 | tf_op jit(solution)/shard_map/ppermute | solution.py:31
  30.9 12.6 %collective-permute-start.10 = (f32[128,256]{1,0:T(8,128)S(1)}, f32[128,256]{1,0:T(8,128)S(1)}, u32[]{:S(2)}, u32[]{:S(2)}) collective-permute-start(f32[128,256]{1,0:T(8,128)S(1)} %shard_map.69.refs_0_), channel_id=1, source_target_pairs={{0,8},{1,9},{2,10},{3,11},{4,12},{5,13},{6,14},{7,15},{8,0},{9,1},... | collective-permute-start | bytes 393224 | tf_op jit(solution)/shard_map/ppermute | solution.py:31
  30.9 12.6 %collective-permute-start.11 = (f32[128,256]{1,0:T(8,128)S(1)}, f32[128,256]{1,0:T(8,128)S(1)}, u32[]{:S(2)}, u32[]{:S(2)}) collective-permute-start(f32[128,256]{1,0:T(8,128)S(1)} %shard_map.69.refs_0_), channel_id=1, source_target_pairs={{0,12},{1,13},{2,14},{3,15},{4,8},{5,9},{6,10},{7,11},{8,4},{9,5},... | collective-permute-start | bytes 393224 | tf_op jit(solution)/shard_map/ppermute | solution.py:31
  35.7 10.1 %collective-permute-start.12 = (f32[128,256]{1,0:T(8,128)S(1)}, f32[128,256]{1,0:T(8,128)S(1)}, u32[]{:S(2)}, u32[]{:S(2)}) collective-permute-start(f32[128,256]{1,0:T(8,128)S(1)} %collective-permute-done.9.refs_1_), channel_id=1, source_target_pairs={{0,1},{1,0},{2,3},{3,2},{4,5},{5,4},{6,7},{7,6},{8,9},{9,8},{10,11... | collective-permute-start | bytes 393224 | tf_op jit(solution)/shard_map/ppermute | solution.py:31
  43.5 2.3 %collective-permute-start.13 = (f32[128,256]{1,0:T(8,128)S(1)}, f32[128,256]{1,0:T(8,128)S(1)}, u32[]{:S(2)}, u32[]{:S(2)}) collective-permute-start(f32[128,256]{1,0:T(8,128)S(1)} %collective-permute-done.10.refs_2_), channel_id=1, source_target_pairs={{0,1},{1,0},{2,3},{3,2},{4,5},{5,4},{6,7},{7,6},{8,9},{9,8},{10,11... | collective-permute-start | bytes 393224 | tf_op jit(solution)/shard_map/ppermute | solution.py:31
  43.5 2.3 %collective-permute-start.14 = (f32[128,256]{1,0:T(8,128)S(1)}, f32[128,256]{1,0:T(8,128)S(1)}, u32[]{:S(2)}, u32[]{:S(2)}) collective-permute-start(f32[128,256]{1,0:T(8,128)S(1)} %collective-permute-done.11.refs_3_), channel_id=1, source_target_pairs={{0,1},{1,0},{2,3},{3,2},{4,5},{5,4},{6,7},{7,6},{8,9},{9,8},{10,11... | collective-permute-start | bytes 393224 | tf_op jit(solution)/shard_map/ppermute | solution.py:31
  46.7 5.9 %collective-permute-start.17 = (f32[136,128]{1,0:T(8,128)S(1)}, f32[136,128]{1,0:T(8,128)S(1)}, u32[]{:S(2)}, u32[]{:S(2)}) collective-permute-start(f32[136,128]{1,0:T(8,128)S(1)} %get-tuple-element.17), channel_id=1, source_target_pairs={{0,18},{1,19},{2,16},{3,17},{4,22},{5,23},{6,20},{7,21},{8,26},{9,... | collective-permute-start | bytes 208904 | tf_op jit(solution)/shard_map/ppermute | solution.py:31
  48.3 5.0 %collective-permute-start.15 = (f32[136,128]{1,0:T(8,128)S(1)}, f32[136,128]{1,0:T(8,128)S(1)}, u32[]{:S(2)}, u32[]{:S(2)}) collective-permute-start(f32[136,128]{1,0:T(8,128)S(1)} %get-tuple-element.15), channel_id=1, source_target_pairs={{0,2},{1,3},{2,0},{3,1},{4,6},{5,7},{6,4},{7,5},{8,10},{9,11},{10,... | collective-permute-start | bytes 208904 | tf_op jit(solution)/shard_map/ppermute | solution.py:31
  49.7 4.3 %collective-permute-start.16 = (f32[136,128]{1,0:T(8,128)S(1)}, f32[136,128]{1,0:T(8,128)S(1)}, u32[]{:S(2)}, u32[]{:S(2)}) collective-permute-start(f32[136,128]{1,0:T(8,128)S(1)} %get-tuple-element.16), channel_id=1, source_target_pairs={{0,16},{1,17},{2,18},{3,19},{4,20},{5,21},{6,22},{7,23},{8,24},{9,... | collective-permute-start | bytes 208904 | tf_op jit(solution)/shard_map/ppermute | solution.py:31
  54.1 7.0 %collective-permute-start.20 = (f32[136,128]{1,0:T(8,128)S(1)}, f32[136,128]{1,0:T(8,128)S(1)}, u32[]{:S(2)}, u32[]{:S(2)}) collective-permute-start(f32[136,128]{1,0:T(8,128)S(1)} %add_add_fusion.1), channel_id=1, source_target_pairs={{0,12},{1,13},{2,14},{3,15},{4,8},{5,9},{6,10},{7,11},{8,4},{9,5},... | collective-permute-start | bytes 208904 | tf_op jit(solution)/shard_map/ppermute | solution.py:31
  54.6 6.5 %collective-permute-start.18 = (f32[136,128]{1,0:T(8,128)S(1)}, f32[136,128]{1,0:T(8,128)S(1)}, u32[]{:S(2)}, u32[]{:S(2)}) collective-permute-start(f32[136,128]{1,0:T(8,128)S(1)} %add_add_fusion.1), channel_id=1, source_target_pairs={{0,4},{1,5},{2,6},{3,7},{4,0},{5,1},{6,2},{7,3},{8,12},{9,13},{10,... | collective-permute-start | bytes 208904 | tf_op jit(solution)/shard_map/ppermute | solution.py:31
  56.7 6.8 %collective-permute-start.19 = (f32[136,128]{1,0:T(8,128)S(1)}, f32[136,128]{1,0:T(8,128)S(1)}, u32[]{:S(2)}, u32[]{:S(2)}) collective-permute-start(f32[136,128]{1,0:T(8,128)S(1)} %add_add_fusion.1), channel_id=1, source_target_pairs={{0,8},{1,9},{2,10},{3,11},{4,12},{5,13},{6,14},{7,15},{8,0},{9,1},... | collective-permute-start | bytes 208904 | tf_op jit(solution)/shard_map/ppermute | solution.py:31
  58.5 8.6 %collective-permute-start.6 = (f32[2,128,256]{2,1,0:T(8,128)S(1)}, f32[2,128,256]{2,1,0:T(8,128)S(1)}, u32[]{:S(2)}, u32[]{:S(2)}) collective-permute-start(f32[2,128,256]{2,1,0:T(8,128)S(1)} %get-tuple-element.13), channel_id=1, source_target_pairs={{0,4},{1,5},{2,6},{3,7},{4,0},{5,1},{6,2},{7,3},{8,12},{9,13},{10,... | collective-permute-start | bytes 786440 | tf_op jit(solution)/shard_map/ppermute | solution.py:31
  63.5 5.7 %collective-permute-start.23 = (f32[136,128]{1,0:T(8,128)S(1)}, f32[136,128]{1,0:T(8,128)S(1)}, u32[]{:S(2)}, u32[]{:S(2)}) collective-permute-start(f32[136,128]{1,0:T(8,128)S(1)} %add_add_fusion.refs_0_), channel_id=1, source_target_pairs={{0,18},{1,19},{2,16},{3,17},{4,22},{5,23},{6,20},{7,21},{8,26},{9,... | collective-permute-start | bytes 208904 | tf_op jit(solution)/shard_map/ppermute | solution.py:31
  64.9 4.8 %collective-permute-start.22 = (f32[136,128]{1,0:T(8,128)S(1)}, f32[136,128]{1,0:T(8,128)S(1)}, u32[]{:S(2)}, u32[]{:S(2)}) collective-permute-start(f32[136,128]{1,0:T(8,128)S(1)} %add_add_fusion.refs_0_), channel_id=1, source_target_pairs={{0,16},{1,17},{2,18},{3,19},{4,20},{5,21},{6,22},{7,23},{8,24},{9,... | collective-permute-start | bytes 208904 | tf_op jit(solution)/shard_map/ppermute | solution.py:31
  66.0 4.3 %collective-permute-start.21 = (f32[136,128]{1,0:T(8,128)S(1)}, f32[136,128]{1,0:T(8,128)S(1)}, u32[]{:S(2)}, u32[]{:S(2)}) collective-permute-start(f32[136,128]{1,0:T(8,128)S(1)} %add_add_fusion.refs_0_), channel_id=1, source_target_pairs={{0,2},{1,3},{2,0},{3,1},{4,6},{5,7},{6,4},{7,5},{8,10},{9,11},{10,... | collective-permute-start | bytes 208904 | tf_op jit(solution)/shard_map/ppermute | solution.py:31
  67.2 8.3 %copy-start = (f32[512,256]{1,0:T(8,128)S(1)}, f32[512,256]{1,0:T(8,128)}, u32[]{:S(2)}) copy-start(f32[512,256]{1,0:T(8,128)} %pivot_ref.1) | copy-start | bytes 1572868
  67.2 7.6 %collective-permute-start.7 = (f32[128,256]{1,0:T(8,128)S(1)}, f32[128,256]{1,0:T(8,128)S(1)}, u32[]{:S(2)}, u32[]{:S(2)}) collective-permute-start(f32[128,256]{1,0:T(8,128)S(1)} %fusion), channel_id=1, source_target_pairs={{0,8},{1,9},{2,10},{3,11},{4,12},{5,13},{6,14},{7,15},{8,0},{9,1},... | collective-permute-start | bytes 393224 | tf_op jit(solution)/shard_map/ppermute | solution.py:31
  70.3 5.2 %collective-permute-start.24 = (f32[256,128]{1,0:T(8,128)S(1)}, f32[256,128]{1,0:T(8,128)S(1)}, u32[]{:S(2)}, u32[]{:S(2)}) collective-permute-start(f32[256,128]{1,0:T(8,128)S(1)} %pad_maximum_fusion), channel_id=1, source_target_pairs={{0,1},{1,0},{2,3},{3,2},{4,5},{5,4},{6,7},{7,6},{8,9},{9,8},{10,11... | collective-permute-start | bytes 393224 | tf_op jit(solution)/shard_map/ppermute | solution.py:31

commit v8 on v7

--- a/solution.py
+++ b/solution.py
@@ -175,8 +175,11 @@
         outs[k][4 * step :, :] = jnp.where(inside, trace, 0.0)
 
 
-def finish_kernel(members, pivot_ref, other_ref, *refs):
-    parts, out_ref, total_ref, between_ref = refs[:members], *refs[members:]
+def finish_kernel(members, summands, pivot_ref, *refs):
+    shares, refs = refs[:summands], refs[summands:]
+    parts, pieces = refs[:members], refs[members : 2 * members]
+    out_ref, columns_ref, total_ref, between_ref = refs[2 * members :]
+    columns_ref[...] = -sum(ref[...] for ref in shares[1:]) - shares[0][...]
     row, col, rep = here()
     place = row * PAIR + col % PAIR
     half = out_ref.shape[1]
@@ -188,8 +191,7 @@
         for i in range(4):
             total_ref[i, rows, :] = parts[k][i * step : (i + 1) * step, :]
         for i in range(2):
-            start = (2 * k + i) * step
-            between_ref[i, rows, :] = other_ref[start : start + step, :]
+            between_ref[i, rows, :] = pieces[k][i * step : (i + 1) * step, :]
         if k:
             trace = trace + parts[k][4 * step : 4 * step + 1, :]
     down, across = square(quarter)
@@ -313,8 +315,6 @@
     taken_shares = send(given_shares, along(1))
     halved = [product[k] + taken_shares[k // PAIR] for k in range(0, planes, PAIR)]
     landed = [send(halved[k], along(k * PAIR)) for k in range(1, planes // PAIR)]
-    ancestor_columns = -(halved[0] + sum(landed))
-
     quarter = half // 2
     step = quarter // members
     parts = call(
@@ -336,12 +336,12 @@
     part = parts[0] + sum(send(parts[k], in_plane(k)) for k in range(1, members))
     part = part + sum(send(part, along(k)) for k in range(1, planes))
     parts = [part] + [send(part, in_plane(k)) for k in range(1, members)]
-    other_between = swap_core(jnp.concatenate([one[2 * step : 4 * step] for one in parts], 0))
-    (diag_block,) = call(
-        functools.partial(finish_kernel, members),
-        [pivot_inverse.shape],
+    pieces = [swap_core(part[2 * step : 4 * step]) for part in parts]
+    diag_block, ancestor_columns = call(
+        functools.partial(finish_kernel, members, len(landed) + 1),
+        [pivot_inverse.shape, (tile, half)],
         "",
-        [pivot_inverse, other_between, *parts],
+        [pivot_inverse, halved[0], *landed, *parts, *pieces],
         [(4, quarter, quarter), (2, quarter, quarter)],
     )
     return ancestor_columns, diag_block

time: 76.8 us -> 76.6 us (level)
  waiting for transfers between devices: 35.3 us -> 37 us
  starting transfers between devices: 31 us -> 29.8 us
    ppermute x25 -> x28, waiting for transfers between devices: 35.3 us -> 37 us  [send(): return lax.ppermute(block, AXES, route)]
    ppermute x25 -> x28, starting transfers between devices: 31 us -> 29.8 us  [send(): return lax.ppermute(block, AXES, route)]
  transfers between devices with their start and end apart: 25 -> 28, of which waited for: 15 -> 17; matrix products, arithmetic and copies ran while one was open for 1% -> 0% of each run, Pallas kernels for 5% -> 5%
where the time goes in v8:
time: 76.6 us; the launch traced here: 76.4 us
  waiting for transfers between devices  37 us (48%)
  starting transfers between devices  29.8 us (39%)
  Pallas kernels  7.99 us (10%)
  between operations  0.79 us (1%)
    ppermute x28, waiting for transfers between devices, send(): return lax.ppermute(block, AXES, route)  37 us
    ppermute x28, starting transfers between devices, send(): return lax.ppermute(block, AXES, route)  29.8 us
    pallas_call x6, Pallas kernels, call(): pl.pallas_call(kernel, out_shape=[jax.ShapeDtypeStruct(shape, F32) for sh...  7.99 us
  transfers between devices with their start and end apart: 28, of which 17 were waited for; matrix products, arithmetic and copies ran while one was open for 0% of the time, Pallas kernels for 5%

profile of v8, /device:TPU:0, one launch (start us, length us, event | category | flops | bytes accessed | tf_op | source)
XLA Modules:
  0.0 76.4 jit_solution(16189723315594352511)
XLA Ops:
  0.6 0.7 copy-done.1
  1.3 1.9 %shard_map.68 = (f32[4,128,256]{2,1,0:T(8,128)S(1)}, f32[2,128,256]{2,1,0:T(8,128)S(1)}) custom-call(s32[2,8]{1,0:T(2,128)S(1)} %bitcast.5, f32[1024,256]{1,0:T(8,128)} %full_ref.1), custom_call_target="tpu_custom_call" | custom-call | bytes 1835072 | tf_op jit(solution)/shard_map/pallas_call | solution.py:243
  3.2 3.0 %collective-permute-start = (f32[2,128,256]{2,1,0:T(8,128)S(1)}, f32[2,128,256]{2,1,0:T(8,128)S(1)}, u32[]{:S(2)}, u32[]{:S(2)}) collective-permute-start(f32[2,128,256]{2,1,0:T(8,128)S(1)} %get-tuple-element.13), channel_id=1, source_target_pairs={{0,2},{1,3},{2,0},{3,1},{4,6},{5,7},{6,4},{7,5},{8,10},{9,11},{10,... | collective-permute-start | bytes 786440 | tf_op jit(solution)/shard_map/ppermute | solution.py:31
  6.2 1.7 %shard_map.69.refs_0_ = f32[128,256]{1,0:T(8,128)S(1)} custom-call(f32[128,512]{1,0:T(8,128)} %factor_ref.3, f32[512,512]{1,0:T(8,128)} %normalizer_ref.3), custom_call_target="tpu_custom_call" | custom-call | bytes 1441792 | tf_op jit(solution)/shard_map/pallas_call | solution.py:243
  7.9 0.7 collective-permute-start.2
  8.6 6.0 %collective-permute-done.mine_ref = f32[2,128,256]{2,1,0:T(8,128)S(1)} collective-permute-done((f32[2,128,256]{2,1,0:T(8,128)S(1)}, f32[2,128,256]{2,1,0:T(8,128)S(1)}, u32[]{:S(2)}, u32[]{:S(2)}) %collective-permute-start) | collective-permute-done | bytes 262176 | tf_op jit(solution)/shard_map/ppermute | solution.py:31
  14.6 0.0 collective-permute-start.1
  14.6 0.0 collective-permute-done.2.refs_0_
  14.6 2.6 %collective-permute-start.3 = (f32[128,256]{1,0:T(8,128)S(1)}, f32[128,256]{1,0:T(8,128)S(1)}, u32[]{:S(2)}, u32[]{:S(2)}) collective-permute-start(f32[128,256]{1,0:T(8,128)S(1)} %collective-permute-done.2.refs_0_), channel_id=1, source_target_pairs={{0,16},{1,17},{2,18},{3,19},{4,20},{5,21},{6,22},{7,23},{8,24},{9,... | collective-permute-start | bytes 393224 | tf_op jit(solution)/shard_map/ppermute | solution.py:31
  17.2 0.7 collective-permute-start.4
  17.9 0.8 collective-permute-start.5
  18.7 1.8 %collective-permute-done.3.refs_1_ = f32[128,256]{1,0:T(8,128)S(1)} collective-permute-done((f32[128,256]{1,0:T(8,128)S(1)}, f32[128,256]{1,0:T(8,128)S(1)}, u32[]{:S(2)}, u32[]{:S(2)}) %collective-permute-start.3) | collective-permute-done | bytes 131104 | tf_op jit(solution)/shard_map/ppermute | solution.py:31
  20.5 2.8 %collective-permute-done.4.refs_2_ = f32[128,256]{1,0:T(8,128)S(1)} collective-permute-done((f32[128,256]{1,0:T(8,128)S(1)}, f32[128,256]{1,0:T(8,128)S(1)}, u32[]{:S(2)}, u32[]{:S(2)}) %collective-permute-start.4) | collective-permute-done | bytes 131104 | tf_op jit(solution)/shard_map/ppermute | solution.py:31
  23.3 1.9 %collective-permute-done.5.refs_3_ = f32[128,256]{1,0:T(8,128)S(1)} collective-permute-done((f32[128,256]{1,0:T(8,128)S(1)}, f32[128,256]{1,0:T(8,128)S(1)}, u32[]{:S(2)}, u32[]{:S(2)}) %collective-permute-start.5) | collective-permute-done | bytes 131104 | tf_op jit(solution)/shard_map/ppermute | solution.py:31
  25.2 0.6 shard_map.70
  25.8 0.1 collective-permute-start.8
  25.9 5.0 %collective-permute-start.9 = (f32[128,256]{1,0:T(8,128)S(1)}, f32[128,256]{1,0:T(8,128)S(1)}, u32[]{:S(2)}, u32[]{:S(2)}) collective-permute-start(f32[128,256]{1,0:T(8,128)S(1)} %shard_map.69.refs_0_), channel_id=1, source_target_pairs={{0,4},{1,5},{2,6},{3,7},{4,0},{5,1},{6,2},{7,3},{8,12},{9,13},{10,... | collective-permute-start | bytes 393224 | tf_op jit(solution)/shard_map/ppermute | solution.py:31
  30.9 0.0 collective-permute-start.10
  30.9 2.4 %collective-permute-start.11 = (f32[128,256]{1,0:T(8,128)S(1)}, f32[128,256]{1,0:T(8,128)S(1)}, u32[]{:S(2)}, u32[]{:S(2)}) collective-permute-start(f32[128,256]{1,0:T(8,128)S(1)} %shard_map.69.refs_0_), channel_id=1, source_target_pairs={{0,12},{1,13},{2,14},{3,15},{4,8},{5,9},{6,10},{7,11},{8,4},{9,5},... | collective-permute-start | bytes 393224 | tf_op jit(solution)/shard_map/ppermute | solution.py:31
  33.3 2.3 %collective-permute-done.9.refs_1_ = f32[128,256]{1,0:T(8,128)S(1)} collective-permute-done((f32[128,256]{1,0:T(8,128)S(1)}, f32[128,256]{1,0:T(8,128)S(1)}, u32[]{:S(2)}, u32[]{:S(2)}) %collective-permute-start.9) | collective-permute-done | bytes 131104 | tf_op jit(solution)/shard_map/ppermute | solution.py:31
  35.7 0.0 collective-permute-start.12
  35.7 7.8 %collective-permute-done.10.refs_2_ = f32[128,256]{1,0:T(8,128)S(1)} collective-permute-done((f32[128,256]{1,0:T(8,128)S(1)}, f32[128,256]{1,0:T(8,128)S(1)}, u32[]{:S(2)}, u32[]{:S(2)}) %collective-permute-start.10) | collective-permute-done | bytes 131104 | tf_op jit(solution)/shard_map/ppermute | solution.py:31
  43.5 0.5 collective-permute-start.14
  44.0 1.7 %shard_map.71.refs_4_ = f32[128,256]{1,0:T(8,128)S(1)} custom-call(f32[128,512]{1,0:T(8,128)} %factor_ref.3, f32[512,512]{1,0:T(8,128)} %normalizer_ref.3), custom_call_target="tpu_custom_call" | custom-call | bytes 1441792 | tf_op jit(solution)/shard_map/pallas_call | solution.py:243
  45.8 0.9 %shard_map.72 = (f32[136,128]{1,0:T(8,128)S(1)}, f32[136,128]{1,0:T(8,128)S(1)}, f32[136,128]{1,0:T(8,128)S(1)}, f32[136,128]{1,0:T(8,128)S(1)}) custom-call(f32[4,128,256]{2,1,0:T(8,128)S(1)} %get-tuple-element.14.share_ref, f32[4,128,256]{2,1,0:T(8,128)S(1)} %collective-permute-done.8.other_ref, f32[128,256]{1,0:T(8,128)S(1)} %shard_map.69.refs_0_, ...), custom_call_target="tpu_custom_call" | custom-call | flops 402653184 | bytes 2375680 | tf_op jit(solution)/shard_map/pallas_call | solution.py:243
  46.7 1.5 %collective-permute-start.17 = (f32[136,128]{1,0:T(8,128)S(1)}, f32[136,128]{1,0:T(8,128)S(1)}, u32[]{:S(2)}, u32[]{:S(2)}) collective-permute-start(f32[136,128]{1,0:T(8,128)S(1)} %get-tuple-element.19), channel_id=1, source_target_pairs={{0,18},{1,19},{2,16},{3,17},{4,22},{5,23},{6,20},{7,21},{8,26},{9,... | collective-permute-start | bytes 208904 | tf_op jit(solution)/shard_map/ppermute | solution.py:31
  48.3 1.5 %collective-permute-start.15 = (f32[136,128]{1,0:T(8,128)S(1)}, f32[136,128]{1,0:T(8,128)S(1)}, u32[]{:S(2)}, u32[]{:S(2)}) collective-permute-start(f32[136,128]{1,0:T(8,128)S(1)} %get-tuple-element.17), channel_id=1, source_target_pairs={{0,2},{1,3},{2,0},{3,1},{4,6},{5,7},{6,4},{7,5},{8,10},{9,11},{10,... | collective-permute-start | bytes 208904 | tf_op jit(solution)/shard_map/ppermute | solution.py:31
  49.7 0.5 collective-permute-start.16
  50.3 2.4 %collective-permute-start.6 = (f32[2,128,256]{2,1,0:T(8,128)S(1)}, f32[2,128,256]{2,1,0:T(8,128)S(1)}, u32[]{:S(2)}, u32[]{:S(2)}) collective-permute-start(f32[2,128,256]{2,1,0:T(8,128)S(1)} %get-tuple-element.15), channel_id=1, source_target_pairs={{0,4},{1,5},{2,6},{3,7},{4,0},{5,1},{6,2},{7,3},{8,12},{9,13},{10,... | collective-permute-start | bytes 786440 | tf_op jit(solution)/shard_map/ppermute | solution.py:31
  52.6 0.7 collective-permute-done.15
  53.3 0.8 collective-permute-done.16
  54.1 0.0 copy-start
  54.1 0.6 collective-permute-start.20
  54.7 2.0 %collective-permute-start.18 = (f32[136,128]{1,0:T(8,128)S(1)}, f32[136,128]{1,0:T(8,128)S(1)}, u32[]{:S(2)}, u32[]{:S(2)}) collective-permute-start(f32[136,128]{1,0:T(8,128)S(1)} %add_add_fusion.1), channel_id=1, source_target_pairs={{0,4},{1,5},{2,6},{3,7},{4,0},{5,1},{6,2},{7,3},{8,12},{9,13},{10,... | collective-permute-start | bytes 208904 | tf_op jit(solution)/shard_map/ppermute | solution.py:31
  56.7 1.8 %collective-permute-start.19 = (f32[136,128]{1,0:T(8,128)S(1)}, f32[136,128]{1,0:T(8,128)S(1)}, u32[]{:S(2)}, u32[]{:S(2)}) collective-permute-start(f32[136,128]{1,0:T(8,128)S(1)} %add_add_fusion.1), channel_id=1, source_target_pairs={{0,8},{1,9},{2,10},{3,11},{4,12},{5,13},{6,14},{7,15},{8,0},{9,1},... | collective-permute-start | bytes 208904 | tf_op jit(solution)/shard_map/ppermute | solution.py:31
  58.5 2.9 %collective-permute-done.6 = f32[2,128,256]{2,1,0:T(8,128)S(1)} collective-permute-done((f32[2,128,256]{2,1,0:T(8,128)S(1)}, f32[2,128,256]{2,1,0:T(8,128)S(1)}, u32[]{:S(2)}, u32[]{:S(2)}) %collective-permute-start.6) | collective-permute-done | bytes 262176 | tf_op jit(solution)/shard_map/ppermute | solution.py:31
  61.5 0.1 collective-permute-start.7
  61.6 0.4 collective-permute-done.20
  62.0 0.6 collective-permute-done.18
  62.6 5.0 %collective-permute-done.19 = f32[136,128]{1,0:T(8,128)S(1)} collective-permute-done((f32[136,128]{1,0:T(8,128)S(1)}, f32[136,128]{1,0:T(8,128)S(1)}, u32[]{:S(2)}, u32[]{:S(2)}) %collective-permute-start.19) | collective-permute-done | bytes 69664 | tf_op jit(solution)/shard_map/ppermute | solution.py:31
  67.7 1.1 %collective-permute-start.21 = (f32[136,128]{1,0:T(8,128)S(1)}, f32[136,128]{1,0:T(8,128)S(1)}, u32[]{:S(2)}, u32[]{:S(2)}) collective-permute-start(f32[136,128]{1,0:T(8,128)S(1)} %add_add_fusion.refs_2_), channel_id=1, source_target_pairs={{0,2},{1,3},{2,0},{3,1},{4,6},{5,7},{6,4},{7,5},{8,10},{9,11},{10,... | collective-permute-start | bytes 208904 | tf_op jit(solution)/shard_map/ppermute | solution.py:31
  68.8 2.4 %collective-permute-start.23 = (f32[136,128]{1,0:T(8,128)S(1)}, f32[136,128]{1,0:T(8,128)S(1)}, u32[]{:S(2)}, u32[]{:S(2)}) collective-permute-start(f32[136,128]{1,0:T(8,128)S(1)} %add_add_fusion.refs_2_), channel_id=1, source_target_pairs={{0,18},{1,19},{2,16},{3,17},{4,22},{5,23},{6,20},{7,21},{8,26},{9,... | collective-permute-start | bytes 208904 | tf_op jit(solution)/shard_map/ppermute | solution.py:31
  71.2 0.8 %collective-permute-done.21.refs_3_ = f32[136,128]{1,0:T(8,128)S(1)} collective-permute-done((f32[136,128]{1,0:T(8,128)S(1)}, f32[136,128]{1,0:T(8,128)S(1)}, u32[]{:S(2)}, u32[]{:S(2)}) %collective-permute-start.21) | collective-permute-done | bytes 69664 | tf_op jit(solution)/shard_map/ppermute | solution.py:31
  72.0 1.1 %collective-permute-done.22.refs_4_ = f32[136,128]{1,0:T(8,128)S(1)} collective-permute-done((f32[136,128]{1,0:T(8,128)S(1)}, f32[136,128]{1,0:T(8,128)S(1)}, u32[]{:S(2)}, u32[]{:S(2)}) %collective-permute-start.22) | collective-permute-done | bytes 69664 | tf_op jit(solution)/shard_map/ppermute | solution.py:31
  73.1 0.9 %collective-permute-done.23.refs_5_ = f32[136,128]{1,0:T(8,128)S(1)} collective-permute-done((f32[136,128]{1,0:T(8,128)S(1)}, f32[136,128]{1,0:T(8,128)S(1)}, u32[]{:S(2)}, u32[]{:S(2)}) %collective-permute-start.23) | collective-permute-done | bytes 69664 | tf_op jit(solution)/shard_map/ppermute | solution.py:31
  74.0 0.3 collective-permute-done.26.refs_8_
  74.3 0.9 %collective-permute-done.27.refs_9_ = f32[64,128]{1,0:T(8,128)S(1)} collective-permute-done((f32[64,128]{1,0:T(8,128)S(1)}, f32[64,128]{1,0:T(8,128)S(1)}, u32[]{:S(2)}, u32[]{:S(2)}) %collective-permute-start.27) | collective-permute-done | bytes 32800 | tf_op jit(solution)/shard_map/ppermute | solution.py:31
  75.2 1.1 %shard_map.73 = (f32[512,256]{1,0:T(8,128)}, f32[128,256]{1,0:T(8,128)}) custom-call(f32[512,256]{1,0:T(8,128)S(1)} %copy-done, f32[128,256]{1,0:T(8,128)S(1)} %get-tuple-element.23.refs_0_, f32[128,256]{1,0:T(8,128)S(1)} %collective-permute-done.7.refs_1_, f32[136,128]{1,0:T(8,128)S(1)} %add_add_fusion.refs_2_, ...), custom_call_target="tpu_custom_call" | custom-call | bytes 1851392 | tf_op jit(solution)/shard_map/pallas_call | solution.py:243
  (25 shorter events, 0.1 us)
Async XLA Ops:
  0.6 0.7 copy-start.1
  3.2 11.4 %collective-permute-start = (f32[2,128,256]{2,1,0:T(8,128)S(1)}, f32[2,128,256]{2,1,0:T(8,128)S(1)}, u32[]{:S(2)}, u32[]{:S(2)}) collective-permute-start(f32[2,128,256]{2,1,0:T(8,128)S(1)} %get-tuple-element.13), channel_id=1, source_target_pairs={{0,2},{1,3},{2,0},{3,1},{4,6},{5,7},{6,4},{7,5},{8,10},{9,11},{10,... | collective-permute-start | bytes 786440 | tf_op jit(solution)/shard_map/ppermute | solution.py:31
  7.9 6.6 %collective-permute-start.2 = (f32[128,256]{1,0:T(8,128)S(1)}, f32[128,256]{1,0:T(8,128)S(1)}, u32[]{:S(2)}, u32[]{:S(2)}) collective-permute-start(f32[128,256]{1,0:T(8,128)S(1)} %shard_map.69.refs_0_), channel_id=1, source_target_pairs={{0,0},{1,1},{2,16},{3,17},{4,2},{5,3},{6,18},{7,19},{8,4},{9,5},{1... | collective-permute-start | bytes 393224 | tf_op jit(solution)/shard_map/ppermute | solution.py:31
  14.6 10.6 %collective-permute-start.1 = (f32[2,128,256]{2,1,0:T(8,128)S(1)}, f32[2,128,256]{2,1,0:T(8,128)S(1)}, u32[]{:S(2)}, u32[]{:S(2)}) collective-permute-start(f32[2,128,256]{2,1,0:T(8,128)S(1)} %collective-permute-done.mine_ref), channel_id=1, source_target_pairs={{0,1},{1,0},{2,3},{3,2},{4,5},{5,4},{6,7},{7,6},{8,9},{9,8},{10,11... | collective-permute-start | bytes 786440 | tf_op jit(solution)/shard_map/ppermute | solution.py:31
  14.6 5.9 %collective-permute-start.3 = (f32[128,256]{1,0:T(8,128)S(1)}, f32[128,256]{1,0:T(8,128)S(1)}, u32[]{:S(2)}, u32[]{:S(2)}) collective-permute-start(f32[128,256]{1,0:T(8,128)S(1)} %collective-permute-done.2.refs_0_), channel_id=1, source_target_pairs={{0,16},{1,17},{2,18},{3,19},{4,20},{5,21},{6,22},{7,23},{8,24},{9,... | collective-permute-start | bytes 393224 | tf_op jit(solution)/shard_map/ppermute | solution.py:31
  17.2 6.1 %collective-permute-start.4 = (f32[128,256]{1,0:T(8,128)S(1)}, f32[128,256]{1,0:T(8,128)S(1)}, u32[]{:S(2)}, u32[]{:S(2)}) collective-permute-start(f32[128,256]{1,0:T(8,128)S(1)} %collective-permute-done.2.refs_0_), channel_id=1, source_target_pairs={{0,2},{1,3},{2,0},{3,1},{4,6},{5,7},{6,4},{7,5},{8,10},{9,11},{10,... | collective-permute-start | bytes 393224 | tf_op jit(solution)/shard_map/ppermute | solution.py:31
  17.9 7.3 %collective-permute-start.5 = (f32[128,256]{1,0:T(8,128)S(1)}, f32[128,256]{1,0:T(8,128)S(1)}, u32[]{:S(2)}, u32[]{:S(2)}) collective-permute-start(f32[128,256]{1,0:T(8,128)S(1)} %collective-permute-done.2.refs_0_), channel_id=1, source_target_pairs={{0,18},{1,19},{2,16},{3,17},{4,22},{5,23},{6,20},{7,21},{8,26},{9,... | collective-permute-start | bytes 393224 | tf_op jit(solution)/shard_map/ppermute | solution.py:31
  25.8 19.9 %collective-permute-start.8 = (f32[4,128,256]{2,1,0:T(8,128)S(1)}, f32[4,128,256]{2,1,0:T(8,128)S(1)}, u32[]{:S(2)}, u32[]{:S(2)}) collective-permute-start(f32[4,128,256]{2,1,0:T(8,128)S(1)} %get-tuple-element.14.share_ref), channel_id=1, source_target_pairs={{0,1},{1,0},{2,3},{3,2},{4,5},{5,4},{6,7},{7,6},{8,9},{9,8},{10,11... | collective-permute-start | bytes 1572872 | tf_op jit(solution)/shard_map/ppermute | solution.py:31
  25.9 9.7 %collective-permute-start.9 = (f32[128,256]{1,0:T(8,128)S(1)}, f32[128,256]{1,0:T(8,128)S(1)}, u32[]{:S(2)}, u32[]{:S(2)}) collective-permute-start(f32[128,256]{1,0:T(8,128)S(1)} %shard_map.69.refs_0_), channel_id=1, source_target_pairs={{0,4},{1,5},{2,6},{3,7},{4,0},{5,1},{6,2},{7,3},{8,12},{9,13},{10,... | collective-permute-start | bytes 393224 | tf_op jit(solution)/shard_map/ppermute | solution.py:31
  30.9 12.6 %collective-permute-start.10 = (f32[128,256]{1,0:T(8,128)S(1)}, f32[128,256]{1,0:T(8,128)S(1)}, u32[]{:S(2)}, u32[]{:S(2)}) collective-permute-start(f32[128,256]{1,0:T(8,128)S(1)} %shard_map.69.refs_0_), channel_id=1, source_target_pairs={{0,8},{1,9},{2,10},{3,11},{4,12},{5,13},{6,14},{7,15},{8,0},{9,1},... | collective-permute-start | bytes 393224 | tf_op jit(solution)/shard_map/ppermute | solution.py:31
  30.9 12.6 %collective-permute-start.11 = (f32[128,256]{1,0:T(8,128)S(1)}, f32[128,256]{1,0:T(8,128)S(1)}, u32[]{:S(2)}, u32[]{:S(2)}) collective-permute-start(f32[128,256]{1,0:T(8,128)S(1)} %shard_map.69.refs_0_), channel_id=1, source_target_pairs={{0,12},{1,13},{2,14},{3,15},{4,8},{5,9},{6,10},{7,11},{8,4},{9,5},... | collective-permute-start | bytes 393224 | tf_op jit(solution)/shard_map/ppermute | solution.py:31
  35.7 10.1 %collective-permute-start.12 = (f32[128,256]{1,0:T(8,128)S(1)}, f32[128,256]{1,0:T(8,128)S(1)}, u32[]{:S(2)}, u32[]{:S(2)}) collective-permute-start(f32[128,256]{1,0:T(8,128)S(1)} %collective-permute-done.9.refs_1_), channel_id=1, source_target_pairs={{0,1},{1,0},{2,3},{3,2},{4,5},{5,4},{6,7},{7,6},{8,9},{9,8},{10,11... | collective-permute-start | bytes 393224 | tf_op jit(solution)/shard_map/ppermute | solution.py:31
  43.5 2.3 %collective-permute-start.13 = (f32[128,256]{1,0:T(8,128)S(1)}, f32[128,256]{1,0:T(8,128)S(1)}, u32[]{:S(2)}, u32[]{:S(2)}) collective-permute-start(f32[128,256]{1,0:T(8,128)S(1)} %collective-permute-done.10.refs_2_), channel_id=1, source_target_pairs={{0,1},{1,0},{2,3},{3,2},{4,5},{5,4},{6,7},{7,6},{8,9},{9,8},{10,11... | collective-permute-start | bytes 393224 | tf_op jit(solution)/shard_map/ppermute | solution.py:31
  43.5 2.3 %collective-permute-start.14 = (f32[128,256]{1,0:T(8,128)S(1)}, f32[128,256]{1,0:T(8,128)S(1)}, u32[]{:S(2)}, u32[]{:S(2)}) collective-permute-start(f32[128,256]{1,0:T(8,128)S(1)} %collective-permute-done.11.refs_3_), channel_id=1, source_target_pairs={{0,1},{1,0},{2,3},{3,2},{4,5},{5,4},{6,7},{7,6},{8,9},{9,8},{10,11... | collective-permute-start | bytes 393224 | tf_op jit(solution)/shard_map/ppermute | solution.py:31
  46.7 5.9 %collective-permute-start.17 = (f32[136,128]{1,0:T(8,128)S(1)}, f32[136,128]{1,0:T(8,128)S(1)}, u32[]{:S(2)}, u32[]{:S(2)}) collective-permute-start(f32[136,128]{1,0:T(8,128)S(1)} %get-tuple-element.19), channel_id=1, source_target_pairs={{0,18},{1,19},{2,16},{3,17},{4,22},{5,23},{6,20},{7,21},{8,26},{9,... | collective-permute-start | bytes 208904 | tf_op jit(solution)/shard_map/ppermute | solution.py:31
  48.3 5.0 %collective-permute-start.15 = (f32[136,128]{1,0:T(8,128)S(1)}, f32[136,128]{1,0:T(8,128)S(1)}, u32[]{:S(2)}, u32[]{:S(2)}) collective-permute-start(f32[136,128]{1,0:T(8,128)S(1)} %get-tuple-element.17), channel_id=1, source_target_pairs={{0,2},{1,3},{2,0},{3,1},{4,6},{5,7},{6,4},{7,5},{8,10},{9,11},{10,... | collective-permute-start | bytes 208904 | tf_op jit(solution)/shard_map/ppermute | solution.py:31
  49.7 4.3 %collective-permute-start.16 = (f32[136,128]{1,0:T(8,128)S(1)}, f32[136,128]{1,0:T(8,128)S(1)}, u32[]{:S(2)}, u32[]{:S(2)}) collective-permute-start(f32[136,128]{1,0:T(8,128)S(1)} %get-tuple-element.18), channel_id=1, source_target_pairs={{0,16},{1,17},{2,18},{3,19},{4,20},{5,21},{6,22},{7,23},{8,24},{9,... | collective-permute-start | bytes 208904 | tf_op jit(solution)/shard_map/ppermute | solution.py:31
  50.3 11.2 %collective-permute-start.6 = (f32[2,128,256]{2,1,0:T(8,128)S(1)}, f32[2,128,256]{2,1,0:T(8,128)S(1)}, u32[]{:S(2)}, u32[]{:S(2)}) collective-permute-start(f32[2,128,256]{2,1,0:T(8,128)S(1)} %get-tuple-element.15), channel_id=1, source_target_pairs={{0,4},{1,5},{2,6},{3,7},{4,0},{5,1},{6,2},{7,3},{8,12},{9,13},{10,... | collective-permute-start | bytes 786440 | tf_op jit(solution)/shard_map/ppermute | solution.py:31
  54.1 21.1 %copy-start = (f32[512,256]{1,0:T(8,128)S(1)}, f32[512,256]{1,0:T(8,128)}, u32[]{:S(2)}) copy-start(f32[512,256]{1,0:T(8,128)} %pivot_ref.1) | copy-start | bytes 1572868
  54.1 7.9 %collective-permute-start.20 = (f32[136,128]{1,0:T(8,128)S(1)}, f32[136,128]{1,0:T(8,128)S(1)}, u32[]{:S(2)}, u32[]{:S(2)}) collective-permute-start(f32[136,128]{1,0:T(8,128)S(1)} %add_add_fusion.1), channel_id=1, source_target_pairs={{0,12},{1,13},{2,14},{3,15},{4,8},{5,9},{6,10},{7,11},{8,4},{9,5},... | collective-permute-start | bytes 208904 | tf_op jit(solution)/shard_map/ppermute | solution.py:31
  54.7 7.9 %collective-permute-start.18 = (f32[136,128]{1,0:T(8,128)S(1)}, f32[136,128]{1,0:T(8,128)S(1)}, u32[]{:S(2)}, u32[]{:S(2)}) collective-permute-start(f32[136,128]{1,0:T(8,128)S(1)} %add_add_fusion.1), channel_id=1, source_target_pairs={{0,4},{1,5},{2,6},{3,7},{4,0},{5,1},{6,2},{7,3},{8,12},{9,13},{10,... | collective-permute-start | bytes 208904 | tf_op jit(solution)/shard_map/ppermute | solution.py:31
  56.7 11.0 %collective-permute-start.19 = (f32[136,128]{1,0:T(8,128)S(1)}, f32[136,128]{1,0:T(8,128)S(1)}, u32[]{:S(2)}, u32[]{:S(2)}) collective-permute-start(f32[136,128]{1,0:T(8,128)S(1)} %add_add_fusion.1), channel_id=1, source_target_pairs={{0,8},{1,9},{2,10},{3,11},{4,12},{5,13},{6,14},{7,15},{8,0},{9,1},... | collective-permute-start | bytes 208904 | tf_op jit(solution)/shard_map/ppermute | solution.py:31
  61.5 12.5 %collective-permute-start.7 = (f32[128,256]{1,0:T(8,128)S(1)}, f32[128,256]{1,0:T(8,128)S(1)}, u32[]{:S(2)}, u32[]{:S(2)}) collective-permute-start(f32[128,256]{1,0:T(8,128)S(1)} %get-tuple-element.22), channel_id=1, source_target_pairs={{0,8},{1,9},{2,10},{3,11},{4,12},{5,13},{6,14},{7,15},{8,0},{9,1},... | collective-permute-start | bytes 393224 | tf_op jit(solution)/shard_map/ppermute | solution.py:31
  67.7 4.4 %collective-permute-start.21 = (f32[136,128]{1,0:T(8,128)S(1)}, f32[136,128]{1,0:T(8,128)S(1)}, u32[]{:S(2)}, u32[]{:S(2)}) collective-permute-start(f32[136,128]{1,0:T(8,128)S(1)} %add_add_fusion.refs_2_), channel_id=1, source_target_pairs={{0,2},{1,3},{2,0},{3,1},{4,6},{5,7},{6,4},{7,5},{8,10},{9,11},{10,... | collective-permute-start | bytes 208904 | tf_op jit(solution)/shard_map/ppermute | solution.py:31
  68.8 4.3 %collective-permute-start.22 = (f32[136,128]{1,0:T(8,128)S(1)}, f32[136,128]{1,0:T(8,128)S(1)}, u32[]{:S(2)}, u32[]{:S(2)}) collective-permute-start(f32[136,128]{1,0:T(8,128)S(1)} %add_add_fusion.refs_2_), channel_id=1, source_target_pairs={{0,16},{1,17},{2,18},{3,19},{4,20},{5,21},{6,22},{7,23},{8,24},{9,... | collective-permute-start | bytes 208904 | tf_op jit(solution)/shard_map/ppermute | solution.py:31
  68.8 5.2 %collective-permute-start.23 = (f32[136,128]{1,0:T(8,128)S(1)}, f32[136,128]{1,0:T(8,128)S(1)}, u32[]{:S(2)}, u32[]{:S(2)}) collective-permute-start(f32[136,128]{1,0:T(8,128)S(1)} %add_add_fusion.refs_2_), channel_id=1, source_target_pairs={{0,18},{1,19},{2,16},{3,17},{4,22},{5,23},{6,20},{7,21},{8,26},{9,... | collective-permute-start | bytes 208904 | tf_op jit(solution)/shard_map/ppermute | solution.py:31
  71.2 2.8 %collective-permute-start.24 = (f32[64,128]{1,0:T(8,128)S(1)}, f32[64,128]{1,0:T(8,128)S(1)}, u32[]{:S(2)}, u32[]{:S(2)}) collective-permute-start(f32[64,128]{1,0:T(8,128)S(1)} %slice.34), channel_id=1, source_target_pairs={{0,1},{1,0},{2,3},{3,2},{4,5},{5,4},{6,7},{7,6},{8,9},{9,8},{10,11... | collective-permute-start | bytes 98312 | tf_op jit(solution)/shard_map/ppermute | solution.py:31
  72.0 2.0 %collective-permute-start.25 = (f32[64,128]{1,0:T(8,128)S(1)}, f32[64,128]{1,0:T(8,128)S(1)}, u32[]{:S(2)}, u32[]{:S(2)}) collective-permute-start(f32[64,128]{1,0:T(8,128)S(1)} %slice.35), channel_id=1, source_target_pairs={{0,1},{1,0},{2,3},{3,2},{4,5},{5,4},{6,7},{7,6},{8,9},{9,8},{10,11... | collective-permute-start | bytes 98312 | tf_op jit(solution)/shard_map/ppermute | solution.py:31
  73.1 1.2 %collective-permute-start.26 = (f32[64,128]{1,0:T(8,128)S(1)}, f32[64,128]{1,0:T(8,128)S(1)}, u32[]{:S(2)}, u32[]{:S(2)}) collective-permute-start(f32[64,128]{1,0:T(8,128)S(1)} %slice.36), channel_id=1, source_target_pairs={{0,1},{1,0},{2,3},{3,2},{4,5},{5,4},{6,7},{7,6},{8,9},{9,8},{10,11... | collective-permute-start | bytes 98312 | tf_op jit(solution)/shard_map/ppermute | solution.py:31
  74.0 1.2 %collective-permute-start.27 = (f32[64,128]{1,0:T(8,128)S(1)}, f32[64,128]{1,0:T(8,128)S(1)}, u32[]{:S(2)}, u32[]{:S(2)}) collective-permute-start(f32[64,128]{1,0:T(8,128)S(1)} %slice.37), channel_id=1, source_target_pairs={{0,1},{1,0},{2,3},{3,2},{4,5},{5,4},{6,7},{7,6},{8,9},{9,8},{10,11... | collective-permute-start | bytes 98312 | tf_op jit(solution)/shard_map/ppermute | solution.py:31

commit v9 on v8

--- a/solution.py
+++ b/solution.py
@@ -100,24 +100,28 @@
     band = PAIR * tile
     copies = load_all(
         [
-            (full_ref.at[tile_at(plane ^ k, band), :], full_in.at[k], sems.at[k])
-            for k in range(planes)
+            (
+                full_ref.at[pl.ds(i * planes * band // 2, planes * band // 2), :],
+                full_in.at[pl.ds(i * planes * band // 2, planes * band // 2), :],
+                sems.at[i],
+            )
+            for i in range(2)
         ]
     )
+    for copy in copies:
+        copy.wait()
 
     def masked(k, wanted, m):
         across = row ^ m
         mark = marks_ref[across, (plane ^ k) * PAIR + wanted].astype(F32)
-        return full_in[k, tile_at(wanted, tile), tile_at(across, tile)] * mark
+        source = (plane ^ k) * PAIR + wanted
+        return full_in[tile_at(source, tile), tile_at(across, tile)] * mark
 
     for k in range(planes):
-        copies[k].wait()
         for m in range(rows):
             kept_ref[k, :, m * tile : (m + 1) * tile] = masked(k, side, m)
-    for m in range(rows):
-
-        @pl.loop(0, cut)
-        def _(k):
+    for k in range(cut):
+        for m in range(rows):
             given_ref[k, :, m * tile : (m + 1) * tile] = masked(k + rep * cut, 1 - side, m)
 
 
@@ -260,7 +264,7 @@
 
     cut, inner = planes // 2, factor.shape[1]
     inner = factor.shape[1]
-    chunks = inner // tile
+    chunks = 1
 
     def normed(other):
         return call(
@@ -268,7 +272,7 @@
             [(tile, half)],
             "hh",
             [factor, factor_normalizer],
-            [(tile, inner), (chunks, tile, half), pltpu.SemaphoreType.DMA((chunks + 1,))],
+            [(tile, inner), (chunks, inner // chunks, half), pltpu.SemaphoreType.DMA((chunks + 1,))],
             room=ROOM_OWN,
         )[0]
 
@@ -278,7 +282,7 @@
         [(planes, tile, depth), (cut, tile, depth)],
         "sh",
         [tile_structure.T, ancestor_inverse],
-        [(planes, PAIR * tile, depth), pltpu.SemaphoreType.DMA((planes,))],
+        [(planes * PAIR * tile, depth), pltpu.SemaphoreType.DMA((2,))],
         room=ROOM_MASK,
     )
     other_normed = normed(True)

time: 76.6 us -> 75.9 us (level)
  transfers between devices with their start and end apart: 28 -> 28, of which waited for: 17 -> 17; matrix products, arithmetic and copies ran while one was open for 0% -> 0% of each run, Pallas kernels for 5% -> 4%
where the time goes in v9:
time: 75.9 us; the launch traced here: 75.7 us
  waiting for transfers between devices  37.5 us (49%)
  starting transfers between devices  29.3 us (39%)
  Pallas kernels  7.34 us (10%)
  between operations  0.79 us (1%)
    ppermute x28, waiting for transfers between devices, send(): return lax.ppermute(block, AXES, route)  37.5 us
    ppermute x28, starting transfers between devices, send(): return lax.ppermute(block, AXES, route)  29.3 us
    pallas_call x6, Pallas kernels, call(): pl.pallas_call(kernel, out_shape=[jax.ShapeDtypeStruct(shape, F32) for sh...  7.34 us
  transfers between devices with their start and end apart: 28, of which 17 were waited for; matrix products, arithmetic and copies ran while one was open for 0% of the time, Pallas kernels for 4%

profile of v9, /device:TPU:0, one launch (start us, length us, event | category | flops | bytes accessed | tf_op | source)
XLA Modules:
  0.0 75.7 jit_solution(17769607054001891552)
XLA Ops:
  0.6 0.7 copy-done.1
  1.3 1.8 %shard_map.68 = (f32[4,128,256]{2,1,0:T(8,128)S(1)}, f32[2,128,256]{2,1,0:T(8,128)S(1)}) custom-call(s32[2,8]{1,0:T(2,128)S(1)} %bitcast.5, f32[1024,256]{1,0:T(8,128)} %full_ref.1), custom_call_target="tpu_custom_call" | custom-call | bytes 1835072 | tf_op jit(solution)/shard_map/pallas_call | solution.py:247
  3.1 3.0 %collective-permute-start = (f32[2,128,256]{2,1,0:T(8,128)S(1)}, f32[2,128,256]{2,1,0:T(8,128)S(1)}, u32[]{:S(2)}, u32[]{:S(2)}) collective-permute-start(f32[2,128,256]{2,1,0:T(8,128)S(1)} %get-tuple-element.13), channel_id=1, source_target_pairs={{0,2},{1,3},{2,0},{3,1},{4,6},{5,7},{6,4},{7,5},{8,10},{9,11},{10,... | collective-permute-start | bytes 786440 | tf_op jit(solution)/shard_map/ppermute | solution.py:31
  6.2 1.4 %shard_map.69.refs_0_ = f32[128,256]{1,0:T(8,128)S(1)} custom-call(f32[128,512]{1,0:T(8,128)} %factor_ref.3, f32[512,512]{1,0:T(8,128)} %normalizer_ref.3), custom_call_target="tpu_custom_call" | custom-call | bytes 1441792 | tf_op jit(solution)/shard_map/pallas_call | solution.py:247
  7.6 0.7 collective-permute-start.2
  8.3 6.3 %collective-permute-done.mine_ref = f32[2,128,256]{2,1,0:T(8,128)S(1)} collective-permute-done((f32[2,128,256]{2,1,0:T(8,128)S(1)}, f32[2,128,256]{2,1,0:T(8,128)S(1)}, u32[]{:S(2)}, u32[]{:S(2)}) %collective-permute-start) | collective-permute-done | bytes 262176 | tf_op jit(solution)/shard_map/ppermute | solution.py:31
  14.5 0.0 collective-permute-start.1
  14.6 0.0 collective-permute-done.2.refs_0_
  14.6 2.3 %collective-permute-start.3 = (f32[128,256]{1,0:T(8,128)S(1)}, f32[128,256]{1,0:T(8,128)S(1)}, u32[]{:S(2)}, u32[]{:S(2)}) collective-permute-start(f32[128,256]{1,0:T(8,128)S(1)} %collective-permute-done.2.refs_0_), channel_id=1, source_target_pairs={{0,16},{1,17},{2,18},{3,19},{4,20},{5,21},{6,22},{7,23},{8,24},{9,... | collective-permute-start | bytes 393224 | tf_op jit(solution)/shard_map/ppermute | solution.py:31
  16.9 0.7 collective-permute-start.4
  17.6 0.9 %collective-permute-start.5 = (f32[128,256]{1,0:T(8,128)S(1)}, f32[128,256]{1,0:T(8,128)S(1)}, u32[]{:S(2)}, u32[]{:S(2)}) collective-permute-start(f32[128,256]{1,0:T(8,128)S(1)} %collective-permute-done.2.refs_0_), channel_id=1, source_target_pairs={{0,18},{1,19},{2,16},{3,17},{4,22},{5,23},{6,20},{7,21},{8,26},{9,... | collective-permute-start | bytes 393224 | tf_op jit(solution)/shard_map/ppermute | solution.py:31
  18.5 2.0 %collective-permute-done.3.refs_1_ = f32[128,256]{1,0:T(8,128)S(1)} collective-permute-done((f32[128,256]{1,0:T(8,128)S(1)}, f32[128,256]{1,0:T(8,128)S(1)}, u32[]{:S(2)}, u32[]{:S(2)}) %collective-permute-start.3) | collective-permute-done | bytes 131104 | tf_op jit(solution)/shard_map/ppermute | solution.py:31
  20.5 2.2 %collective-permute-done.4.refs_2_ = f32[128,256]{1,0:T(8,128)S(1)} collective-permute-done((f32[128,256]{1,0:T(8,128)S(1)}, f32[128,256]{1,0:T(8,128)S(1)}, u32[]{:S(2)}, u32[]{:S(2)}) %collective-permute-start.4) | collective-permute-done | bytes 131104 | tf_op jit(solution)/shard_map/ppermute | solution.py:31
  22.7 2.5 %collective-permute-done.5.refs_3_ = f32[128,256]{1,0:T(8,128)S(1)} collective-permute-done((f32[128,256]{1,0:T(8,128)S(1)}, f32[128,256]{1,0:T(8,128)S(1)}, u32[]{:S(2)}, u32[]{:S(2)}) %collective-permute-start.5) | collective-permute-done | bytes 131104 | tf_op jit(solution)/shard_map/ppermute | solution.py:31
  25.2 0.0 collective-permute-done.1.theirs_ref
  25.2 0.6 shard_map.70
  25.8 0.1 collective-permute-start.8
  25.9 4.7 %collective-permute-start.9 = (f32[128,256]{1,0:T(8,128)S(1)}, f32[128,256]{1,0:T(8,128)S(1)}, u32[]{:S(2)}, u32[]{:S(2)}) collective-permute-start(f32[128,256]{1,0:T(8,128)S(1)} %shard_map.69.refs_0_), channel_id=1, source_target_pairs={{0,4},{1,5},{2,6},{3,7},{4,0},{5,1},{6,2},{7,3},{8,12},{9,13},{10,... | collective-permute-start | bytes 393224 | tf_op jit(solution)/shard_map/ppermute | solution.py:31
  30.6 2.4 %collective-permute-start.11 = (f32[128,256]{1,0:T(8,128)S(1)}, f32[128,256]{1,0:T(8,128)S(1)}, u32[]{:S(2)}, u32[]{:S(2)}) collective-permute-start(f32[128,256]{1,0:T(8,128)S(1)} %shard_map.69.refs_0_), channel_id=1, source_target_pairs={{0,12},{1,13},{2,14},{3,15},{4,8},{5,9},{6,10},{7,11},{8,4},{9,5},... | collective-permute-start | bytes 393224 | tf_op jit(solution)/shard_map/ppermute | solution.py:31
  33.0 2.3 %collective-permute-done.9.refs_1_ = f32[128,256]{1,0:T(8,128)S(1)} collective-permute-done((f32[128,256]{1,0:T(8,128)S(1)}, f32[128,256]{1,0:T(8,128)S(1)}, u32[]{:S(2)}, u32[]{:S(2)}) %collective-permute-start.9) | collective-permute-done | bytes 131104 | tf_op jit(solution)/shard_map/ppermute | solution.py:31
  35.3 7.8 %collective-permute-done.10.refs_2_ = f32[128,256]{1,0:T(8,128)S(1)} collective-permute-done((f32[128,256]{1,0:T(8,128)S(1)}, f32[128,256]{1,0:T(8,128)S(1)}, u32[]{:S(2)}, u32[]{:S(2)}) %collective-permute-start.10) | collective-permute-done | bytes 131104 | tf_op jit(solution)/shard_map/ppermute | solution.py:31
  43.2 0.5 collective-permute-start.14
  43.7 1.4 %shard_map.71.refs_4_ = f32[128,256]{1,0:T(8,128)S(1)} custom-call(f32[128,512]{1,0:T(8,128)} %factor_ref.3, f32[512,512]{1,0:T(8,128)} %normalizer_ref.3), custom_call_target="tpu_custom_call" | custom-call | bytes 1441792 | tf_op jit(solution)/shard_map/pallas_call | solution.py:247
  45.1 0.9 %shard_map.72 = (f32[136,128]{1,0:T(8,128)S(1)}, f32[136,128]{1,0:T(8,128)S(1)}, f32[136,128]{1,0:T(8,128)S(1)}, f32[136,128]{1,0:T(8,128)S(1)}) custom-call(f32[4,128,256]{2,1,0:T(8,128)S(1)} %get-tuple-element.14.share_ref, f32[4,128,256]{2,1,0:T(8,128)S(1)} %collective-permute-done.8.other_ref, f32[128,256]{1,0:T(8,128)S(1)} %shard_map.69.refs_0_, ...), custom_call_target="tpu_custom_call" | custom-call | flops 402653184 | bytes 2375680 | tf_op jit(solution)/shard_map/pallas_call | solution.py:247
  46.1 1.5 %collective-permute-start.17 = (f32[136,128]{1,0:T(8,128)S(1)}, f32[136,128]{1,0:T(8,128)S(1)}, u32[]{:S(2)}, u32[]{:S(2)}) collective-permute-start(f32[136,128]{1,0:T(8,128)S(1)} %get-tuple-element.19), channel_id=1, source_target_pairs={{0,18},{1,19},{2,16},{3,17},{4,22},{5,23},{6,20},{7,21},{8,26},{9,... | collective-permute-start | bytes 208904 | tf_op jit(solution)/shard_map/ppermute | solution.py:31
  47.6 1.5 %collective-permute-start.15 = (f32[136,128]{1,0:T(8,128)S(1)}, f32[136,128]{1,0:T(8,128)S(1)}, u32[]{:S(2)}, u32[]{:S(2)}) collective-permute-start(f32[136,128]{1,0:T(8,128)S(1)} %get-tuple-element.17), channel_id=1, source_target_pairs={{0,2},{1,3},{2,0},{3,1},{4,6},{5,7},{6,4},{7,5},{8,10},{9,11},{10,... | collective-permute-start | bytes 208904 | tf_op jit(solution)/shard_map/ppermute | solution.py:31
  49.1 0.5 collective-permute-start.16
  49.6 2.3 %collective-permute-start.6 = (f32[2,128,256]{2,1,0:T(8,128)S(1)}, f32[2,128,256]{2,1,0:T(8,128)S(1)}, u32[]{:S(2)}, u32[]{:S(2)}) collective-permute-start(f32[2,128,256]{2,1,0:T(8,128)S(1)} %get-tuple-element.15), channel_id=1, source_target_pairs={{0,4},{1,5},{2,6},{3,7},{4,0},{5,1},{6,2},{7,3},{8,12},{9,13},{10,... | collective-permute-start | bytes 786440 | tf_op jit(solution)/shard_map/ppermute | solution.py:31
  52.0 0.0 collective-permute-done.17
  52.0 0.7 collective-permute-done.15
  52.6 0.8 collective-permute-done.16
  53.4 0.0 copy-start
  53.4 0.6 collective-permute-start.20
  54.0 2.0 %collective-permute-start.18 = (f32[136,128]{1,0:T(8,128)S(1)}, f32[136,128]{1,0:T(8,128)S(1)}, u32[]{:S(2)}, u32[]{:S(2)}) collective-permute-start(f32[136,128]{1,0:T(8,128)S(1)} %add_add_fusion.1), channel_id=1, source_target_pairs={{0,4},{1,5},{2,6},{3,7},{4,0},{5,1},{6,2},{7,3},{8,12},{9,13},{10,... | collective-permute-start | bytes 208904 | tf_op jit(solution)/shard_map/ppermute | solution.py:31
  56.0 1.8 %collective-permute-start.19 = (f32[136,128]{1,0:T(8,128)S(1)}, f32[136,128]{1,0:T(8,128)S(1)}, u32[]{:S(2)}, u32[]{:S(2)}) collective-permute-start(f32[136,128]{1,0:T(8,128)S(1)} %add_add_fusion.1), channel_id=1, source_target_pairs={{0,8},{1,9},{2,10},{3,11},{4,12},{5,13},{6,14},{7,15},{8,0},{9,1},... | collective-permute-start | bytes 208904 | tf_op jit(solution)/shard_map/ppermute | solution.py:31
  57.9 2.9 %collective-permute-done.6 = f32[2,128,256]{2,1,0:T(8,128)S(1)} collective-permute-done((f32[2,128,256]{2,1,0:T(8,128)S(1)}, f32[2,128,256]{2,1,0:T(8,128)S(1)}, u32[]{:S(2)}, u32[]{:S(2)}) %collective-permute-start.6) | collective-permute-done | bytes 262176 | tf_op jit(solution)/shard_map/ppermute | solution.py:31
  60.8 0.1 collective-permute-start.7
  60.9 0.4 collective-permute-done.20
  61.4 0.6 collective-permute-done.18
  62.0 5.0 %collective-permute-done.19 = f32[136,128]{1,0:T(8,128)S(1)} collective-permute-done((f32[136,128]{1,0:T(8,128)S(1)}, f32[136,128]{1,0:T(8,128)S(1)}, u32[]{:S(2)}, u32[]{:S(2)}) %collective-permute-start.19) | collective-permute-done | bytes 69664 | tf_op jit(solution)/shard_map/ppermute | solution.py:31
  67.0 1.1 %collective-permute-start.21 = (f32[136,128]{1,0:T(8,128)S(1)}, f32[136,128]{1,0:T(8,128)S(1)}, u32[]{:S(2)}, u32[]{:S(2)}) collective-permute-start(f32[136,128]{1,0:T(8,128)S(1)} %add_add_fusion.refs_2_), channel_id=1, source_target_pairs={{0,2},{1,3},{2,0},{3,1},{4,6},{5,7},{6,4},{7,5},{8,10},{9,11},{10,... | collective-permute-start | bytes 208904 | tf_op jit(solution)/shard_map/ppermute | solution.py:31
  68.1 2.4 %collective-permute-start.23 = (f32[136,128]{1,0:T(8,128)S(1)}, f32[136,128]{1,0:T(8,128)S(1)}, u32[]{:S(2)}, u32[]{:S(2)}) collective-permute-start(f32[136,128]{1,0:T(8,128)S(1)} %add_add_fusion.refs_2_), channel_id=1, source_target_pairs={{0,18},{1,19},{2,16},{3,17},{4,22},{5,23},{6,20},{7,21},{8,26},{9,... | collective-permute-start | bytes 208904 | tf_op jit(solution)/shard_map/ppermute | solution.py:31
  70.6 0.8 %collective-permute-done.21.refs_3_ = f32[136,128]{1,0:T(8,128)S(1)} collective-permute-done((f32[136,128]{1,0:T(8,128)S(1)}, f32[136,128]{1,0:T(8,128)S(1)}, u32[]{:S(2)}, u32[]{:S(2)}) %collective-permute-start.21) | collective-permute-done | bytes 69664 | tf_op jit(solution)/shard_map/ppermute | solution.py:31
  71.4 1.1 %collective-permute-done.22.refs_4_ = f32[136,128]{1,0:T(8,128)S(1)} collective-permute-done((f32[136,128]{1,0:T(8,128)S(1)}, f32[136,128]{1,0:T(8,128)S(1)}, u32[]{:S(2)}, u32[]{:S(2)}) %collective-permute-start.22) | collective-permute-done | bytes 69664 | tf_op jit(solution)/shard_map/ppermute | solution.py:31
  72.5 0.9 %collective-permute-done.23.refs_5_ = f32[136,128]{1,0:T(8,128)S(1)} collective-permute-done((f32[136,128]{1,0:T(8,128)S(1)}, f32[136,128]{1,0:T(8,128)S(1)}, u32[]{:S(2)}, u32[]{:S(2)}) %collective-permute-start.23) | collective-permute-done | bytes 69664 | tf_op jit(solution)/shard_map/ppermute | solution.py:31
  73.4 0.3 collective-permute-done.26.refs_8_
  73.7 0.9 %collective-permute-done.27.refs_9_ = f32[64,128]{1,0:T(8,128)S(1)} collective-permute-done((f32[64,128]{1,0:T(8,128)S(1)}, f32[64,128]{1,0:T(8,128)S(1)}, u32[]{:S(2)}, u32[]{:S(2)}) %collective-permute-start.27) | collective-permute-done | bytes 32800 | tf_op jit(solution)/shard_map/ppermute | solution.py:31
  74.6 1.1 %shard_map.73 = (f32[512,256]{1,0:T(8,128)}, f32[128,256]{1,0:T(8,128)}) custom-call(f32[512,256]{1,0:T(8,128)S(1)} %copy-done, f32[128,256]{1,0:T(8,128)S(1)} %get-tuple-element.23.refs_0_, f32[128,256]{1,0:T(8,128)S(1)} %collective-permute-done.7.refs_1_, f32[136,128]{1,0:T(8,128)S(1)} %add_add_fusion.refs_2_, ...), custom_call_target="tpu_custom_call" | custom-call | bytes 1851392 | tf_op jit(solution)/shard_map/pallas_call | solution.py:247
  (25 shorter events, 0.1 us)
Async XLA Ops:
  0.6 0.7 copy-start.1
  3.1 11.4 %collective-permute-start = (f32[2,128,256]{2,1,0:T(8,128)S(1)}, f32[2,128,256]{2,1,0:T(8,128)S(1)}, u32[]{:S(2)}, u32[]{:S(2)}) collective-permute-start(f32[2,128,256]{2,1,0:T(8,128)S(1)} %get-tuple-element.13), channel_id=1, source_target_pairs={{0,2},{1,3},{2,0},{3,1},{4,6},{5,7},{6,4},{7,5},{8,10},{9,11},{10,... | collective-permute-start | bytes 786440 | tf_op jit(solution)/shard_map/ppermute | solution.py:31
  7.6 6.9 %collective-permute-start.2 = (f32[128,256]{1,0:T(8,128)S(1)}, f32[128,256]{1,0:T(8,128)S(1)}, u32[]{:S(2)}, u32[]{:S(2)}) collective-permute-start(f32[128,256]{1,0:T(8,128)S(1)} %shard_map.69.refs_0_), channel_id=1, source_target_pairs={{0,0},{1,1},{2,16},{3,17},{4,2},{5,3},{6,18},{7,19},{8,4},{9,5},{1... | collective-permute-start | bytes 393224 | tf_op jit(solution)/shard_map/ppermute | solution.py:31
  14.5 10.6 %collective-permute-start.1 = (f32[2,128,256]{2,1,0:T(8,128)S(1)}, f32[2,128,256]{2,1,0:T(8,128)S(1)}, u32[]{:S(2)}, u32[]{:S(2)}) collective-permute-start(f32[2,128,256]{2,1,0:T(8,128)S(1)} %collective-permute-done.mine_ref), channel_id=1, source_target_pairs={{0,1},{1,0},{2,3},{3,2},{4,5},{5,4},{6,7},{7,6},{8,9},{9,8},{10,11... | collective-permute-start | bytes 786440 | tf_op jit(solution)/shard_map/ppermute | solution.py:31
  14.6 5.9 %collective-permute-start.3 = (f32[128,256]{1,0:T(8,128)S(1)}, f32[128,256]{1,0:T(8,128)S(1)}, u32[]{:S(2)}, u32[]{:S(2)}) collective-permute-start(f32[128,256]{1,0:T(8,128)S(1)} %collective-permute-done.2.refs_0_), channel_id=1, source_target_pairs={{0,16},{1,17},{2,18},{3,19},{4,20},{5,21},{6,22},{7,23},{8,24},{9,... | collective-permute-start | bytes 393224 | tf_op jit(solution)/shard_map/ppermute | solution.py:31
  16.9 5.8 %collective-permute-start.4 = (f32[128,256]{1,0:T(8,128)S(1)}, f32[128,256]{1,0:T(8,128)S(1)}, u32[]{:S(2)}, u32[]{:S(2)}) collective-permute-start(f32[128,256]{1,0:T(8,128)S(1)} %collective-permute-done.2.refs_0_), channel_id=1, source_target_pairs={{0,2},{1,3},{2,0},{3,1},{4,6},{5,7},{6,4},{7,5},{8,10},{9,11},{10,... | collective-permute-start | bytes 393224 | tf_op jit(solution)/shard_map/ppermute | solution.py:31
  17.6 7.6 %collective-permute-start.5 = (f32[128,256]{1,0:T(8,128)S(1)}, f32[128,256]{1,0:T(8,128)S(1)}, u32[]{:S(2)}, u32[]{:S(2)}) collective-permute-start(f32[128,256]{1,0:T(8,128)S(1)} %collective-permute-done.2.refs_0_), channel_id=1, source_target_pairs={{0,18},{1,19},{2,16},{3,17},{4,22},{5,23},{6,20},{7,21},{8,26},{9,... | collective-permute-start | bytes 393224 | tf_op jit(solution)/shard_map/ppermute | solution.py:31
  25.8 19.3 %collective-permute-start.8 = (f32[4,128,256]{2,1,0:T(8,128)S(1)}, f32[4,128,256]{2,1,0:T(8,128)S(1)}, u32[]{:S(2)}, u32[]{:S(2)}) collective-permute-start(f32[4,128,256]{2,1,0:T(8,128)S(1)} %get-tuple-element.14.share_ref), channel_id=1, source_target_pairs={{0,1},{1,0},{2,3},{3,2},{4,5},{5,4},{6,7},{7,6},{8,9},{9,8},{10,11... | collective-permute-start | bytes 1572872 | tf_op jit(solution)/shard_map/ppermute | solution.py:31
  25.9 9.4 %collective-permute-start.9 = (f32[128,256]{1,0:T(8,128)S(1)}, f32[128,256]{1,0:T(8,128)S(1)}, u32[]{:S(2)}, u32[]{:S(2)}) collective-permute-start(f32[128,256]{1,0:T(8,128)S(1)} %shard_map.69.refs_0_), channel_id=1, source_target_pairs={{0,4},{1,5},{2,6},{3,7},{4,0},{5,1},{6,2},{7,3},{8,12},{9,13},{10,... | collective-permute-start | bytes 393224 | tf_op jit(solution)/shard_map/ppermute | solution.py:31
  30.6 12.6 %collective-permute-start.10 = (f32[128,256]{1,0:T(8,128)S(1)}, f32[128,256]{1,0:T(8,128)S(1)}, u32[]{:S(2)}, u32[]{:S(2)}) collective-permute-start(f32[128,256]{1,0:T(8,128)S(1)} %shard_map.69.refs_0_), channel_id=1, source_target_pairs={{0,8},{1,9},{2,10},{3,11},{4,12},{5,13},{6,14},{7,15},{8,0},{9,1},... | collective-permute-start | bytes 393224 | tf_op jit(solution)/shard_map/ppermute | solution.py:31
  30.6 12.6 %collective-permute-start.11 = (f32[128,256]{1,0:T(8,128)S(1)}, f32[128,256]{1,0:T(8,128)S(1)}, u32[]{:S(2)}, u32[]{:S(2)}) collective-permute-start(f32[128,256]{1,0:T(8,128)S(1)} %shard_map.69.refs_0_), channel_id=1, source_target_pairs={{0,12},{1,13},{2,14},{3,15},{4,8},{5,9},{6,10},{7,11},{8,4},{9,5},... | collective-permute-start | bytes 393224 | tf_op jit(solution)/shard_map/ppermute | solution.py:31
  35.3 9.8 %collective-permute-start.12 = (f32[128,256]{1,0:T(8,128)S(1)}, f32[128,256]{1,0:T(8,128)S(1)}, u32[]{:S(2)}, u32[]{:S(2)}) collective-permute-start(f32[128,256]{1,0:T(8,128)S(1)} %collective-permute-done.9.refs_1_), channel_id=1, source_target_pairs={{0,1},{1,0},{2,3},{3,2},{4,5},{5,4},{6,7},{7,6},{8,9},{9,8},{10,11... | collective-permute-start | bytes 393224 | tf_op jit(solution)/shard_map/ppermute | solution.py:31
  43.1 2.0 %collective-permute-start.13 = (f32[128,256]{1,0:T(8,128)S(1)}, f32[128,256]{1,0:T(8,128)S(1)}, u32[]{:S(2)}, u32[]{:S(2)}) collective-permute-start(f32[128,256]{1,0:T(8,128)S(1)} %collective-permute-done.10.refs_2_), channel_id=1, source_target_pairs={{0,1},{1,0},{2,3},{3,2},{4,5},{5,4},{6,7},{7,6},{8,9},{9,8},{10,11... | collective-permute-start | bytes 393224 | tf_op jit(solution)/shard_map/ppermute | solution.py:31
  43.2 2.0 %collective-permute-start.14 = (f32[128,256]{1,0:T(8,128)S(1)}, f32[128,256]{1,0:T(8,128)S(1)}, u32[]{:S(2)}, u32[]{:S(2)}) collective-permute-start(f32[128,256]{1,0:T(8,128)S(1)} %collective-permute-done.11.refs_3_), channel_id=1, source_target_pairs={{0,1},{1,0},{2,3},{3,2},{4,5},{5,4},{6,7},{7,6},{8,9},{9,8},{10,11... | collective-permute-start | bytes 393224 | tf_op jit(solution)/shard_map/ppermute | solution.py:31
  46.1 5.9 %collective-permute-start.17 = (f32[136,128]{1,0:T(8,128)S(1)}, f32[136,128]{1,0:T(8,128)S(1)}, u32[]{:S(2)}, u32[]{:S(2)}) collective-permute-start(f32[136,128]{1,0:T(8,128)S(1)} %get-tuple-element.19), channel_id=1, source_target_pairs={{0,18},{1,19},{2,16},{3,17},{4,22},{5,23},{6,20},{7,21},{8,26},{9,... | collective-permute-start | bytes 208904 | tf_op jit(solution)/shard_map/ppermute | solution.py:31
  47.6 5.0 %collective-permute-start.15 = (f32[136,128]{1,0:T(8,128)S(1)}, f32[136,128]{1,0:T(8,128)S(1)}, u32[]{:S(2)}, u32[]{:S(2)}) collective-permute-start(f32[136,128]{1,0:T(8,128)S(1)} %get-tuple-element.17), channel_id=1, source_target_pairs={{0,2},{1,3},{2,0},{3,1},{4,6},{5,7},{6,4},{7,5},{8,10},{9,11},{10,... | collective-permute-start | bytes 208904 | tf_op jit(solution)/shard_map/ppermute | solution.py:31
  49.1 4.3 %collective-permute-start.16 = (f32[136,128]{1,0:T(8,128)S(1)}, f32[136,128]{1,0:T(8,128)S(1)}, u32[]{:S(2)}, u32[]{:S(2)}) collective-permute-start(f32[136,128]{1,0:T(8,128)S(1)} %get-tuple-element.18), channel_id=1, source_target_pairs={{0,16},{1,17},{2,18},{3,19},{4,20},{5,21},{6,22},{7,23},{8,24},{9,... | collective-permute-start | bytes 208904 | tf_op jit(solution)/shard_map/ppermute | solution.py:31
  49.6 11.2 %collective-permute-start.6 = (f32[2,128,256]{2,1,0:T(8,128)S(1)}, f32[2,128,256]{2,1,0:T(8,128)S(1)}, u32[]{:S(2)}, u32[]{:S(2)}) collective-permute-start(f32[2,128,256]{2,1,0:T(8,128)S(1)} %get-tuple-element.15), channel_id=1, source_target_pairs={{0,4},{1,5},{2,6},{3,7},{4,0},{5,1},{6,2},{7,3},{8,12},{9,13},{10,... | collective-permute-start | bytes 786440 | tf_op jit(solution)/shard_map/ppermute | solution.py:31
  53.4 21.1 %copy-start = (f32[512,256]{1,0:T(8,128)S(1)}, f32[512,256]{1,0:T(8,128)}, u32[]{:S(2)}) copy-start(f32[512,256]{1,0:T(8,128)} %pivot_ref.1) | copy-start | bytes 1572868
  53.4 7.9 %collective-permute-start.20 = (f32[136,128]{1,0:T(8,128)S(1)}, f32[136,128]{1,0:T(8,128)S(1)}, u32[]{:S(2)}, u32[]{:S(2)}) collective-permute-start(f32[136,128]{1,0:T(8,128)S(1)} %add_add_fusion.1), channel_id=1, source_target_pairs={{0,12},{1,13},{2,14},{3,15},{4,8},{5,9},{6,10},{7,11},{8,4},{9,5},... | collective-permute-start | bytes 208904 | tf_op jit(solution)/shard_map/ppermute | solution.py:31
  54.0 8.0 %collective-permute-start.18 = (f32[136,128]{1,0:T(8,128)S(1)}, f32[136,128]{1,0:T(8,128)S(1)}, u32[]{:S(2)}, u32[]{:S(2)}) collective-permute-start(f32[136,128]{1,0:T(8,128)S(1)} %add_add_fusion.1), channel_id=1, source_target_pairs={{0,4},{1,5},{2,6},{3,7},{4,0},{5,1},{6,2},{7,3},{8,12},{9,13},{10,... | collective-permute-start | bytes 208904 | tf_op jit(solution)/shard_map/ppermute | solution.py:31
  56.0 10.9 %collective-permute-start.19 = (f32[136,128]{1,0:T(8,128)S(1)}, f32[136,128]{1,0:T(8,128)S(1)}, u32[]{:S(2)}, u32[]{:S(2)}) collective-permute-start(f32[136,128]{1,0:T(8,128)S(1)} %add_add_fusion.1), channel_id=1, source_target_pairs={{0,8},{1,9},{2,10},{3,11},{4,12},{5,13},{6,14},{7,15},{8,0},{9,1},... | collective-permute-start | bytes 208904 | tf_op jit(solution)/shard_map/ppermute | solution.py:31
  60.8 12.5 %collective-permute-start.7 = (f32[128,256]{1,0:T(8,128)S(1)}, f32[128,256]{1,0:T(8,128)S(1)}, u32[]{:S(2)}, u32[]{:S(2)}) collective-permute-start(f32[128,256]{1,0:T(8,128)S(1)} %get-tuple-element.22), channel_id=1, source_target_pairs={{0,8},{1,9},{2,10},{3,11},{4,12},{5,13},{6,14},{7,15},{8,0},{9,1},... | collective-permute-start | bytes 393224 | tf_op jit(solution)/shard_map/ppermute | solution.py:31
  67.0 4.4 %collective-permute-start.21 = (f32[136,128]{1,0:T(8,128)S(1)}, f32[136,128]{1,0:T(8,128)S(1)}, u32[]{:S(2)}, u32[]{:S(2)}) collective-permute-start(f32[136,128]{1,0:T(8,128)S(1)} %add_add_fusion.refs_2_), channel_id=1, source_target_pairs={{0,2},{1,3},{2,0},{3,1},{4,6},{5,7},{6,4},{7,5},{8,10},{9,11},{10,... | collective-permute-start | bytes 208904 | tf_op jit(solution)/shard_map/ppermute | solution.py:31
  68.1 4.3 %collective-permute-start.22 = (f32[136,128]{1,0:T(8,128)S(1)}, f32[136,128]{1,0:T(8,128)S(1)}, u32[]{:S(2)}, u32[]{:S(2)}) collective-permute-start(f32[136,128]{1,0:T(8,128)S(1)} %add_add_fusion.refs_2_), channel_id=1, source_target_pairs={{0,16},{1,17},{2,18},{3,19},{4,20},{5,21},{6,22},{7,23},{8,24},{9,... | collective-permute-start | bytes 208904 | tf_op jit(solution)/shard_map/ppermute | solution.py:31
  68.1 5.2 %collective-permute-start.23 = (f32[136,128]{1,0:T(8,128)S(1)}, f32[136,128]{1,0:T(8,128)S(1)}, u32[]{:S(2)}, u32[]{:S(2)}) collective-permute-start(f32[136,128]{1,0:T(8,128)S(1)} %add_add_fusion.refs_2_), channel_id=1, source_target_pairs={{0,18},{1,19},{2,16},{3,17},{4,22},{5,23},{6,20},{7,21},{8,26},{9,... | collective-permute-start | bytes 208904 | tf_op jit(solution)/shard_map/ppermute | solution.py:31
  70.6 2.8 %collective-permute-start.24 = (f32[64,128]{1,0:T(8,128)S(1)}, f32[64,128]{1,0:T(8,128)S(1)}, u32[]{:S(2)}, u32[]{:S(2)}) collective-permute-start(f32[64,128]{1,0:T(8,128)S(1)} %slice.34), channel_id=1, source_target_pairs={{0,1},{1,0},{2,3},{3,2},{4,5},{5,4},{6,7},{7,6},{8,9},{9,8},{10,11... | collective-permute-start | bytes 98312 | tf_op jit(solution)/shard_map/ppermute | solution.py:31
  71.4 2.0 %collective-permute-start.25 = (f32[64,128]{1,0:T(8,128)S(1)}, f32[64,128]{1,0:T(8,128)S(1)}, u32[]{:S(2)}, u32[]{:S(2)}) collective-permute-start(f32[64,128]{1,0:T(8,128)S(1)} %slice.35), channel_id=1, source_target_pairs={{0,1},{1,0},{2,3},{3,2},{4,5},{5,4},{6,7},{7,6},{8,9},{9,8},{10,11... | collective-permute-start | bytes 98312 | tf_op jit(solution)/shard_map/ppermute | solution.py:31
  72.4 1.2 %collective-permute-start.26 = (f32[64,128]{1,0:T(8,128)S(1)}, f32[64,128]{1,0:T(8,128)S(1)}, u32[]{:S(2)}, u32[]{:S(2)}) collective-permute-start(f32[64,128]{1,0:T(8,128)S(1)} %slice.36), channel_id=1, source_target_pairs={{0,1},{1,0},{2,3},{3,2},{4,5},{5,4},{6,7},{7,6},{8,9},{9,8},{10,11... | collective-permute-start | bytes 98312 | tf_op jit(solution)/shard_map/ppermute | solution.py:31
  73.3 1.2 %collective-permute-start.27 = (f32[64,128]{1,0:T(8,128)S(1)}, f32[64,128]{1,0:T(8,128)S(1)}, u32[]{:S(2)}, u32[]{:S(2)}) collective-permute-start(f32[64,128]{1,0:T(8,128)S(1)} %slice.37), channel_id=1, source_target_pairs={{0,1},{1,0},{2,3},{3,2},{4,5},{5,4},{6,7},{7,6},{8,9},{9,8},{10,11... | collective-permute-start | bytes 98312 | tf_op jit(solution)/shard_map/ppermute | solution.py:31
